TPU v7x, 256 devices: a whole 4x4x8 slice. The times are simulated.
256 devices in a mesh: kr: 32 (over z_lo, x, y), kc: 8 (over z_hi, core).
Axes of the slice: x: 4, y: 4, z: 8 (z_hi: 4, z_lo: 2; z = z_hi * 2 + z_lo), core: 2. Of those that a mesh axis runs over, the one named last changes fastest.
Arguments:
- pair_conduction: bfloat16 [768, 64, 4096], P('kr', None, 'kc'), may hold values from -6 to 6
- pair_valence: bfloat16 [768, 64, 4096], P('kr', None, 'kc'), may hold values from -6 to 6
- screened: bfloat16 [32, 4096, 4096], P('kr', 'kc'), may hold values from -0.09375 to 0.09375
- sphere_sizes: int32 [32], replicated, may hold values from 2048 to 4096
Outputs:
- kernels: float32 [768, 64, 64], P('kr', 'kc')
All inputs are finite; a program needn't handle non-finite values.
Results may differ from a plain program's by a relative error of at most 0.0029.
Values may be sent and summed in bfloat16 or wider, within the bound.
No kernel may reach another device: no remote copies, remote signals or barrier semaphores. Data moves between devices by JAX's collectives and lax.ppermute only.
A program may use at most 128 MiB of HBM per device.

v0:
```python
import functools

import jax
import jax.numpy as jnp
from jax import lax
from jax.experimental import pallas as pl
from jax.experimental.pallas import tpu as pltpu
from jax.sharding import PartitionSpec as P

prefactor = 0.015625
AXES = ("kr", "kc")
VMEM = pl.BlockSpec(memory_space=pltpu.VMEM)
SMEM = pl.BlockSpec(memory_space=pltpu.SMEM)
CONTRACT_LAST = (((1,), (1,)), ((), ()))


def moves(owners, quarters, target):
    pairs = []
    for i in range(owners):
        for k in range(quarters):
            for c in range(2):
                ti, tk, tc = target(i, k, c)
                pairs.append(
                    (
                        (i * quarters + k) * 2 + c,
                        ((ti % owners) * quarters + tk % quarters) * 2 + tc,
                    )
                )
    return pairs


def turn(group, q, owners):
    if group == 1:
        return -1 if q == owners - 1 else 1
    if group == 2:
        return 1 if q == 0 else -1
    return 1


def restrict_kernel(quarters, rows, info_ref, slab_ref, mine_ref, give_ref):
    core, sphere = info_ref[0], info_ref[2]
    block = slab_ref.shape[0]
    first = info_ref[1] + pl.program_id(0) * block
    row = first + lax.broadcasted_iota(jnp.int32, (block, rows), 0)
    col = lax.broadcasted_iota(jnp.int32, (block, rows), 1)
    row_inside = row < sphere
    for j in range(quarters):
        kept = []
        for t in range(2):
            at = (2 * j + t) * rows
            keep = row_inside & (at + col < sphere)
            x = slab_ref[:, at : at + rows].astype(jnp.float32)
            kept.append(jnp.where(keep, x, 0.0))
        even = core == 0
        span = pl.ds(j * rows, rows)
        mine_ref[:, span] = jnp.where(even, kept[0], kept[1]).astype(mine_ref.dtype)
        give_ref[:, span] = jnp.where(even, kept[1], kept[0]).astype(give_ref.dtype)


def first_kernel(group_size, bands, rows, info_ref, own, ahead, behind, w0, w1, acc):
    for s, w in enumerate((w0, w1)):
        total = None
        for n, x in enumerate((own, ahead, behind)):
            at = pl.multiple_of(info_ref[n] * rows, rows)
            y = lax.dot_general(
                x[...].reshape(group_size * bands, rows),
                w[:, pl.ds(at, rows)],
                CONTRACT_LAST,
                preferred_element_type=jnp.float32,
            )
            total = y if total is None else total + y
        acc[s] = total


def last_kernel(
    sizes, info_ref, acc, far0, far1, w0, w1, c0, c1, keep_ref, give_ref
):
    group_size, bands, rows, quarters = sizes
    half = group_size // 2
    at = pl.multiple_of(info_ref[0] * rows, rows)
    quarter, core = info_ref[1], info_ref[2]
    for h, x in enumerate((far0, far1)):
        base = h * half * bands
        high, low = [], []
        for s, w in enumerate((w0, w1)):
            y = acc[s, base : base + half * bands] + lax.dot_general(
                x[...].reshape(half * bands, rows),
                w[:, pl.ds(at, rows)],
                CONTRACT_LAST,
                preferred_element_type=jnp.float32,
            )
            top = y.astype(jnp.bfloat16)
            high.append(top)
            low.append((y - top.astype(jnp.float32)).astype(jnp.bfloat16))
        for n in range(half):
            p = h * half + n
            part = None
            for s, c in enumerate((c0, c1)):
                for piece in (high[s], low[s]):
                    y = lax.dot_general(
                        c[p],
                        piece[n * bands : (n + 1) * bands],
                        CONTRACT_LAST,
                        preferred_element_type=jnp.float32,
                    )
                    part = y if part is None else part + y
            part = part * prefactor
            part = part.reshape(quarters, 2, -1, part.shape[-1])
            even = core == 0
            for j in range(quarters):
                d = lax.rem(j - quarter + quarters, quarters)
                keep_ref[d, p] = jnp.where(even, part[j, 0], part[j, 1])
                give_ref[d, p] = jnp.where(even, part[j, 1], part[j, 0])


def shards(pair_conduction, pair_valence, screened, sphere_sizes):
    owners = lax.axis_size("kr")
    quarters = lax.axis_size("kc") // 2
    rows, gvectors = screened.shape[1:]
    group_size = pair_valence.shape[0] // 3
    bands = pair_valence.shape[1]
    cbands = pair_conduction.shape[1]
    half = group_size // 2
    owner = lax.axis_index("kr")
    place = lax.axis_index("kc")
    quarter = place // 2
    core = place % 2
    shift = (0, -1, 1)

    def send(x, target):
        return lax.ppermute(x, AXES, moves(owners, quarters, target))

    def swap(x):
        return send(x, lambda i, k, c: (i, k, 1 - c))

    v = [pair_valence[g * group_size : (g + 1) * group_size] for g in range(3)]
    cond = [pair_conduction[g * group_size : (g + 1) * group_size] for g in range(3)]
    sigma = (
        jnp.int32(1),
        jnp.where(owner == owners - 1, -1, 1),
        jnp.where(owner == 0, 1, -1),
    )

    own, ahead, behind = {0: v[0]}, {}, {}
    for g in (1, 2):
        own[g] = send(v[g], lambda i, k, c: (i + shift[g], k, c))
    for g in (1, 2):
        ahead[g] = send(
            v[g],
            lambda i, k, c: (
                i + shift[g],
                k + turn(g, (i + shift[g]) % owners, owners),
                c,
            ),
        )
    c_own = {0: cond[0]}
    for g in (1, 2):
        c_own[g] = send(cond[g], lambda i, k, c: (i + shift[g], k, c))
    for g in (1, 2):
        behind[g] = send(own[g], lambda i, k, c: (i, k - turn(g, i, owners), c))
    up = [
        send(v[0][h * half : (h + 1) * half], lambda i, k, c: (i, k + 1, c))
        for h in range(2)
    ]
    down = [
        send(v[0][h * half : (h + 1) * half], lambda i, k, c: (i, k - 1, c))
        for h in (1, 0)
    ][::-1]
    forward_up, forward_down = [], []
    for g in (1, 2):
        forward_up.append(
            jnp.where(sigma[g] > 0, ahead[g][:half], behind[g][:half])
        )
        forward_down.append(
            jnp.where(sigma[g] > 0, behind[g][half:], ahead[g][half:])
        )
    far_up = send(jnp.concatenate(forward_up, 0), lambda i, k, c: (i, k + 1, c))
    far_down = send(jnp.concatenate(forward_down, 0), lambda i, k, c: (i, k - 1, c))
    far = {
        1: (far_up[:half], far_down[:half]),
        2: (far_up[half:], far_down[half:]),
        0: (
            send(up[0], lambda i, k, c: (i, k + 1, c)),
            send(down[1], lambda i, k, c: (i, k - 1, c)),
        ),
    }
    ahead[0] = jnp.concatenate(up, 0)
    behind[0] = jnp.concatenate(down, 0)

    info = jnp.stack([core, place * rows, sphere_sizes[owner]])
    block = rows // 4
    w0, give = pl.pallas_call(
        functools.partial(restrict_kernel, quarters, rows),
        grid=(rows // block,),
        in_specs=[SMEM, pl.BlockSpec((block, gvectors), lambda r: (r, 0))],
        out_specs=[pl.BlockSpec((block, gvectors // 2), lambda r: (r, 0))] * 2,
        out_shape=[jax.ShapeDtypeStruct((rows, gvectors // 2), screened.dtype)] * 2,
        name="restrict",
    )(info, screened[0])
    w1 = swap(give)
    c_par = {g: swap(c_own[g]) for g in range(3)}

    kept, given = {}, {}
    for g in (1, 2, 0):
        at = jnp.stack(
            [
                quarter,
                lax.rem(quarter - sigma[g] + quarters, quarters),
                lax.rem(quarter + sigma[g] + quarters, quarters),
            ]
        )
        acc = pl.pallas_call(
            functools.partial(first_kernel, group_size, bands, rows),
            in_specs=[SMEM] + [VMEM] * 5,
            out_specs=VMEM,
            out_shape=jax.ShapeDtypeStruct((2, group_size * bands, rows), jnp.float32),
        )(at, own[g], ahead[g], behind[g], w0, w1)
        at = jnp.stack([lax.rem(quarter + 2, quarters), quarter, core])
        shape = (quarters, group_size, cbands // quarters // 2, bands)
        kept[g], given[g] = pl.pallas_call(
            functools.partial(last_kernel, (group_size, bands, rows, quarters)),
            in_specs=[SMEM] + [VMEM] * 7,
            out_specs=[VMEM] * 2,
            out_shape=[jax.ShapeDtypeStruct(shape, jnp.float32)] * 2,
        )(at, acc, *far[g], w0, w1, c_own[g], c_par[g])

    def exchange(keep, give):
        keep = keep + swap(give)
        out = keep[0]
        for d in (1, 3, 2):
            out = out + send(keep[d], lambda i, k, c: (i, k + d, c))
        return out

    both = exchange(
        jnp.concatenate([kept[1], kept[2]], 1), jnp.concatenate([given[1], given[2]], 1)
    )
    results = [
        send(
            both[(g - 1) * group_size : g * group_size],
            lambda i, k, c: (i - shift[g], k, c),
        )
        for g in (1, 2)
    ]
    results.insert(0, exchange(kept[0], given[0]))
    return jnp.concatenate(results, 0)


def solution(mesh):
    return jax.shard_map(
        shards,
        mesh=mesh,
        in_specs=(P("kr", None, "kc"), P("kr", None, "kc"), P("kr", "kc", None), P()),
        out_specs=P("kr", "kc", None),
        check_vma=False,
    )
```

profile of v0, /device:TPU:30, one launch (start us, length us, event | category | flops | bytes accessed | tf_op | source)
XLA Modules:
  0.0 223.8 jit_solution(9252624179380016930)
XLA Ops:
  0.0 2.6 %fusion.8 = (bf16[8,64,512]{2,1,0:T(8,128)(2,1)}, bf16[8,64,512]{2,1,0:T(8,128)(2,1)}, bf16[8,64,512]{2,1,0:T(8,128)(2,1)}) fusion(bf16[24,64,512]{2,1,0:T(8,128)(2,1)} %param.5), kind=kLoop, calls=%fused_computation.32 | loop fusion | bytes 3145728 | tf_op jit(solution)/shard_map/slice | solution.py:136
  3.3 5.5 %collective-permute-start.16 = (bf16[8,64,512]{2,1,0:T(8,128)(2,1)}, bf16[8,64,512]{2,1,0:T(8,128)(2,1)}, u32[]{:S(2)}, u32[]{:S(2)}) collective-permute-start(bf16[8,64,512]{2,1,0:T(8,128)(2,1)} %get-tuple-element.27), channel_id=1, source_target_pairs={{0,8},{1,9},{2,10},{3,11},{4,12},{5,13},{6,14},{7,15},{8,16},{9,17... | collective-permute-start | bytes 1572872 | tf_op jit(solution)/shard_map/ppermute | solution.py:131
  10.7 5.3 %restrict.1 = (bf16[512,2048]{1,0:T(8,128)(2,1)}, bf16[512,2048]{1,0:T(8,128)(2,1)}) custom-call(s32[3]{0:T(128)} %pad_add_fusion.2.info_ref, bf16[512,4096]{1,0:T(8,128)(2,1)} %bitcast.39), custom_call_target="tpu_custom_call" | custom-call | tf_op jit(solution)/shard_map/restrict/pallas_call | solution.py:192
  16.0 7.4 %collective-permute-start.15 = (bf16[8,64,512]{2,1,0:T(8,128)(2,1)}, bf16[8,64,512]{2,1,0:T(8,128)(2,1)S(1)}, u32[]{:S(2)}, u32[]{:S(2)}) collective-permute-start(bf16[8,64,512]{2,1,0:T(8,128)(2,1)} %get-tuple-element.27), channel_id=1, source_target_pairs={{0,14},{1,15},{2,8},{3,9},{4,10},{5,11},{6,12},{7,13},{8,22},{9,23... | collective-permute-start | bytes 1572872 | tf_op jit(solution)/shard_map/ppermute | solution.py:131
  23.4 5.1 %collective-permute-start.14 = (bf16[8,64,512]{2,1,0:T(8,128)(2,1)}, bf16[8,64,512]{2,1,0:T(8,128)(2,1)}, u32[]{:S(2)}, u32[]{:S(2)}) collective-permute-start(bf16[8,64,512]{2,1,0:T(8,128)(2,1)} %collective-permute-done.12.own), channel_id=1, source_target_pairs={{0,6},{1,7},{2,0},{3,1},{4,2},{5,3},{6,4},{7,5},{8,14},{9,15},{10,... | collective-permute-start | bytes 1572872 | tf_op jit(solution)/shard_map/ppermute | solution.py:131
  30.8 5.1 %collective-permute-start.17 = (bf16[8,64,512]{2,1,0:T(8,128)(2,1)}, bf16[8,64,512]{2,1,0:T(8,128)(2,1)S(1)}, u32[]{:S(2)}, u32[]{:S(2)}) collective-permute-start(bf16[8,64,512]{2,1,0:T(8,128)(2,1)} %collective-permute-done.16.own), channel_id=1, source_target_pairs={{0,6},{1,7},{2,0},{3,1},{4,2},{5,3},{6,4},{7,5},{8,10},{9,11},{10,... | collective-permute-start | bytes 1572872 | tf_op jit(solution)/shard_map/ppermute | solution.py:131
  36.0 2.6 %fusion.6 = (bf16[8,64,512]{2,1,0:T(8,128)(2,1)}, bf16[8,64,512]{2,1,0:T(8,128)(2,1)}, bf16[8,64,512]{2,1,0:T(8,128)(2,1)}) fusion(bf16[24,64,512]{2,1,0:T(8,128)(2,1)} %param.4), kind=kLoop, calls=%fused_computation.30 | loop fusion | bytes 3145728 | tf_op jit(solution)/shard_map/slice | solution.py:137
  38.5 5.5 %collective-permute-done.13.ahead = bf16[8,64,512]{2,1,0:T(8,128)(2,1)S(1)} collective-permute-done((bf16[8,64,512]{2,1,0:T(8,128)(2,1)}, bf16[8,64,512]{2,1,0:T(8,128)(2,1)S(1)}, u32[]{:S(2)}, u32[]{:S(2)}) %collective-permute-start.13) | collective-permute-done | bytes 524320 | tf_op jit(solution)/shard_map/ppermute | solution.py:131
  44.0 3.3 %collective-permute-start = (bf16[4,64,512]{2,1,0:T(8,128)(2,1)S(1)}, bf16[4,64,512]{2,1,0:T(8,128)(2,1)}, u32[]{:S(2)}, u32[]{:S(2)}) collective-permute-start(bf16[4,64,512]{2,1,0:T(8,128)(2,1)S(1)} %get-tuple-element.24), channel_id=1, source_target_pairs={{0,2},{1,3},{2,4},{3,5},{4,6},{5,7},{6,0},{7,1},{8,10},{9,11},{10,... | collective-permute-start | bytes 786440 | tf_op jit(solution)/shard_map/ppermute | solution.py:131
  49.0 6.7 %collective-permute-start.1 = (bf16[4,64,512]{2,1,0:T(8,128)(2,1)}, bf16[4,64,512]{2,1,0:T(8,128)(2,1)S(1)}, u32[]{:S(2)}, u32[]{:S(2)}) collective-permute-start(bf16[4,64,512]{2,1,0:T(8,128)(2,1)} %get-tuple-element.25), channel_id=1, source_target_pairs={{0,2},{1,3},{2,4},{3,5},{4,6},{5,7},{6,0},{7,1},{8,10},{9,11},{10,... | collective-permute-start | bytes 786440 | tf_op jit(solution)/shard_map/ppermute | solution.py:131
  57.0 5.3 %collective-permute-done.17.behind = bf16[8,64,512]{2,1,0:T(8,128)(2,1)S(1)} collective-permute-done((bf16[8,64,512]{2,1,0:T(8,128)(2,1)}, bf16[8,64,512]{2,1,0:T(8,128)(2,1)S(1)}, u32[]{:S(2)}, u32[]{:S(2)}) %collective-permute-start.17) | collective-permute-done | bytes 524320 | tf_op jit(solution)/shard_map/ppermute | solution.py:131
  62.3 13.1 %collective-permute-start.20 = (bf16[8,64,512]{2,1,0:T(8,128)(2,1)}, bf16[8,64,512]{2,1,0:T(8,128)(2,1)}, u32[]{:S(2)}, u32[]{:S(2)}) collective-permute-start(bf16[8,64,512]{2,1,0:T(8,128)(2,1)} %get-tuple-element.23), channel_id=1, source_target_pairs={{0,248},{1,249},{2,250},{3,251},{4,252},{5,253},{6,254},{7,255},{8... | collective-permute-start | bytes 1572872 | tf_op jit(solution)/shard_map/ppermute | solution.py:131
  77.1 3.0 %collective-permute-start.19 = (bf16[8,64,512]{2,1,0:T(8,128)(2,1)}, bf16[8,64,512]{2,1,0:T(8,128)(2,1)}, u32[]{:S(2)}, u32[]{:S(2)}) collective-permute-start(bf16[8,64,512]{2,1,0:T(8,128)(2,1)} %pad_maximum_fusion.3), channel_id=1, source_target_pairs={{0,6},{1,7},{2,0},{3,1},{4,2},{5,3},{6,4},{7,5},{8,14},{9,15},{10,... | collective-permute-start | bytes 1572872 | tf_op jit(solution)/shard_map/ppermute | solution.py:131
  82.5 43.7 %collective-permute-done.20.c0 = bf16[8,64,512]{2,1,0:T(8,128)(2,1)} collective-permute-done((bf16[8,64,512]{2,1,0:T(8,128)(2,1)}, bf16[8,64,512]{2,1,0:T(8,128)(2,1)}, u32[]{:S(2)}, u32[]{:S(2)}) %collective-permute-start.20) | collective-permute-done | bytes 524320 | tf_op jit(solution)/shard_map/ppermute | solution.py:131
  126.2 4.4 %collective-permute-start.18 = (bf16[8,64,512]{2,1,0:T(8,128)(2,1)}, bf16[8,64,512]{2,1,0:T(8,128)(2,1)}, u32[]{:S(2)}, u32[]{:S(2)}) collective-permute-start(bf16[8,64,512]{2,1,0:T(8,128)(2,1)} %pad_maximum_fusion.2), channel_id=1, source_target_pairs={{0,2},{1,3},{2,4},{3,5},{4,6},{5,7},{6,0},{7,1},{8,10},{9,11},{10,... | collective-permute-start | bytes 1572872 | tf_op jit(solution)/shard_map/ppermute | solution.py:131
  132.1 1.9 pad_maximum_fusion.ahead
  134.3 1.9 fusion.9
  136.2 12.2 %collective-permute-done.18 = bf16[8,64,512]{2,1,0:T(8,128)(2,1)} collective-permute-done((bf16[8,64,512]{2,1,0:T(8,128)(2,1)}, bf16[8,64,512]{2,1,0:T(8,128)(2,1)}, u32[]{:S(2)}, u32[]{:S(2)}) %collective-permute-start.18) | collective-permute-done | bytes 524320 | tf_op jit(solution)/shard_map/ppermute | solution.py:131
  148.4 5.3 %collective-permute-start.5 = (bf16[4,64,512]{2,1,0:T(8,128)(2,1)}, bf16[4,64,512]{2,1,0:T(8,128)(2,1)S(1)}, u32[]{:S(2)}, u32[]{:S(2)}) collective-permute-start(bf16[4,64,512]{2,1,0:T(8,128)(2,1)} %collective-permute-done), channel_id=1, source_target_pairs={{0,2},{1,3},{2,4},{3,5},{4,6},{5,7},{6,0},{7,1},{8,10},{9,11},{10,... | collective-permute-start | bytes 786440 | tf_op jit(solution)/shard_map/ppermute | solution.py:131
  153.7 2.2 fusion.10
  155.9 5.9 %shard_map.48.acc = f32[2,512,512]{2,1,0:T(8,128)} custom-call(s32[3]{0:T(128)} %pad_add_fusion.3.info_ref, bf16[8,64,512]{2,1,0:T(8,128)(2,1)} %collective-permute-done.12.own, bf16[8,64,512]{2,1,0:T(8,128)(2,1)} %copy-done.2, bf16[8,64,512]{2,1,0:T(8,128)(2,1)} %collective-permute-done.14.behind, bf16[512,2048]{1,0:T(8,128)(2,1)} %get-tuple-element.13.w0, ...), custom_call_target="tpu_custom_call" | custom-call | tf_op jit(solution)/shard_map/pallas_call | solution.py:212
  161.9 5.9 %shard_map.50.acc = f32[2,512,512]{2,1,0:T(8,128)} custom-call(s32[3]{0:T(128)} %pad_add_fusion.4.info_ref, bf16[8,64,512]{2,1,0:T(8,128)(2,1)} %collective-permute-done.16.own, bf16[8,64,512]{2,1,0:T(8,128)(2,1)} %copy-done.1, bf16[8,64,512]{2,1,0:T(8,128)(2,1)} %copy-done.3, bf16[512,2048]{1,0:T(8,128)(2,1)} %get-tuple-element.13.w0, bf16[512,2048]{1,0:T(8,128)(2,1)} %copy-done), custom_call_target="tpu_custom_call" | custom-call | tf_op jit(solution)/shard_map/pallas_call | solution.py:212
  167.8 5.4 %shard_map.49 = (f32[4,8,8,64]{3,2,1,0:T(8,128)}, f32[4,8,8,64]{3,2,1,0:T(8,128)}) custom-call(s32[3]{0:T(128)} %pad_add_fusion.info_ref, f32[2,512,512]{2,1,0:T(8,128)} %shard_map.48.acc, bf16[4,64,512]{2,1,0:T(8,128)(2,1)} %get-tuple-element.35.far0, bf16[4,64,512]{2,1,0:T(8,128)(2,1)} %get-tuple-element.33.far1, bf16[512,2048]{1,0:T(8,128)(2,1)} %get-tuple-element.13.w0, ...), custom_call_target="tpu_custom_call" | custom-call | tf_op jit(solution)/shard_map/pallas_call | solution.py:220
  173.2 5.3 %shard_map.51 = (f32[4,8,8,64]{3,2,1,0:T(8,128)}, f32[4,8,8,64]{3,2,1,0:T(8,128)}) custom-call(s32[3]{0:T(128)} %pad_add_fusion.info_ref, f32[2,512,512]{2,1,0:T(8,128)} %shard_map.50.acc, bf16[4,64,512]{2,1,0:T(8,128)(2,1)} %get-tuple-element.36.far0, bf16[4,64,512]{2,1,0:T(8,128)(2,1)} %get-tuple-element.34.far1, bf16[512,2048]{1,0:T(8,128)(2,1)} %get-tuple-element.13.w0, ...), custom_call_target="tpu_custom_call" | custom-call | tf_op jit(solution)/shard_map/pallas_call | solution.py:220
  179.5 1.9 pad_maximum_fusion.1.behind
  181.4 5.9 %shard_map.46.acc = f32[2,512,512]{2,1,0:T(8,128)} custom-call(s32[3]{0:T(128)} %pad_add_fusion.1.info_ref, bf16[8,64,512]{2,1,0:T(8,128)(2,1)} %get-tuple-element.26.own, bf16[8,64,512]{2,1,0:T(8,128)(2,1)} %pad_maximum_fusion.ahead, bf16[8,64,512]{2,1,0:T(8,128)(2,1)} %pad_maximum_fusion.1.behind, bf16[512,2048]{1,0:T(8,128)(2,1)} %get-tuple-element.13.w0, ...), custom_call_target="tpu_custom_call" | custom-call | tf_op jit(solution)/shard_map/pallas_call | solution.py:212
  188.2 5.3 %shard_map.47 = (f32[4,8,8,64]{3,2,1,0:T(8,128)}, f32[4,8,8,64]{3,2,1,0:T(8,128)}) custom-call(s32[3]{0:T(128)} %pad_add_fusion.info_ref, f32[2,512,512]{2,1,0:T(8,128)} %shard_map.46.acc, bf16[4,64,512]{2,1,0:T(8,128)(2,1)} %copy-done.6, bf16[4,64,512]{2,1,0:T(8,128)(2,1)} %collective-permute-done.6.far1, bf16[512,2048]{1,0:T(8,128)(2,1)} %get-tuple-element.13.w0, ...), custom_call_target="tpu_custom_call" | custom-call | tf_op jit(solution)/shard_map/pallas_call | solution.py:220
  196.2 2.6 %collective-permute-start.25 = (f32[16,8,64]{2,1,0:T(8,128)S(1)}, f32[16,8,64]{2,1,0:T(8,128)S(1)}, u32[]{:S(2)}, u32[]{:S(2)}) collective-permute-start(f32[16,8,64]{2,1,0:T(8,128)S(1)} %get-tuple-element.37), channel_id=1, source_target_pairs={{0,2},{1,3},{2,4},{3,5},{4,6},{5,7},{6,0},{7,1},{8,10},{9,11},{10,... | collective-permute-start | bytes 98312 | tf_op jit(solution)/shard_map/ppermute | solution.py:131
  200.4 3.3 %collective-permute-start.27 = (f32[16,8,64]{2,1,0:T(8,128)S(1)}, f32[16,8,64]{2,1,0:T(8,128)S(1)}, u32[]{:S(2)}, u32[]{:S(2)}) collective-permute-start(f32[16,8,64]{2,1,0:T(8,128)S(1)} %get-tuple-element.38), channel_id=1, source_target_pairs={{0,4},{1,5},{2,6},{3,7},{4,0},{5,1},{6,2},{7,3},{8,12},{9,13},{10,... | collective-permute-start | bytes 98312 | tf_op jit(solution)/shard_map/ppermute | solution.py:131
  206.5 2.8 %collective-permute-start.9 = (f32[8,8,64]{2,1,0:T(8,128)S(1)}, f32[8,8,64]{2,1,0:T(8,128)S(1)}, u32[]{:S(2)}, u32[]{:S(2)}) collective-permute-start(f32[8,8,64]{2,1,0:T(8,128)S(1)} %get-tuple-element.40), channel_id=1, source_target_pairs={{0,2},{1,3},{2,4},{3,5},{4,6},{5,7},{6,0},{7,1},{8,10},{9,11},{10,... | collective-permute-start | bytes 49160 | tf_op jit(solution)/shard_map/ppermute | solution.py:131
  209.4 5.6 %collective-permute-start.28 = (f32[8,8,64]{2,1,0:T(8,128)S(1)}, f32[8,8,64]{2,1,0:T(8,128)S(1)}, u32[]{:S(2)}, u32[]{:S(2)}) collective-permute-start(f32[8,8,64]{2,1,0:T(8,128)S(1)} %get-tuple-element.43), channel_id=1, source_target_pairs={{0,8},{1,9},{2,10},{3,11},{4,12},{5,13},{6,14},{7,15},{8,16},{9,17... | collective-permute-start | bytes 49160 | tf_op jit(solution)/shard_map/ppermute | solution.py:131
  216.6 6.5 %collective-permute-done.29 = f32[8,8,64]{2,1,0:T(8,128)S(1)} collective-permute-done((f32[8,8,64]{2,1,0:T(8,128)S(1)}, f32[8,8,64]{2,1,0:T(8,128)S(1)}, u32[]{:S(2)}, u32[]{:S(2)}) %collective-permute-start.29) | collective-permute-done | bytes 16416 | tf_op jit(solution)/shard_map/ppermute | solution.py:131
  (87 shorter events, 25.0 us)
Async XLA Ops:
  2.6 20.8 %collective-permute-start.12 = (bf16[8,64,512]{2,1,0:T(8,128)(2,1)}, bf16[8,64,512]{2,1,0:T(8,128)(2,1)}, u32[]{:S(2)}, u32[]{:S(2)}) collective-permute-start(bf16[8,64,512]{2,1,0:T(8,128)(2,1)} %get-tuple-element.28), channel_id=1, source_target_pairs={{0,248},{1,249},{2,250},{3,251},{4,252},{5,253},{6,254},{7,255},{8... | collective-permute-start | bytes 1572872 | tf_op jit(solution)/shard_map/ppermute | solution.py:131
  3.3 27.5 %collective-permute-start.16 = (bf16[8,64,512]{2,1,0:T(8,128)(2,1)}, bf16[8,64,512]{2,1,0:T(8,128)(2,1)}, u32[]{:S(2)}, u32[]{:S(2)}) collective-permute-start(bf16[8,64,512]{2,1,0:T(8,128)(2,1)} %get-tuple-element.27), channel_id=1, source_target_pairs={{0,8},{1,9},{2,10},{3,11},{4,12},{5,13},{6,14},{7,15},{8,16},{9,17... | collective-permute-start | bytes 1572872 | tf_op jit(solution)/shard_map/ppermute | solution.py:131
  15.9 137.8 %collective-permute-start.4 = (bf16[512,2048]{1,0:T(8,128)(2,1)}, bf16[512,2048]{1,0:T(8,128)(2,1)S(1)}, u32[]{:S(2)}, u32[]{:S(2)}) collective-permute-start(bf16[512,2048]{1,0:T(8,128)(2,1)} %get-tuple-element.14), channel_id=1, source_target_pairs={{0,1},{1,0},{2,3},{3,2},{4,5},{5,4},{6,7},{7,6},{8,9},{9,8},{10,11... | collective-permute-start | bytes 6291464 | tf_op jit(solution)/shard_map/ppermute | solution.py:131
  15.9 28.0 %collective-permute-start.13 = (bf16[8,64,512]{2,1,0:T(8,128)(2,1)}, bf16[8,64,512]{2,1,0:T(8,128)(2,1)S(1)}, u32[]{:S(2)}, u32[]{:S(2)}) collective-permute-start(bf16[8,64,512]{2,1,0:T(8,128)(2,1)} %get-tuple-element.28), channel_id=1, source_target_pairs={{0,254},{1,255},{2,248},{3,249},{4,250},{5,251},{6,252},{7,253},{8... | collective-permute-start | bytes 1572872 | tf_op jit(solution)/shard_map/ppermute | solution.py:131
  16.0 40.9 %collective-permute-start.15 = (bf16[8,64,512]{2,1,0:T(8,128)(2,1)}, bf16[8,64,512]{2,1,0:T(8,128)(2,1)S(1)}, u32[]{:S(2)}, u32[]{:S(2)}) collective-permute-start(bf16[8,64,512]{2,1,0:T(8,128)(2,1)} %get-tuple-element.27), channel_id=1, source_target_pairs={{0,14},{1,15},{2,8},{3,9},{4,10},{5,11},{6,12},{7,13},{8,22},{9,23... | collective-permute-start | bytes 1572872 | tf_op jit(solution)/shard_map/ppermute | solution.py:131
  23.4 25.6 %collective-permute-start.14 = (bf16[8,64,512]{2,1,0:T(8,128)(2,1)}, bf16[8,64,512]{2,1,0:T(8,128)(2,1)}, u32[]{:S(2)}, u32[]{:S(2)}) collective-permute-start(bf16[8,64,512]{2,1,0:T(8,128)(2,1)} %collective-permute-done.12.own), channel_id=1, source_target_pairs={{0,6},{1,7},{2,0},{3,1},{4,2},{5,3},{6,4},{7,5},{8,14},{9,15},{10,... | collective-permute-start | bytes 1572872 | tf_op jit(solution)/shard_map/ppermute | solution.py:131
  30.8 31.4 %collective-permute-start.17 = (bf16[8,64,512]{2,1,0:T(8,128)(2,1)}, bf16[8,64,512]{2,1,0:T(8,128)(2,1)S(1)}, u32[]{:S(2)}, u32[]{:S(2)}) collective-permute-start(bf16[8,64,512]{2,1,0:T(8,128)(2,1)} %collective-permute-done.16.own), channel_id=1, source_target_pairs={{0,6},{1,7},{2,0},{3,1},{4,2},{5,3},{6,4},{7,5},{8,10},{9,11},{10,... | collective-permute-start | bytes 1572872 | tf_op jit(solution)/shard_map/ppermute | solution.py:131
  44.0 33.1 %copy-start.2 = (bf16[8,64,512]{2,1,0:T(8,128)(2,1)}, bf16[8,64,512]{2,1,0:T(8,128)(2,1)S(1)}, u32[]{:S(2)}) copy-start(bf16[8,64,512]{2,1,0:T(8,128)(2,1)S(1)} %collective-permute-done.13.ahead) | copy-start | bytes 1572868
  44.0 32.2 %collective-permute-start = (bf16[4,64,512]{2,1,0:T(8,128)(2,1)S(1)}, bf16[4,64,512]{2,1,0:T(8,128)(2,1)}, u32[]{:S(2)}, u32[]{:S(2)}) collective-permute-start(bf16[4,64,512]{2,1,0:T(8,128)(2,1)S(1)} %get-tuple-element.24), channel_id=1, source_target_pairs={{0,2},{1,3},{2,4},{3,5},{4,6},{5,7},{6,0},{7,1},{8,10},{9,11},{10,... | collective-permute-start | bytes 786440 | tf_op jit(solution)/shard_map/ppermute | solution.py:131
  49.0 28.0 %collective-permute-start.1 = (bf16[4,64,512]{2,1,0:T(8,128)(2,1)}, bf16[4,64,512]{2,1,0:T(8,128)(2,1)S(1)}, u32[]{:S(2)}, u32[]{:S(2)}) collective-permute-start(bf16[4,64,512]{2,1,0:T(8,128)(2,1)} %get-tuple-element.25), channel_id=1, source_target_pairs={{0,2},{1,3},{2,4},{3,5},{4,6},{5,7},{6,0},{7,1},{8,10},{9,11},{10,... | collective-permute-start | bytes 786440 | tf_op jit(solution)/shard_map/ppermute | solution.py:131
  56.9 77.1 %copy-start.1 = (bf16[8,64,512]{2,1,0:T(8,128)(2,1)}, bf16[8,64,512]{2,1,0:T(8,128)(2,1)S(1)}, u32[]{:S(2)}) copy-start(bf16[8,64,512]{2,1,0:T(8,128)(2,1)S(1)} %collective-permute-done.15.ahead) | copy-start | bytes 1572868
  56.9 69.3 %collective-permute-start.3 = (bf16[4,64,512]{2,1,0:T(8,128)(2,1)}, bf16[4,64,512]{2,1,0:T(8,128)(2,1)}, u32[]{:S(2)}, u32[]{:S(2)}) collective-permute-start(bf16[4,64,512]{2,1,0:T(8,128)(2,1)} %get-tuple-element.25), channel_id=1, source_target_pairs={{0,6},{1,7},{2,0},{3,1},{4,2},{5,3},{6,4},{7,5},{8,14},{9,15},{10,... | collective-permute-start | bytes 786440 | tf_op jit(solution)/shard_map/ppermute | solution.py:131
  62.3 63.9 %collective-permute-start.20 = (bf16[8,64,512]{2,1,0:T(8,128)(2,1)}, bf16[8,64,512]{2,1,0:T(8,128)(2,1)}, u32[]{:S(2)}, u32[]{:S(2)}) collective-permute-start(bf16[8,64,512]{2,1,0:T(8,128)(2,1)} %get-tuple-element.23), channel_id=1, source_target_pairs={{0,248},{1,249},{2,250},{3,251},{4,252},{5,253},{6,254},{7,255},{8... | collective-permute-start | bytes 1572872 | tf_op jit(solution)/shard_map/ppermute | solution.py:131
  76.2 55.7 %collective-permute-start.22 = (bf16[8,64,512]{2,1,0:T(8,128)(2,1)}, bf16[8,64,512]{2,1,0:T(8,128)(2,1)}, u32[]{:S(2)}, u32[]{:S(2)}) collective-permute-start(bf16[8,64,512]{2,1,0:T(8,128)(2,1)} %get-tuple-element.22), channel_id=1, source_target_pairs={{0,8},{1,9},{2,10},{3,11},{4,12},{5,13},{6,14},{7,15},{8,16},{9,17... | collective-permute-start | bytes 1572872 | tf_op jit(solution)/shard_map/ppermute | solution.py:131
  77.1 56.9 %collective-permute-start.19 = (bf16[8,64,512]{2,1,0:T(8,128)(2,1)}, bf16[8,64,512]{2,1,0:T(8,128)(2,1)}, u32[]{:S(2)}, u32[]{:S(2)}) collective-permute-start(bf16[8,64,512]{2,1,0:T(8,128)(2,1)} %pad_maximum_fusion.3), channel_id=1, source_target_pairs={{0,6},{1,7},{2,0},{3,1},{4,2},{5,3},{6,4},{7,5},{8,14},{9,15},{10,... | collective-permute-start | bytes 1572872 | tf_op jit(solution)/shard_map/ppermute | solution.py:131
  126.2 10.0 %collective-permute-start.21 = (bf16[8,64,512]{2,1,0:T(8,128)(2,1)}, bf16[8,64,512]{2,1,0:T(8,128)(2,1)S(1)}, u32[]{:S(2)}, u32[]{:S(2)}) collective-permute-start(bf16[8,64,512]{2,1,0:T(8,128)(2,1)} %collective-permute-done.20.c0), channel_id=1, source_target_pairs={{0,1},{1,0},{2,3},{3,2},{4,5},{5,4},{6,7},{7,6},{8,9},{9,8},{10,11... | collective-permute-start | bytes 1572872 | tf_op jit(solution)/shard_map/ppermute | solution.py:131
  126.2 22.2 %collective-permute-start.18 = (bf16[8,64,512]{2,1,0:T(8,128)(2,1)}, bf16[8,64,512]{2,1,0:T(8,128)(2,1)}, u32[]{:S(2)}, u32[]{:S(2)}) collective-permute-start(bf16[8,64,512]{2,1,0:T(8,128)(2,1)} %pad_maximum_fusion.2), channel_id=1, source_target_pairs={{0,2},{1,3},{2,4},{3,5},{4,6},{5,7},{6,0},{7,1},{8,10},{9,11},{10,... | collective-permute-start | bytes 1572872 | tf_op jit(solution)/shard_map/ppermute | solution.py:131
  131.9 41.3 %collective-permute-start.23 = (bf16[8,64,512]{2,1,0:T(8,128)(2,1)}, bf16[8,64,512]{2,1,0:T(8,128)(2,1)}, u32[]{:S(2)}, u32[]{:S(2)}) collective-permute-start(bf16[8,64,512]{2,1,0:T(8,128)(2,1)} %collective-permute-done.22.c0), channel_id=1, source_target_pairs={{0,1},{1,0},{2,3},{3,2},{4,5},{5,4},{6,7},{7,6},{8,9},{9,8},{10,11... | collective-permute-start | bytes 1572872 | tf_op jit(solution)/shard_map/ppermute | solution.py:131
  134.0 53.3 %collective-permute-start.7 = (bf16[8,64,512]{2,1,0:T(8,128)(2,1)}, bf16[8,64,512]{2,1,0:T(8,128)(2,1)S(1)}, u32[]{:S(2)}, u32[]{:S(2)}) collective-permute-start(bf16[8,64,512]{2,1,0:T(8,128)(2,1)} %get-tuple-element.21.c0), channel_id=1, source_target_pairs={{0,1},{1,0},{2,3},{3,2},{4,5},{5,4},{6,7},{7,6},{8,9},{9,8},{10,11... | collective-permute-start | bytes 1572872 | tf_op jit(solution)/shard_map/ppermute | solution.py:131
  136.2 43.4 %collective-permute-start.2 = (bf16[4,64,512]{2,1,0:T(8,128)(2,1)}, bf16[4,64,512]{2,1,0:T(8,128)(2,1)}, u32[]{:S(2)}, u32[]{:S(2)}) collective-permute-start(bf16[4,64,512]{2,1,0:T(8,128)(2,1)} %copy-done.7), channel_id=1, source_target_pairs={{0,6},{1,7},{2,0},{3,1},{4,2},{5,3},{6,4},{7,5},{8,14},{9,15},{10,... | collective-permute-start | bytes 786440 | tf_op jit(solution)/shard_map/ppermute | solution.py:131
  148.4 38.9 %collective-permute-start.5 = (bf16[4,64,512]{2,1,0:T(8,128)(2,1)}, bf16[4,64,512]{2,1,0:T(8,128)(2,1)S(1)}, u32[]{:S(2)}, u32[]{:S(2)}) collective-permute-start(bf16[4,64,512]{2,1,0:T(8,128)(2,1)} %collective-permute-done), channel_id=1, source_target_pairs={{0,2},{1,3},{2,4},{3,5},{4,6},{5,7},{6,0},{7,1},{8,10},{9,11},{10,... | collective-permute-start | bytes 786440 | tf_op jit(solution)/shard_map/ppermute | solution.py:131
  153.7 33.7 %collective-permute-start.6 = (bf16[4,64,512]{2,1,0:T(8,128)(2,1)}, bf16[4,64,512]{2,1,0:T(8,128)(2,1)}, u32[]{:S(2)}, u32[]{:S(2)}) collective-permute-start(bf16[4,64,512]{2,1,0:T(8,128)(2,1)} %collective-permute-done.3), channel_id=1, source_target_pairs={{0,6},{1,7},{2,0},{3,1},{4,2},{5,3},{6,4},{7,5},{8,14},{9,15},{10,... | collective-permute-start | bytes 786440 | tf_op jit(solution)/shard_map/ppermute | solution.py:131
  179.4 16.7 %collective-permute-start.24 = (f32[4,16,8,64]{3,2,1,0:T(8,128)S(1)}, f32[4,16,8,64]{3,2,1,0:T(8,128)S(1)}, u32[]{:S(2)}, u32[]{:S(2)}) collective-permute-start(f32[4,16,8,64]{3,2,1,0:T(8,128)S(1)} %pad_maximum_fusion.4), channel_id=1, source_target_pairs={{0,1},{1,0},{2,3},{3,2},{4,5},{5,4},{6,7},{7,6},{8,9},{9,8},{10,11... | collective-permute-start | bytes 393224 | tf_op jit(solution)/shard_map/ppermute | solution.py:131
  193.5 1.7 collective-permute-start.8
  196.2 10.3 %collective-permute-start.25 = (f32[16,8,64]{2,1,0:T(8,128)S(1)}, f32[16,8,64]{2,1,0:T(8,128)S(1)}, u32[]{:S(2)}, u32[]{:S(2)}) collective-permute-start(f32[16,8,64]{2,1,0:T(8,128)S(1)} %get-tuple-element.37), channel_id=1, source_target_pairs={{0,2},{1,3},{2,4},{3,5},{4,6},{5,7},{6,0},{7,1},{8,10},{9,11},{10,... | collective-permute-start | bytes 98312 | tf_op jit(solution)/shard_map/ppermute | solution.py:131
  198.8 10.5 %collective-permute-start.26 = (f32[16,8,64]{2,1,0:T(8,128)S(1)}, f32[16,8,64]{2,1,0:T(8,128)S(1)}, u32[]{:S(2)}, u32[]{:S(2)}) collective-permute-start(f32[16,8,64]{2,1,0:T(8,128)S(1)} %get-tuple-element.39), channel_id=1, source_target_pairs={{0,6},{1,7},{2,0},{3,1},{4,2},{5,3},{6,4},{7,5},{8,14},{9,15},{10,... | collective-permute-start | bytes 98312 | tf_op jit(solution)/shard_map/ppermute | solution.py:131
  200.4 9.0 %collective-permute-start.27 = (f32[16,8,64]{2,1,0:T(8,128)S(1)}, f32[16,8,64]{2,1,0:T(8,128)S(1)}, u32[]{:S(2)}, u32[]{:S(2)}) collective-permute-start(f32[16,8,64]{2,1,0:T(8,128)S(1)} %get-tuple-element.38), channel_id=1, source_target_pairs={{0,4},{1,5},{2,6},{3,7},{4,0},{5,1},{6,2},{7,3},{8,12},{9,13},{10,... | collective-permute-start | bytes 98312 | tf_op jit(solution)/shard_map/ppermute | solution.py:131
  203.7 11.3 %collective-permute-start.10 = (f32[8,8,64]{2,1,0:T(8,128)S(1)}, f32[8,8,64]{2,1,0:T(8,128)S(1)}, u32[]{:S(2)}, u32[]{:S(2)}) collective-permute-start(f32[8,8,64]{2,1,0:T(8,128)S(1)} %get-tuple-element.42), channel_id=1, source_target_pairs={{0,6},{1,7},{2,0},{3,1},{4,2},{5,3},{6,4},{7,5},{8,14},{9,15},{10,... | collective-permute-start | bytes 49160 | tf_op jit(solution)/shard_map/ppermute | solution.py:131
  205.4 9.6 %collective-permute-start.11 = (f32[8,8,64]{2,1,0:T(8,128)S(1)}, f32[8,8,64]{2,1,0:T(8,128)S(1)}, u32[]{:S(2)}, u32[]{:S(2)}) collective-permute-start(f32[8,8,64]{2,1,0:T(8,128)S(1)} %get-tuple-element.41), channel_id=1, source_target_pairs={{0,4},{1,5},{2,6},{3,7},{4,0},{5,1},{6,2},{7,3},{8,12},{9,13},{10,... | collective-permute-start | bytes 49160 | tf_op jit(solution)/shard_map/ppermute | solution.py:131
  206.5 8.5 %collective-permute-start.9 = (f32[8,8,64]{2,1,0:T(8,128)S(1)}, f32[8,8,64]{2,1,0:T(8,128)S(1)}, u32[]{:S(2)}, u32[]{:S(2)}) collective-permute-start(f32[8,8,64]{2,1,0:T(8,128)S(1)} %get-tuple-element.40), channel_id=1, source_target_pairs={{0,2},{1,3},{2,4},{3,5},{4,6},{5,7},{6,0},{7,1},{8,10},{9,11},{10,... | collective-permute-start | bytes 49160 | tf_op jit(solution)/shard_map/ppermute | solution.py:131
  209.4 7.2 %collective-permute-start.28 = (f32[8,8,64]{2,1,0:T(8,128)S(1)}, f32[8,8,64]{2,1,0:T(8,128)S(1)}, u32[]{:S(2)}, u32[]{:S(2)}) collective-permute-start(f32[8,8,64]{2,1,0:T(8,128)S(1)} %get-tuple-element.43), channel_id=1, source_target_pairs={{0,8},{1,9},{2,10},{3,11},{4,12},{5,13},{6,14},{7,15},{8,16},{9,17... | collective-permute-start | bytes 49160 | tf_op jit(solution)/shard_map/ppermute | solution.py:131
  215.0 8.1 %collective-permute-start.29 = (f32[8,8,64]{2,1,0:T(8,128)S(1)}, f32[8,8,64]{2,1,0:T(8,128)S(1)}, u32[]{:S(2)}, u32[]{:S(2)}) collective-permute-start(f32[8,8,64]{2,1,0:T(8,128)S(1)} %get-tuple-element.44), channel_id=1, source_target_pairs={{0,248},{1,249},{2,250},{3,251},{4,252},{5,253},{6,254},{7,255},{8... | collective-permute-start | bytes 49160 | tf_op jit(solution)/shard_map/ppermute | solution.py:131
  (11 other events, 105.3 us)
where the time goes:
time: 224 us
  starting transfers between devices  79.7 us (36%)
  waiting for transfers between devices  77.8 us (35%)
  Pallas kernels  39 us (17%)
  other arithmetic  14.5 us (6%)
  local copies, waits for them, and re-layouts  12.5 us (6%)
    ppermute x30, starting transfers between devices, send(): return lax.ppermute(x, AXES, moves(owners, quarters, target))  79.7 us
    ppermute x30, waiting for transfers between devices, send(): return lax.ppermute(x, AXES, moves(owners, quarters, target))  77.8 us
    pallas_call x3, Pallas kernels, shards(): pl.pallas_call(functools.partial(first_kernel, group_size, bands, rows),...  17.8 us
    pallas_call x3, Pallas kernels, shards(): pl.pallas_call(functools.partial(last_kernel, (group_size, bands, rows, q...  16 us
    pallas_call x1, Pallas kernels, shards(): pl.pallas_call(functools.partial(restrict_kernel, quarters, rows), grid=(...  5.26 us
  transfers between devices with their start and end apart: 30, of which 8 were waited for; matrix products, arithmetic and copies ran while one was open for 10% of the time, Pallas kernels for 17%

commit v1 on v0

v1 whole, which is shorter than its diff:
```python
import functools

import jax
import jax.numpy as jnp
from jax import lax
from jax.experimental import pallas as pl
from jax.experimental.pallas import tpu as pltpu
from jax.sharding import PartitionSpec as P


prefactor = 0.015625
AXES = ("kr", "kc")
VMEM = pl.BlockSpec(memory_space=pltpu.VMEM)
SMEM = pl.BlockSpec(memory_space=pltpu.SMEM)
CONTRACT_LAST = (((1,), (1,)), ((), ()))


def moves(owners, quarters, target):
    pairs = []
    for i in range(owners):
        for k in range(quarters):
            for c in range(2):
                ti, tk, tc = target(i, k, c)
                pairs.append(
                    (
                        (i * quarters + k) * 2 + c,
                        ((ti % owners) * quarters + tk % quarters) * 2 + tc,
                    )
                )
    return pairs


def turn(group, q, owners):
    if group == 1:
        return -1 if q == owners - 1 else 1
    if group == 2:
        return 1 if q == 0 else -1
    return 1


def where_am_i():
    place = lax.axis_index("kc")
    return lax.axis_index("kr"), lax.div(place, 2), lax.rem(place, 2)


def heading(group, owner, owners):
    if group == 1:
        return jnp.where(owner == owners - 1, -1, 1)
    if group == 2:
        return jnp.where(owner == 0, 1, -1)
    return jnp.int32(1)


def restrict_kernel(quarters, rows, spheres_ref, slab_ref, mine_ref, give_ref):
    owner, quarter, core = where_am_i()
    sphere = spheres_ref[owner]
    block = slab_ref.shape[0]
    first = (2 * quarter + core) * rows + pl.program_id(0) * block
    row = first + lax.broadcasted_iota(jnp.int32, (block, rows), 0)
    col = lax.broadcasted_iota(jnp.int32, (block, rows), 1)
    row_inside = row < sphere
    even = core == 0
    for j in range(quarters):
        kept = []
        for t in range(2):
            at = (2 * j + t) * rows
            keep = row_inside & (at + col < sphere)
            x = slab_ref[:, at : at + rows].astype(jnp.float32)
            kept.append(jnp.where(keep, x, 0.0))
        span = pl.ds(j * rows, rows)
        mine_ref[:, span] = jnp.where(even, kept[0], kept[1]).astype(mine_ref.dtype)
        give_ref[:, span] = jnp.where(even, kept[1], kept[0]).astype(give_ref.dtype)


def forward_kernel(owners, half, a1, b1, a2, b2, up_ref, down_ref):
    owner, _, _ = where_am_i()
    for n, (a, b) in enumerate(((a1, b1), (a2, b2))):
        ahead_up = heading(n + 1, owner, owners) > 0

        @pl.when(ahead_up)
        def _():
            up_ref[n * half : (n + 1) * half] = a[:half]
            down_ref[n * half : (n + 1) * half] = b[half:]

        @pl.when(jnp.logical_not(ahead_up))
        def _():
            up_ref[n * half : (n + 1) * half] = b[:half]
            down_ref[n * half : (n + 1) * half] = a[half:]


def flat(x):
    x = x[...]
    return x.reshape(x.shape[0] * x.shape[1], x.shape[2])


def first_kernel(group, owners, quarters, counts, *refs):
    blocks, (w0, w1, acc) = refs[:-3], refs[-3:]
    owner, quarter, _ = where_am_i()
    rows = acc.shape[2]
    sigma = heading(group, owner, owners)
    columns = (
        quarter,
        lax.rem(quarter - sigma + quarters, quarters),
        lax.rem(quarter + sigma + quarters, quarters),
    )
    for s, w in enumerate((w0, w1)):
        base, size = 0, acc.shape[1]
        for h in range(counts):
            total = None
            for n in range(3):
                pieces = blocks[n * counts : (n + 1) * counts]
                at = pl.multiple_of(columns[n] * rows, rows)
                y = lax.dot_general(
                    flat(pieces[h]),
                    w[:, pl.ds(at, rows)],
                    CONTRACT_LAST,
                    preferred_element_type=jnp.float32,
                )
                total = y if total is None else total + y
            acc[s, base : base + size // counts] = total
            base += size // counts


def last_kernel(groups, quarters, half, *refs):
    accs, refs = refs[:groups], refs[groups:]
    far, (w0, w1), refs = refs[:2], refs[2:4], refs[4:]
    conduction, (keep_ref, give_ref) = refs[:-2], refs[-2:]
    _, quarter, core = where_am_i()
    bands, rows = far[0].shape[1:]
    at = pl.multiple_of(lax.rem(quarter + 2, quarters) * rows, rows)
    even = core == 0
    for g in range(groups):
        for h, x in enumerate(far):
            base = h * half * bands
            both = []
            for s, w in enumerate((w0, w1)):
                y = accs[g][s, base : base + half * bands] + lax.dot_general(
                    x[g * half : (g + 1) * half].reshape(half * bands, rows),
                    w[:, pl.ds(at, rows)],
                    CONTRACT_LAST,
                    preferred_element_type=jnp.float32,
                )
                high = y.astype(jnp.bfloat16)
                low = (y - high.astype(jnp.float32)).astype(jnp.bfloat16)
                both.append((high, low))
            for n in range(half):
                p = h * half + n
                part = None
                for s in range(2):
                    c = conduction[2 * g + s]
                    span = slice(n * bands, (n + 1) * bands)
                    y = lax.dot_general(
                        c[p],
                        jnp.concatenate([both[s][0][span], both[s][1][span]], 0),
                        CONTRACT_LAST,
                        preferred_element_type=jnp.float32,
                    )
                    part = y if part is None else part + y
                part = (part[:, :bands] + part[:, bands:]) * prefactor
                part = part.reshape(quarters, 2, -1, bands)
                for j in range(quarters):
                    d = lax.rem(j - quarter + quarters, quarters)
                    q = g * 2 * half + p
                    keep_ref[d, q] = jnp.where(even, part[j, 0], part[j, 1])
                    give_ref[d, q] = jnp.where(even, part[j, 1], part[j, 0])


def shards(pair_conduction, pair_valence, screened, sphere_sizes):
    owners = lax.axis_size("kr")
    quarters = lax.axis_size("kc") // 2
    rows, gvectors = screened.shape[1:]
    group_size = pair_valence.shape[0] // 3
    bands = pair_valence.shape[1]
    cbands = pair_conduction.shape[1]
    half = group_size // 2
    shift = (0, -1, 1)
    params = pltpu.CompilerParams(vmem_limit_bytes=24 * 2**20)

    def send(x, target):
        return lax.ppermute(x, AXES, moves(owners, quarters, target))

    def swap(x):
        return send(x, lambda i, k, c: (i, k, 1 - c))

    def call(body, out_shape, operands, in_specs=None, out_specs=None, **kw):
        many = isinstance(out_shape, list)
        return pl.pallas_call(
            body,
            in_specs=in_specs or [VMEM] * len(operands),
            out_specs=out_specs or ([VMEM] * len(out_shape) if many else VMEM),
            out_shape=out_shape,
            compiler_params=params,
            **kw,
        )(*operands)

    v = [pair_valence[g * group_size : (g + 1) * group_size] for g in range(3)]
    cond = [pair_conduction[g * group_size : (g + 1) * group_size] for g in range(3)]

    own, ahead, behind = {}, {}, {}
    for g in (1, 2):
        own[g] = send(v[g], lambda i, k, c: (i + shift[g], k, c))
    for g in (1, 2):
        ahead[g] = send(
            v[g],
            lambda i, k, c: (
                i + shift[g],
                k + turn(g, (i + shift[g]) % owners, owners),
                c,
            ),
        )
    c_own = {0: cond[0]}
    for g in (1, 2):
        c_own[g] = send(cond[g], lambda i, k, c: (i + shift[g], k, c))
    for g in (1, 2):
        behind[g] = send(own[g], lambda i, k, c: (i, k - turn(g, i, owners), c))
    v0 = [v[0][:half], v[0][half:]]
    up, down = [None, None], [None, None]
    for n in range(2):
        up[n] = send(v0[n], lambda i, k, c: (i, k + 1, c))
        down[1 - n] = send(v0[1 - n], lambda i, k, c: (i, k - 1, c))
    going_up, going_down = call(
        functools.partial(forward_kernel, owners, half),
        [jax.ShapeDtypeStruct(v[0].shape, v[0].dtype)] * 2,
        (ahead[1], behind[1], ahead[2], behind[2]),
    )
    far = (
        send(going_up, lambda i, k, c: (i, k + 1, c)),
        send(going_down, lambda i, k, c: (i, k - 1, c)),
    )
    far0 = (
        send(up[0], lambda i, k, c: (i, k + 1, c)),
        send(down[1], lambda i, k, c: (i, k - 1, c)),
    )

    block = rows // 4
    w0, give = call(
        functools.partial(restrict_kernel, quarters, rows),
        [jax.ShapeDtypeStruct((rows, gvectors // 2), screened.dtype)] * 2,
        (sphere_sizes, screened[0]),
        in_specs=[SMEM, pl.BlockSpec((block, gvectors), lambda r: (r, 0))],
        out_specs=[pl.BlockSpec((block, gvectors // 2), lambda r: (r, 0))] * 2,
        grid=(rows // block,),
    )
    w1 = swap(give)
    c_par = {g: swap(c_own[g]) for g in range(3)}

    def first(g, counts, blocks):
        return call(
            functools.partial(first_kernel, g, owners, quarters, counts),
            jax.ShapeDtypeStruct((2, group_size * bands, rows), jnp.float32),
            (*blocks, w0, w1),
        )

    def last(groups, accs, far):
        shape = (
            quarters,
            len(groups) * group_size,
            cbands // quarters // 2,
            bands,
        )
        conduction = [x[g] for g in groups for x in (c_own, c_par)]
        return call(
            functools.partial(last_kernel, len(groups), quarters, half),
            [jax.ShapeDtypeStruct(shape, jnp.float32)] * 2,
            (*accs, *far, w0, w1, *conduction),
        )

    def exchange(keep, give):
        keep = keep + swap(give)
        parts = [send(keep[d], lambda i, k, c: (i, k + d, c)) for d in (1, 3, 2)]
        return keep[0] + parts[0] + parts[1] + parts[2]

    accs = [first(g, 1, (own[g], ahead[g], behind[g])) for g in (1, 2)]
    both = exchange(*last((1, 2), accs, far))
    results = [
        send(
            both[(g - 1) * group_size : g * group_size],
            lambda i, k, c: (i - shift[g], k, c),
        )
        for g in (1, 2)
    ]
    acc = first(0, 2, (*v0, *up, *down))
    results.insert(0, exchange(*last((0,), [acc], far0)))
    return jnp.concatenate(results, 0)


def solution(mesh):
    return jax.shard_map(
        shards,
        mesh=mesh,
        in_specs=(P("kr", None, "kc"), P("kr", None, "kc"), P("kr", "kc", None), P()),
        out_specs=P("kr", "kc", None),
        check_vma=False,
    )
```

time: 224 us -> 196 us (0.88)
  the two profiles are of different devices: /device:TPU:30 before, /device:TPU:96 now
where the time goes in v1:
time: 196 us
  waiting for transfers between devices  107 us (55%)
  starting transfers between devices  72.5 us (37%)
  Pallas kernels  12.1 us (6%)
  local copies, waits for them, and re-layouts  3.15 us (2%)
    ppermute x30, waiting for transfers between devices, send(): return lax.ppermute(x, AXES, moves(owners, quarters, target))  107 us
    ppermute x30, starting transfers between devices, send(): return lax.ppermute(x, AXES, moves(owners, quarters, target))  72.5 us
    pallas_call x7, Pallas kernels, call(): pl.pallas_call(body, in_specs=in_specs or [VMEM] * len(operands), out_spe...  12.1 us
  transfers between devices with their start and end apart: 30, of which 12 were waited for; matrix products, arithmetic and copies ran while one was open for 0% of the time, Pallas kernels for 5%

profile of v1, /device:TPU:96, one launch (start us, length us, event | category | flops | bytes accessed | tf_op | source)
XLA Modules:
  0.0 196.2 jit_solution(10976654464316523848)
XLA Ops:
  0.0 2.2 %copy-done = bf16[1,512,4096]{2,1,0:T(8,128)(2,1)S(1)} copy-done((bf16[1,512,4096]{2,1,0:T(8,128)(2,1)S(1)}, bf16[1,512,4096]{2,1,0:T(8,128)(2,1)}, u32[]{:S(2)}) %copy-start) | copy-done | bytes 4194328
  2.8 2.0 %shard_map.46 = (bf16[512,2048]{1,0:T(8,128)(2,1)S(1)}, bf16[512,2048]{1,0:T(8,128)(2,1)S(1)}) custom-call(s32[32]{0:T(128)S(1)} %copy-done.1, bf16[512,4096]{1,0:T(8,128)(2,1)S(1)} %bitcast.29), custom_call_target="tpu_custom_call" | custom-call | tf_op jit(solution)/shard_map/pallas_call | solution.py:187
  5.1 4.8 %collective-permute-start.12 = (bf16[8,64,512]{2,1,0:T(8,128)(2,1)S(1)}, bf16[8,64,512]{2,1,0:T(8,128)(2,1)S(1)}, u32[]{:S(2)}, u32[]{:S(2)}) collective-permute-start(bf16[8,64,512]{2,1,0:T(8,128)(2,1)S(1)} %get-tuple-element.27), channel_id=1, source_target_pairs={{0,248},{1,249},{2,250},{3,251},{4,252},{5,253},{6,254},{7,255},{8... | collective-permute-start | bytes 1572872 | tf_op jit(solution)/shard_map/ppermute | solution.py:180
  9.9 3.8 %collective-permute-start.13 = (bf16[8,64,512]{2,1,0:T(8,128)(2,1)S(1)}, bf16[8,64,512]{2,1,0:T(8,128)(2,1)S(1)}, u32[]{:S(2)}, u32[]{:S(2)}) collective-permute-start(bf16[8,64,512]{2,1,0:T(8,128)(2,1)S(1)} %get-tuple-element.27), channel_id=1, source_target_pairs={{0,254},{1,255},{2,248},{3,249},{4,250},{5,251},{6,252},{7,253},{8... | collective-permute-start | bytes 1572872 | tf_op jit(solution)/shard_map/ppermute | solution.py:180
  13.7 2.2 %collective-permute-start.15 = (bf16[8,64,512]{2,1,0:T(8,128)(2,1)S(1)}, bf16[8,64,512]{2,1,0:T(8,128)(2,1)S(1)}, u32[]{:S(2)}, u32[]{:S(2)}) collective-permute-start(bf16[8,64,512]{2,1,0:T(8,128)(2,1)S(1)} %get-tuple-element.26), channel_id=1, source_target_pairs={{0,8},{1,9},{2,10},{3,11},{4,12},{5,13},{6,14},{7,15},{8,16},{9,17... | collective-permute-start | bytes 1572872 | tf_op jit(solution)/shard_map/ppermute | solution.py:180
  16.0 15.8 %collective-permute-done.12.refs_0_ = bf16[8,64,512]{2,1,0:T(8,128)(2,1)S(1)} collective-permute-done((bf16[8,64,512]{2,1,0:T(8,128)(2,1)S(1)}, bf16[8,64,512]{2,1,0:T(8,128)(2,1)S(1)}, u32[]{:S(2)}, u32[]{:S(2)}) %collective-permute-start.12) | collective-permute-done | bytes 524320 | tf_op jit(solution)/shard_map/ppermute | solution.py:180
  31.9 12.1 %collective-permute-start.20 = (bf16[8,64,512]{2,1,0:T(8,128)(2,1)S(1)}, bf16[8,64,512]{2,1,0:T(8,128)(2,1)S(1)}, u32[]{:S(2)}, u32[]{:S(2)}) collective-permute-start(bf16[8,64,512]{2,1,0:T(8,128)(2,1)S(1)} %get-tuple-element.23), channel_id=1, source_target_pairs={{0,248},{1,249},{2,250},{3,251},{4,252},{5,253},{6,254},{7,255},{8... | collective-permute-start | bytes 1572872 | tf_op jit(solution)/shard_map/ppermute | solution.py:180
  44.0 34.1 %collective-permute-done.15.refs_0_ = bf16[8,64,512]{2,1,0:T(8,128)(2,1)S(1)} collective-permute-done((bf16[8,64,512]{2,1,0:T(8,128)(2,1)S(1)}, bf16[8,64,512]{2,1,0:T(8,128)(2,1)S(1)}, u32[]{:S(2)}, u32[]{:S(2)}) %collective-permute-start.15) | collective-permute-done | bytes 524320 | tf_op jit(solution)/shard_map/ppermute | solution.py:180
  78.1 4.0 %collective-permute-done.16.refs_1_.a2 = bf16[8,64,512]{2,1,0:T(8,128)(2,1)S(1)} collective-permute-done((bf16[8,64,512]{2,1,0:T(8,128)(2,1)S(1)}, bf16[8,64,512]{2,1,0:T(8,128)(2,1)S(1)}, u32[]{:S(2)}, u32[]{:S(2)}) %collective-permute-start.16) | collective-permute-done | bytes 524320 | tf_op jit(solution)/shard_map/ppermute | solution.py:180
  82.1 17.2 %collective-permute-start.17 = (bf16[8,64,512]{2,1,0:T(8,128)(2,1)S(1)}, bf16[8,64,512]{2,1,0:T(8,128)(2,1)S(1)}, u32[]{:S(2)}, u32[]{:S(2)}) collective-permute-start(bf16[8,64,512]{2,1,0:T(8,128)(2,1)S(1)} %collective-permute-done.15.refs_0_), channel_id=1, source_target_pairs={{0,6},{1,7},{2,0},{3,1},{4,2},{5,3},{6,4},{7,5},{8,10},{9,11},{10,... | collective-permute-start | bytes 1572872 | tf_op jit(solution)/shard_map/ppermute | solution.py:180
  99.4 16.4 %collective-permute-done.20.refs_6_ = bf16[8,64,512]{2,1,0:T(8,128)(2,1)S(1)} collective-permute-done((bf16[8,64,512]{2,1,0:T(8,128)(2,1)S(1)}, bf16[8,64,512]{2,1,0:T(8,128)(2,1)S(1)}, u32[]{:S(2)}, u32[]{:S(2)}) %collective-permute-start.20) | collective-permute-done | bytes 524320 | tf_op jit(solution)/shard_map/ppermute | solution.py:180
  115.8 6.2 %collective-permute-start = (bf16[4,64,512]{2,1,0:T(8,128)(2,1)S(1)}, bf16[4,64,512]{2,1,0:T(8,128)(2,1)S(1)}, u32[]{:S(2)}, u32[]{:S(2)}) collective-permute-start(bf16[4,64,512]{2,1,0:T(8,128)(2,1)S(1)} %get-tuple-element.25.refs_0_), channel_id=1, source_target_pairs={{0,2},{1,3},{2,4},{3,5},{4,6},{5,7},{6,0},{7,1},{8,10},{9,11},{10,... | collective-permute-start | bytes 786440 | tf_op jit(solution)/shard_map/ppermute | solution.py:180
  122.0 13.4 %collective-permute-done.14.refs_2_.b1 = bf16[8,64,512]{2,1,0:T(8,128)(2,1)S(1)} collective-permute-done((bf16[8,64,512]{2,1,0:T(8,128)(2,1)S(1)}, bf16[8,64,512]{2,1,0:T(8,128)(2,1)S(1)}, u32[]{:S(2)}, u32[]{:S(2)}) %collective-permute-start.14) | collective-permute-done | bytes 524320 | tf_op jit(solution)/shard_map/ppermute | solution.py:180
  136.0 1.0 collective-permute-start.18
  137.1 3.8 %collective-permute-done.3.refs_5_ = bf16[4,64,512]{2,1,0:T(8,128)(2,1)S(1)} collective-permute-done((bf16[4,64,512]{2,1,0:T(8,128)(2,1)S(1)}, bf16[4,64,512]{2,1,0:T(8,128)(2,1)S(1)}, u32[]{:S(2)}, u32[]{:S(2)}) %collective-permute-start.3) | collective-permute-done | bytes 262176 | tf_op jit(solution)/shard_map/ppermute | solution.py:180
  140.9 4.4 %collective-permute-start.1 = (bf16[4,64,512]{2,1,0:T(8,128)(2,1)S(1)}, bf16[4,64,512]{2,1,0:T(8,128)(2,1)S(1)}, u32[]{:S(2)}, u32[]{:S(2)}) collective-permute-start(bf16[4,64,512]{2,1,0:T(8,128)(2,1)S(1)} %get-tuple-element.24.refs_1_), channel_id=1, source_target_pairs={{0,2},{1,3},{2,4},{3,5},{4,6},{5,7},{6,0},{7,1},{8,10},{9,11},{10,... | collective-permute-start | bytes 786440 | tf_op jit(solution)/shard_map/ppermute | solution.py:180
  145.3 6.5 %collective-permute-done.18.refs_2_ = bf16[8,64,512]{2,1,0:T(8,128)(2,1)S(1)} collective-permute-done((bf16[8,64,512]{2,1,0:T(8,128)(2,1)S(1)}, bf16[8,64,512]{2,1,0:T(8,128)(2,1)S(1)}, u32[]{:S(2)}, u32[]{:S(2)}) %collective-permute-start.18) | collective-permute-done | bytes 524320 | tf_op jit(solution)/shard_map/ppermute | solution.py:180
  151.8 6.0 %collective-permute-done.19.refs_3_ = bf16[8,64,512]{2,1,0:T(8,128)(2,1)S(1)} collective-permute-done((bf16[8,64,512]{2,1,0:T(8,128)(2,1)S(1)}, bf16[8,64,512]{2,1,0:T(8,128)(2,1)S(1)}, u32[]{:S(2)}, u32[]{:S(2)}) %collective-permute-start.19) | collective-permute-done | bytes 524320 | tf_op jit(solution)/shard_map/ppermute | solution.py:180
  157.8 2.9 %collective-permute-start.6 = (bf16[4,64,512]{2,1,0:T(8,128)(2,1)S(1)}, bf16[4,64,512]{2,1,0:T(8,128)(2,1)S(1)}, u32[]{:S(2)}, u32[]{:S(2)}) collective-permute-start(bf16[4,64,512]{2,1,0:T(8,128)(2,1)S(1)} %collective-permute-done.3.refs_5_), channel_id=1, source_target_pairs={{0,6},{1,7},{2,0},{3,1},{4,2},{5,3},{6,4},{7,5},{8,14},{9,15},{10,... | collective-permute-start | bytes 786440 | tf_op jit(solution)/shard_map/ppermute | solution.py:180
  160.8 1.8 shard_map.49.refs_0_
  162.6 1.8 shard_map.50.refs_1_
  164.4 2.9 %shard_map.52 = (f32[4,16,8,64]{3,2,1,0:T(8,128)S(1)}, f32[4,16,8,64]{3,2,1,0:T(8,128)S(1)}) custom-call(f32[2,512,512]{2,1,0:T(8,128)S(1)} %shard_map.49.refs_0_, f32[2,512,512]{2,1,0:T(8,128)S(1)} %shard_map.50.refs_1_, bf16[8,64,512]{2,1,0:T(8,128)(2,1)S(1)} %collective-permute-done.18.refs_2_, bf16[8,64,512]{2,1,0:T(8,128)(2,1)S(1)} %collective-permute-done.19.refs_3_, ...), custom_call_target="tpu_custom_call" | custom-call | tf_op jit(solution)/shard_map/pallas_call | solution.py:187
  167.5 1.8 shard_map.47.refs_0_
  169.4 1.6 shard_map.48
  171.5 1.0 collective-permute-done.8
  172.9 3.5 %collective-permute-start.26 = (f32[16,8,64]{2,1,0:T(8,128)S(1)}, f32[16,8,64]{2,1,0:T(8,128)S(1)}, u32[]{:S(2)}, u32[]{:S(2)}) collective-permute-start(f32[16,8,64]{2,1,0:T(8,128)S(1)} %get-tuple-element.30), channel_id=1, source_target_pairs={{0,6},{1,7},{2,0},{3,1},{4,2},{5,3},{6,4},{7,5},{8,14},{9,15},{10,... | collective-permute-start | bytes 98312 | tf_op jit(solution)/shard_map/ppermute | solution.py:180
  176.5 0.7 collective-permute-start.25
  177.2 5.9 %collective-permute-start.11 = (f32[8,8,64]{2,1,0:T(8,128)S(1)}, f32[8,8,64]{2,1,0:T(8,128)S(1)}, u32[]{:S(2)}, u32[]{:S(2)}) collective-permute-start(f32[8,8,64]{2,1,0:T(8,128)S(1)} %get-tuple-element.32), channel_id=1, source_target_pairs={{0,4},{1,5},{2,6},{3,7},{4,0},{5,1},{6,2},{7,3},{8,12},{9,13},{10,... | collective-permute-start | bytes 49160 | tf_op jit(solution)/shard_map/ppermute | solution.py:180
  183.2 4.0 %collective-permute-start.9 = (f32[8,8,64]{2,1,0:T(8,128)S(1)}, f32[8,8,64]{2,1,0:T(8,128)S(1)}, u32[]{:S(2)}, u32[]{:S(2)}) collective-permute-start(f32[8,8,64]{2,1,0:T(8,128)S(1)} %get-tuple-element.31), channel_id=1, source_target_pairs={{0,2},{1,3},{2,4},{3,5},{4,6},{5,7},{6,0},{7,1},{8,10},{9,11},{10,... | collective-permute-start | bytes 49160 | tf_op jit(solution)/shard_map/ppermute | solution.py:180
  187.4 2.0 %collective-permute-start.28 = (f32[8,8,64]{2,1,0:T(8,128)S(1)}, f32[8,8,64]{2,1,0:T(8,128)S(1)}, u32[]{:S(2)}, u32[]{:S(2)}) collective-permute-start(f32[8,8,64]{2,1,0:T(8,128)S(1)} %get-tuple-element.34), channel_id=1, source_target_pairs={{0,8},{1,9},{2,10},{3,11},{4,12},{5,13},{6,14},{7,15},{8,16},{9,17... | collective-permute-start | bytes 49160 | tf_op jit(solution)/shard_map/ppermute | solution.py:180
  189.4 1.9 collective-permute-done.29
  191.3 4.3 %collective-permute-done.28 = f32[8,8,64]{2,1,0:T(8,128)S(1)} collective-permute-done((f32[8,8,64]{2,1,0:T(8,128)S(1)}, f32[8,8,64]{2,1,0:T(8,128)S(1)}, u32[]{:S(2)}, u32[]{:S(2)}) %collective-permute-start.28) | collective-permute-done | bytes 16416 | tf_op jit(solution)/shard_map/ppermute | solution.py:180
  (54 shorter events, 3.6 us)
Async XLA Ops:
  0.0 2.2 %copy-start = (bf16[1,512,4096]{2,1,0:T(8,128)(2,1)S(1)}, bf16[1,512,4096]{2,1,0:T(8,128)(2,1)}, u32[]{:S(2)}) copy-start(bf16[1,512,4096]{2,1,0:T(8,128)(2,1)} %param.6) | copy-start | bytes 12582916
  4.9 11.0 %copy-start.2 = (bf16[24,64,512]{2,1,0:T(8,128)(2,1)S(1)}, bf16[24,64,512]{2,1,0:T(8,128)(2,1)}, u32[]{:S(2)}) copy-start(bf16[24,64,512]{2,1,0:T(8,128)(2,1)} %param.4) | copy-start | bytes 4718596
  4.9 152.9 %collective-permute-start.4 = (bf16[512,2048]{1,0:T(8,128)(2,1)S(1)}, bf16[512,2048]{1,0:T(8,128)(2,1)S(1)}, u32[]{:S(2)}, u32[]{:S(2)}) collective-permute-start(bf16[512,2048]{1,0:T(8,128)(2,1)S(1)} %get-tuple-element.14), channel_id=1, source_target_pairs={{0,1},{1,0},{2,3},{3,2},{4,5},{5,4},{6,7},{7,6},{8,9},{9,8},{10,11... | collective-permute-start | bytes 6291464 | tf_op jit(solution)/shard_map/ppermute | solution.py:180
  5.1 26.8 %collective-permute-start.12 = (bf16[8,64,512]{2,1,0:T(8,128)(2,1)S(1)}, bf16[8,64,512]{2,1,0:T(8,128)(2,1)S(1)}, u32[]{:S(2)}, u32[]{:S(2)}) collective-permute-start(bf16[8,64,512]{2,1,0:T(8,128)(2,1)S(1)} %get-tuple-element.27), channel_id=1, source_target_pairs={{0,248},{1,249},{2,250},{3,251},{4,252},{5,253},{6,254},{7,255},{8... | collective-permute-start | bytes 1572872 | tf_op jit(solution)/shard_map/ppermute | solution.py:180
  9.9 34.1 %collective-permute-start.13 = (bf16[8,64,512]{2,1,0:T(8,128)(2,1)S(1)}, bf16[8,64,512]{2,1,0:T(8,128)(2,1)S(1)}, u32[]{:S(2)}, u32[]{:S(2)}) collective-permute-start(bf16[8,64,512]{2,1,0:T(8,128)(2,1)S(1)} %get-tuple-element.27), channel_id=1, source_target_pairs={{0,254},{1,255},{2,248},{3,249},{4,250},{5,251},{6,252},{7,253},{8... | collective-permute-start | bytes 1572872 | tf_op jit(solution)/shard_map/ppermute | solution.py:180
  13.7 64.4 %collective-permute-start.15 = (bf16[8,64,512]{2,1,0:T(8,128)(2,1)S(1)}, bf16[8,64,512]{2,1,0:T(8,128)(2,1)S(1)}, u32[]{:S(2)}, u32[]{:S(2)}) collective-permute-start(bf16[8,64,512]{2,1,0:T(8,128)(2,1)S(1)} %get-tuple-element.26), channel_id=1, source_target_pairs={{0,8},{1,9},{2,10},{3,11},{4,12},{5,13},{6,14},{7,15},{8,16},{9,17... | collective-permute-start | bytes 1572872 | tf_op jit(solution)/shard_map/ppermute | solution.py:180
  15.9 66.3 %collective-permute-start.16 = (bf16[8,64,512]{2,1,0:T(8,128)(2,1)S(1)}, bf16[8,64,512]{2,1,0:T(8,128)(2,1)S(1)}, u32[]{:S(2)}, u32[]{:S(2)}) collective-permute-start(bf16[8,64,512]{2,1,0:T(8,128)(2,1)S(1)} %get-tuple-element.26), channel_id=1, source_target_pairs={{0,14},{1,15},{2,8},{3,9},{4,10},{5,11},{6,12},{7,13},{8,22},{9,23... | collective-permute-start | bytes 1572872 | tf_op jit(solution)/shard_map/ppermute | solution.py:180
  31.9 84.0 %collective-permute-start.20 = (bf16[8,64,512]{2,1,0:T(8,128)(2,1)S(1)}, bf16[8,64,512]{2,1,0:T(8,128)(2,1)S(1)}, u32[]{:S(2)}, u32[]{:S(2)}) collective-permute-start(bf16[8,64,512]{2,1,0:T(8,128)(2,1)S(1)} %get-tuple-element.23), channel_id=1, source_target_pairs={{0,248},{1,249},{2,250},{3,251},{4,252},{5,253},{6,254},{7,255},{8... | collective-permute-start | bytes 1572872 | tf_op jit(solution)/shard_map/ppermute | solution.py:180
  44.0 78.0 %collective-permute-start.22 = (bf16[8,64,512]{2,1,0:T(8,128)(2,1)S(1)}, bf16[8,64,512]{2,1,0:T(8,128)(2,1)S(1)}, u32[]{:S(2)}, u32[]{:S(2)}) collective-permute-start(bf16[8,64,512]{2,1,0:T(8,128)(2,1)S(1)} %get-tuple-element.22), channel_id=1, source_target_pairs={{0,8},{1,9},{2,10},{3,11},{4,12},{5,13},{6,14},{7,15},{8,16},{9,17... | collective-permute-start | bytes 1572872 | tf_op jit(solution)/shard_map/ppermute | solution.py:180
  78.1 57.3 %collective-permute-start.14 = (bf16[8,64,512]{2,1,0:T(8,128)(2,1)S(1)}, bf16[8,64,512]{2,1,0:T(8,128)(2,1)S(1)}, u32[]{:S(2)}, u32[]{:S(2)}) collective-permute-start(bf16[8,64,512]{2,1,0:T(8,128)(2,1)S(1)} %collective-permute-done.12.refs_0_), channel_id=1, source_target_pairs={{0,6},{1,7},{2,0},{3,1},{4,2},{5,3},{6,4},{7,5},{8,14},{9,15},{10,... | collective-permute-start | bytes 1572872 | tf_op jit(solution)/shard_map/ppermute | solution.py:180
  82.1 53.3 %collective-permute-start.17 = (bf16[8,64,512]{2,1,0:T(8,128)(2,1)S(1)}, bf16[8,64,512]{2,1,0:T(8,128)(2,1)S(1)}, u32[]{:S(2)}, u32[]{:S(2)}) collective-permute-start(bf16[8,64,512]{2,1,0:T(8,128)(2,1)S(1)} %collective-permute-done.15.refs_0_), channel_id=1, source_target_pairs={{0,6},{1,7},{2,0},{3,1},{4,2},{5,3},{6,4},{7,5},{8,10},{9,11},{10,... | collective-permute-start | bytes 1572872 | tf_op jit(solution)/shard_map/ppermute | solution.py:180
  115.8 20.2 %collective-permute-start = (bf16[4,64,512]{2,1,0:T(8,128)(2,1)S(1)}, bf16[4,64,512]{2,1,0:T(8,128)(2,1)S(1)}, u32[]{:S(2)}, u32[]{:S(2)}) collective-permute-start(bf16[4,64,512]{2,1,0:T(8,128)(2,1)S(1)} %get-tuple-element.25.refs_0_), channel_id=1, source_target_pairs={{0,2},{1,3},{2,4},{3,5},{4,6},{5,7},{6,0},{7,1},{8,10},{9,11},{10,... | collective-permute-start | bytes 786440 | tf_op jit(solution)/shard_map/ppermute | solution.py:180
  122.0 18.9 %collective-permute-start.3 = (bf16[4,64,512]{2,1,0:T(8,128)(2,1)S(1)}, bf16[4,64,512]{2,1,0:T(8,128)(2,1)S(1)}, u32[]{:S(2)}, u32[]{:S(2)}) collective-permute-start(bf16[4,64,512]{2,1,0:T(8,128)(2,1)S(1)} %get-tuple-element.24.refs_1_), channel_id=1, source_target_pairs={{0,6},{1,7},{2,0},{3,1},{4,2},{5,3},{6,4},{7,5},{8,14},{9,15},{10,... | collective-permute-start | bytes 786440 | tf_op jit(solution)/shard_map/ppermute | solution.py:180
  135.4 5.5 %collective-permute-start.21 = (bf16[8,64,512]{2,1,0:T(8,128)(2,1)S(1)}, bf16[8,64,512]{2,1,0:T(8,128)(2,1)S(1)}, u32[]{:S(2)}, u32[]{:S(2)}) collective-permute-start(bf16[8,64,512]{2,1,0:T(8,128)(2,1)S(1)} %collective-permute-done.20.refs_6_), channel_id=1, source_target_pairs={{0,1},{1,0},{2,3},{3,2},{4,5},{5,4},{6,7},{7,6},{8,9},{9,8},{10,11... | collective-permute-start | bytes 1572872 | tf_op jit(solution)/shard_map/ppermute | solution.py:180
  135.4 5.5 %collective-permute-start.23 = (bf16[8,64,512]{2,1,0:T(8,128)(2,1)S(1)}, bf16[8,64,512]{2,1,0:T(8,128)(2,1)S(1)}, u32[]{:S(2)}, u32[]{:S(2)}) collective-permute-start(bf16[8,64,512]{2,1,0:T(8,128)(2,1)S(1)} %collective-permute-done.22.refs_8_), channel_id=1, source_target_pairs={{0,1},{1,0},{2,3},{3,2},{4,5},{5,4},{6,7},{7,6},{8,9},{9,8},{10,11... | collective-permute-start | bytes 1572872 | tf_op jit(solution)/shard_map/ppermute | solution.py:180
  136.0 15.8 %collective-permute-start.18 = (bf16[8,64,512]{2,1,0:T(8,128)(2,1)S(1)}, bf16[8,64,512]{2,1,0:T(8,128)(2,1)S(1)}, u32[]{:S(2)}, u32[]{:S(2)}) collective-permute-start(bf16[8,64,512]{2,1,0:T(8,128)(2,1)S(1)} %get-tuple-element.17), channel_id=1, source_target_pairs={{0,2},{1,3},{2,4},{3,5},{4,6},{5,7},{6,0},{7,1},{8,10},{9,11},{10,... | collective-permute-start | bytes 1572872 | tf_op jit(solution)/shard_map/ppermute | solution.py:180
  140.9 16.9 %collective-permute-start.19 = (bf16[8,64,512]{2,1,0:T(8,128)(2,1)S(1)}, bf16[8,64,512]{2,1,0:T(8,128)(2,1)S(1)}, u32[]{:S(2)}, u32[]{:S(2)}) collective-permute-start(bf16[8,64,512]{2,1,0:T(8,128)(2,1)S(1)} %get-tuple-element.18), channel_id=1, source_target_pairs={{0,6},{1,7},{2,0},{3,1},{4,2},{5,3},{6,4},{7,5},{8,14},{9,15},{10,... | collective-permute-start | bytes 1572872 | tf_op jit(solution)/shard_map/ppermute | solution.py:180
  140.9 28.4 %collective-permute-start.7 = (bf16[8,64,512]{2,1,0:T(8,128)(2,1)S(1)}, bf16[8,64,512]{2,1,0:T(8,128)(2,1)S(1)}, u32[]{:S(2)}, u32[]{:S(2)}) collective-permute-start(bf16[8,64,512]{2,1,0:T(8,128)(2,1)S(1)} %get-tuple-element.21.refs_5_), channel_id=1, source_target_pairs={{0,1},{1,0},{2,3},{3,2},{4,5},{5,4},{6,7},{7,6},{8,9},{9,8},{10,11... | collective-permute-start | bytes 1572872 | tf_op jit(solution)/shard_map/ppermute | solution.py:180
  140.9 26.4 %collective-permute-start.1 = (bf16[4,64,512]{2,1,0:T(8,128)(2,1)S(1)}, bf16[4,64,512]{2,1,0:T(8,128)(2,1)S(1)}, u32[]{:S(2)}, u32[]{:S(2)}) collective-permute-start(bf16[4,64,512]{2,1,0:T(8,128)(2,1)S(1)} %get-tuple-element.24.refs_1_), channel_id=1, source_target_pairs={{0,2},{1,3},{2,4},{3,5},{4,6},{5,7},{6,0},{7,1},{8,10},{9,11},{10,... | collective-permute-start | bytes 786440 | tf_op jit(solution)/shard_map/ppermute | solution.py:180
  151.8 15.7 %collective-permute-start.2 = (bf16[4,64,512]{2,1,0:T(8,128)(2,1)S(1)}, bf16[4,64,512]{2,1,0:T(8,128)(2,1)S(1)}, u32[]{:S(2)}, u32[]{:S(2)}) collective-permute-start(bf16[4,64,512]{2,1,0:T(8,128)(2,1)S(1)} %get-tuple-element.25.refs_0_), channel_id=1, source_target_pairs={{0,6},{1,7},{2,0},{3,1},{4,2},{5,3},{6,4},{7,5},{8,14},{9,15},{10,... | collective-permute-start | bytes 786440 | tf_op jit(solution)/shard_map/ppermute | solution.py:180
  157.8 11.5 %collective-permute-start.5 = (bf16[4,64,512]{2,1,0:T(8,128)(2,1)S(1)}, bf16[4,64,512]{2,1,0:T(8,128)(2,1)S(1)}, u32[]{:S(2)}, u32[]{:S(2)}) collective-permute-start(bf16[4,64,512]{2,1,0:T(8,128)(2,1)S(1)} %collective-permute-done.refs_2_), channel_id=1, source_target_pairs={{0,2},{1,3},{2,4},{3,5},{4,6},{5,7},{6,0},{7,1},{8,10},{9,11},{10,... | collective-permute-start | bytes 786440 | tf_op jit(solution)/shard_map/ppermute | solution.py:180
  157.8 11.5 %collective-permute-start.6 = (bf16[4,64,512]{2,1,0:T(8,128)(2,1)S(1)}, bf16[4,64,512]{2,1,0:T(8,128)(2,1)S(1)}, u32[]{:S(2)}, u32[]{:S(2)}) collective-permute-start(bf16[4,64,512]{2,1,0:T(8,128)(2,1)S(1)} %collective-permute-done.3.refs_5_), channel_id=1, source_target_pairs={{0,6},{1,7},{2,0},{3,1},{4,2},{5,3},{6,4},{7,5},{8,14},{9,15},{10,... | collective-permute-start | bytes 786440 | tf_op jit(solution)/shard_map/ppermute | solution.py:180
  167.4 5.2 %collective-permute-start.24 = (f32[4,16,8,64]{3,2,1,0:T(8,128)S(1)}, f32[4,16,8,64]{3,2,1,0:T(8,128)S(1)}, u32[]{:S(2)}, u32[]{:S(2)}) collective-permute-start(f32[4,16,8,64]{3,2,1,0:T(8,128)S(1)} %get-tuple-element.20), channel_id=1, source_target_pairs={{0,1},{1,0},{2,3},{3,2},{4,5},{5,4},{6,7},{7,6},{8,9},{9,8},{10,11... | collective-permute-start | bytes 393224 | tf_op jit(solution)/shard_map/ppermute | solution.py:180
  171.0 1.5 collective-permute-start.8
  172.6 10.6 %collective-permute-start.27 = (f32[16,8,64]{2,1,0:T(8,128)S(1)}, f32[16,8,64]{2,1,0:T(8,128)S(1)}, u32[]{:S(2)}, u32[]{:S(2)}) collective-permute-start(f32[16,8,64]{2,1,0:T(8,128)S(1)} %get-tuple-element.29), channel_id=1, source_target_pairs={{0,4},{1,5},{2,6},{3,7},{4,0},{5,1},{6,2},{7,3},{8,12},{9,13},{10,... | collective-permute-start | bytes 98312 | tf_op jit(solution)/shard_map/ppermute | solution.py:180
  172.9 14.3 %collective-permute-start.26 = (f32[16,8,64]{2,1,0:T(8,128)S(1)}, f32[16,8,64]{2,1,0:T(8,128)S(1)}, u32[]{:S(2)}, u32[]{:S(2)}) collective-permute-start(f32[16,8,64]{2,1,0:T(8,128)S(1)} %get-tuple-element.30), channel_id=1, source_target_pairs={{0,6},{1,7},{2,0},{3,1},{4,2},{5,3},{6,4},{7,5},{8,14},{9,15},{10,... | collective-permute-start | bytes 98312 | tf_op jit(solution)/shard_map/ppermute | solution.py:180
  176.5 10.7 %collective-permute-start.25 = (f32[16,8,64]{2,1,0:T(8,128)S(1)}, f32[16,8,64]{2,1,0:T(8,128)S(1)}, u32[]{:S(2)}, u32[]{:S(2)}) collective-permute-start(f32[16,8,64]{2,1,0:T(8,128)S(1)} %get-tuple-element.28), channel_id=1, source_target_pairs={{0,2},{1,3},{2,4},{3,5},{4,6},{5,7},{6,0},{7,1},{8,10},{9,11},{10,... | collective-permute-start | bytes 98312 | tf_op jit(solution)/shard_map/ppermute | solution.py:180
  177.2 12.2 %collective-permute-start.11 = (f32[8,8,64]{2,1,0:T(8,128)S(1)}, f32[8,8,64]{2,1,0:T(8,128)S(1)}, u32[]{:S(2)}, u32[]{:S(2)}) collective-permute-start(f32[8,8,64]{2,1,0:T(8,128)S(1)} %get-tuple-element.32), channel_id=1, source_target_pairs={{0,4},{1,5},{2,6},{3,7},{4,0},{5,1},{6,2},{7,3},{8,12},{9,13},{10,... | collective-permute-start | bytes 49160 | tf_op jit(solution)/shard_map/ppermute | solution.py:180
  183.1 6.3 %collective-permute-start.10 = (f32[8,8,64]{2,1,0:T(8,128)S(1)}, f32[8,8,64]{2,1,0:T(8,128)S(1)}, u32[]{:S(2)}, u32[]{:S(2)}) collective-permute-start(f32[8,8,64]{2,1,0:T(8,128)S(1)} %get-tuple-element.33), channel_id=1, source_target_pairs={{0,6},{1,7},{2,0},{3,1},{4,2},{5,3},{6,4},{7,5},{8,14},{9,15},{10,... | collective-permute-start | bytes 49160 | tf_op jit(solution)/shard_map/ppermute | solution.py:180
  183.2 6.2 %collective-permute-start.9 = (f32[8,8,64]{2,1,0:T(8,128)S(1)}, f32[8,8,64]{2,1,0:T(8,128)S(1)}, u32[]{:S(2)}, u32[]{:S(2)}) collective-permute-start(f32[8,8,64]{2,1,0:T(8,128)S(1)} %get-tuple-element.31), channel_id=1, source_target_pairs={{0,2},{1,3},{2,4},{3,5},{4,6},{5,7},{6,0},{7,1},{8,10},{9,11},{10,... | collective-permute-start | bytes 49160 | tf_op jit(solution)/shard_map/ppermute | solution.py:180
  187.3 4.0 %collective-permute-start.29 = (f32[8,8,64]{2,1,0:T(8,128)S(1)}, f32[8,8,64]{2,1,0:T(8,128)S(1)}, u32[]{:S(2)}, u32[]{:S(2)}) collective-permute-start(f32[8,8,64]{2,1,0:T(8,128)S(1)} %get-tuple-element.35), channel_id=1, source_target_pairs={{0,248},{1,249},{2,250},{3,251},{4,252},{5,253},{6,254},{7,255},{8... | collective-permute-start | bytes 49160 | tf_op jit(solution)/shard_map/ppermute | solution.py:180
  187.4 8.2 %collective-permute-start.28 = (f32[8,8,64]{2,1,0:T(8,128)S(1)}, f32[8,8,64]{2,1,0:T(8,128)S(1)}, u32[]{:S(2)}, u32[]{:S(2)}) collective-permute-start(f32[8,8,64]{2,1,0:T(8,128)S(1)} %get-tuple-element.34), channel_id=1, source_target_pairs={{0,8},{1,9},{2,10},{3,11},{4,12},{5,13},{6,14},{7,15},{8,16},{9,17... | collective-permute-start | bytes 49160 | tf_op jit(solution)/shard_map/ppermute | solution.py:180
  (2 other events, 2.8 us)

commit v2 on v1

--- a/solution.py
+++ b/solution.py
@@ -31,11 +31,7 @@
 
 
 def turn(group, q, owners):
-    if group == 1:
-        return -1 if q == owners - 1 else 1
-    if group == 2:
-        return 1 if q == 0 else -1
-    return 1
+    return 1 if group == 0 or q < owners // 2 else -1
 
 
 def where_am_i():
@@ -44,11 +40,7 @@
 
 
 def heading(group, owner, owners):
-    if group == 1:
-        return jnp.where(owner == owners - 1, -1, 1)
-    if group == 2:
-        return jnp.where(owner == 0, 1, -1)
-    return jnp.int32(1)
+    return jnp.int32(1) if group == 0 else jnp.where(owner < owners // 2, 1, -1)
 
 
 def restrict_kernel(quarters, rows, spheres_ref, slab_ref, mine_ref, give_ref):

time: 196 us -> 182 us (0.929)
  the two profiles are of different devices: /device:TPU:96 before, /device:TPU:64 now
where the time goes in v2:
time: 182 us
  starting transfers between devices  85.5 us (47%)
  waiting for transfers between devices  80.6 us (44%)
  Pallas kernels  12.1 us (7%)
  local copies, waits for them, and re-layouts  3.15 us (2%)
    ppermute x30, starting transfers between devices, send(): return lax.ppermute(x, AXES, moves(owners, quarters, target))  85.5 us
    ppermute x30, waiting for transfers between devices, send(): return lax.ppermute(x, AXES, moves(owners, quarters, target))  80.6 us
    pallas_call x7, Pallas kernels, call(): pl.pallas_call(body, in_specs=in_specs or [VMEM] * len(operands), out_spe...  12.1 us
  transfers between devices with their start and end apart: 30, of which 12 were waited for; matrix products, arithmetic and copies ran while one was open for 0% of the time, Pallas kernels for 6%

profile of v2, /device:TPU:64, one launch (start us, length us, event | category | flops | bytes accessed | tf_op | source)
XLA Modules:
  0.0 182.2 jit_solution(9658059496077908363)
XLA Ops:
  0.0 2.2 %copy-done = bf16[1,512,4096]{2,1,0:T(8,128)(2,1)S(1)} copy-done((bf16[1,512,4096]{2,1,0:T(8,128)(2,1)S(1)}, bf16[1,512,4096]{2,1,0:T(8,128)(2,1)}, u32[]{:S(2)}) %copy-start) | copy-done | bytes 4194328
  2.8 2.0 %shard_map.46 = (bf16[512,2048]{1,0:T(8,128)(2,1)S(1)}, bf16[512,2048]{1,0:T(8,128)(2,1)S(1)}) custom-call(s32[32]{0:T(128)S(1)} %copy-done.1, bf16[512,4096]{1,0:T(8,128)(2,1)S(1)} %bitcast.29), custom_call_target="tpu_custom_call" | custom-call | tf_op jit(solution)/shard_map/pallas_call | solution.py:179
  5.1 6.6 %collective-permute-start.12 = (bf16[8,64,512]{2,1,0:T(8,128)(2,1)S(1)}, bf16[8,64,512]{2,1,0:T(8,128)(2,1)S(1)}, u32[]{:S(2)}, u32[]{:S(2)}) collective-permute-start(bf16[8,64,512]{2,1,0:T(8,128)(2,1)S(1)} %get-tuple-element.27), channel_id=1, source_target_pairs={{0,248},{1,249},{2,250},{3,251},{4,252},{5,253},{6,254},{7,255},{8... | collective-permute-start | bytes 1572872 | tf_op jit(solution)/shard_map/ppermute | solution.py:172
  11.7 5.0 %collective-permute-start.15 = (bf16[8,64,512]{2,1,0:T(8,128)(2,1)S(1)}, bf16[8,64,512]{2,1,0:T(8,128)(2,1)S(1)}, u32[]{:S(2)}, u32[]{:S(2)}) collective-permute-start(bf16[8,64,512]{2,1,0:T(8,128)(2,1)S(1)} %get-tuple-element.26), channel_id=1, source_target_pairs={{0,8},{1,9},{2,10},{3,11},{4,12},{5,13},{6,14},{7,15},{8,16},{9,17... | collective-permute-start | bytes 1572872 | tf_op jit(solution)/shard_map/ppermute | solution.py:172
  17.8 17.4 %collective-permute-done.12.refs_0_ = bf16[8,64,512]{2,1,0:T(8,128)(2,1)S(1)} collective-permute-done((bf16[8,64,512]{2,1,0:T(8,128)(2,1)S(1)}, bf16[8,64,512]{2,1,0:T(8,128)(2,1)S(1)}, u32[]{:S(2)}, u32[]{:S(2)}) %collective-permute-start.12) | collective-permute-done | bytes 524320 | tf_op jit(solution)/shard_map/ppermute | solution.py:172
  35.2 6.7 %collective-permute-start.20 = (bf16[8,64,512]{2,1,0:T(8,128)(2,1)S(1)}, bf16[8,64,512]{2,1,0:T(8,128)(2,1)S(1)}, u32[]{:S(2)}, u32[]{:S(2)}) collective-permute-start(bf16[8,64,512]{2,1,0:T(8,128)(2,1)S(1)} %get-tuple-element.23), channel_id=1, source_target_pairs={{0,248},{1,249},{2,250},{3,251},{4,252},{5,253},{6,254},{7,255},{8... | collective-permute-start | bytes 1572872 | tf_op jit(solution)/shard_map/ppermute | solution.py:172
  41.9 2.0 %collective-permute-done.13.refs_1_.a1 = bf16[8,64,512]{2,1,0:T(8,128)(2,1)S(1)} collective-permute-done((bf16[8,64,512]{2,1,0:T(8,128)(2,1)S(1)}, bf16[8,64,512]{2,1,0:T(8,128)(2,1)S(1)}, u32[]{:S(2)}, u32[]{:S(2)}) %collective-permute-start.13) | collective-permute-done | bytes 524320 | tf_op jit(solution)/shard_map/ppermute | solution.py:172
  43.9 2.5 %collective-permute-done.15.refs_0_ = bf16[8,64,512]{2,1,0:T(8,128)(2,1)S(1)} collective-permute-done((bf16[8,64,512]{2,1,0:T(8,128)(2,1)S(1)}, bf16[8,64,512]{2,1,0:T(8,128)(2,1)S(1)}, u32[]{:S(2)}, u32[]{:S(2)}) %collective-permute-start.15) | collective-permute-done | bytes 524320 | tf_op jit(solution)/shard_map/ppermute | solution.py:172
  46.4 27.8 %collective-permute-start.14 = (bf16[8,64,512]{2,1,0:T(8,128)(2,1)S(1)}, bf16[8,64,512]{2,1,0:T(8,128)(2,1)S(1)}, u32[]{:S(2)}, u32[]{:S(2)}) collective-permute-start(bf16[8,64,512]{2,1,0:T(8,128)(2,1)S(1)} %collective-permute-done.12.refs_0_), channel_id=1, source_target_pairs={{0,6},{1,7},{2,0},{3,1},{4,2},{5,3},{6,4},{7,5},{8,14},{9,15},{10,... | collective-permute-start | bytes 1572872 | tf_op jit(solution)/shard_map/ppermute | solution.py:172
  74.3 11.0 %collective-permute-done.20.refs_6_ = bf16[8,64,512]{2,1,0:T(8,128)(2,1)S(1)} collective-permute-done((bf16[8,64,512]{2,1,0:T(8,128)(2,1)S(1)}, bf16[8,64,512]{2,1,0:T(8,128)(2,1)S(1)}, u32[]{:S(2)}, u32[]{:S(2)}) %collective-permute-start.20) | collective-permute-done | bytes 524320 | tf_op jit(solution)/shard_map/ppermute | solution.py:172
  85.3 2.9 %collective-permute-start.3 = (bf16[4,64,512]{2,1,0:T(8,128)(2,1)S(1)}, bf16[4,64,512]{2,1,0:T(8,128)(2,1)S(1)}, u32[]{:S(2)}, u32[]{:S(2)}) collective-permute-start(bf16[4,64,512]{2,1,0:T(8,128)(2,1)S(1)} %get-tuple-element.24.refs_1_), channel_id=1, source_target_pairs={{0,6},{1,7},{2,0},{3,1},{4,2},{5,3},{6,4},{7,5},{8,14},{9,15},{10,... | collective-permute-start | bytes 786440 | tf_op jit(solution)/shard_map/ppermute | solution.py:172
  88.2 6.0 %collective-permute-done.17.refs_2_.b2 = bf16[8,64,512]{2,1,0:T(8,128)(2,1)S(1)} collective-permute-done((bf16[8,64,512]{2,1,0:T(8,128)(2,1)S(1)}, bf16[8,64,512]{2,1,0:T(8,128)(2,1)S(1)}, u32[]{:S(2)}, u32[]{:S(2)}) %collective-permute-start.17) | collective-permute-done | bytes 524320 | tf_op jit(solution)/shard_map/ppermute | solution.py:172
  94.3 1.3 collective-permute-start.18
  95.6 5.2 %collective-permute-done.3.refs_5_ = bf16[4,64,512]{2,1,0:T(8,128)(2,1)S(1)} collective-permute-done((bf16[4,64,512]{2,1,0:T(8,128)(2,1)S(1)}, bf16[4,64,512]{2,1,0:T(8,128)(2,1)S(1)}, u32[]{:S(2)}, u32[]{:S(2)}) %collective-permute-start.3) | collective-permute-done | bytes 262176 | tf_op jit(solution)/shard_map/ppermute | solution.py:172
  101.3 4.0 %collective-permute-start.1 = (bf16[4,64,512]{2,1,0:T(8,128)(2,1)S(1)}, bf16[4,64,512]{2,1,0:T(8,128)(2,1)S(1)}, u32[]{:S(2)}, u32[]{:S(2)}) collective-permute-start(bf16[4,64,512]{2,1,0:T(8,128)(2,1)S(1)} %get-tuple-element.24.refs_1_), channel_id=1, source_target_pairs={{0,2},{1,3},{2,4},{3,5},{4,6},{5,7},{6,0},{7,1},{8,10},{9,11},{10,... | collective-permute-start | bytes 786440 | tf_op jit(solution)/shard_map/ppermute | solution.py:172
  105.3 20.7 %collective-permute-done.18.refs_2_ = bf16[8,64,512]{2,1,0:T(8,128)(2,1)S(1)} collective-permute-done((bf16[8,64,512]{2,1,0:T(8,128)(2,1)S(1)}, bf16[8,64,512]{2,1,0:T(8,128)(2,1)S(1)}, u32[]{:S(2)}, u32[]{:S(2)}) %collective-permute-start.18) | collective-permute-done | bytes 524320 | tf_op jit(solution)/shard_map/ppermute | solution.py:172
  126.0 3.8 %collective-permute-start.2 = (bf16[4,64,512]{2,1,0:T(8,128)(2,1)S(1)}, bf16[4,64,512]{2,1,0:T(8,128)(2,1)S(1)}, u32[]{:S(2)}, u32[]{:S(2)}) collective-permute-start(bf16[4,64,512]{2,1,0:T(8,128)(2,1)S(1)} %get-tuple-element.25.refs_0_), channel_id=1, source_target_pairs={{0,6},{1,7},{2,0},{3,1},{4,2},{5,3},{6,4},{7,5},{8,14},{9,15},{10,... | collective-permute-start | bytes 786440 | tf_op jit(solution)/shard_map/ppermute | solution.py:172
  130.1 2.5 %collective-permute-start.6 = (bf16[4,64,512]{2,1,0:T(8,128)(2,1)S(1)}, bf16[4,64,512]{2,1,0:T(8,128)(2,1)S(1)}, u32[]{:S(2)}, u32[]{:S(2)}) collective-permute-start(bf16[4,64,512]{2,1,0:T(8,128)(2,1)S(1)} %collective-permute-done.3.refs_5_), channel_id=1, source_target_pairs={{0,6},{1,7},{2,0},{3,1},{4,2},{5,3},{6,4},{7,5},{8,14},{9,15},{10,... | collective-permute-start | bytes 786440 | tf_op jit(solution)/shard_map/ppermute | solution.py:172
  132.7 1.8 shard_map.49.refs_0_
  134.5 1.8 %shard_map.50.refs_1_ = f32[2,512,512]{2,1,0:T(8,128)S(1)} custom-call(bf16[8,64,512]{2,1,0:T(8,128)(2,1)S(1)} %collective-permute-done.15.refs_0_, bf16[8,64,512]{2,1,0:T(8,128)(2,1)S(1)} %collective-permute-done.16.refs_1_.a2, bf16[8,64,512]{2,1,0:T(8,128)(2,1)S(1)} %collective-permute-done.17.refs_2_.b2, ...), custom_call_target="tpu_custom_call" | custom-call | tf_op jit(solution)/shard_map/pallas_call | solution.py:179
  136.3 2.9 %shard_map.52 = (f32[4,16,8,64]{3,2,1,0:T(8,128)S(1)}, f32[4,16,8,64]{3,2,1,0:T(8,128)S(1)}) custom-call(f32[2,512,512]{2,1,0:T(8,128)S(1)} %shard_map.49.refs_0_, f32[2,512,512]{2,1,0:T(8,128)S(1)} %shard_map.50.refs_1_, bf16[8,64,512]{2,1,0:T(8,128)(2,1)S(1)} %collective-permute-done.18.refs_2_, bf16[8,64,512]{2,1,0:T(8,128)(2,1)S(1)} %collective-permute-done.19.refs_3_, ...), custom_call_target="tpu_custom_call" | custom-call | tf_op jit(solution)/shard_map/pallas_call | solution.py:179
  139.4 2.6 %collective-permute-done.2.refs_4_ = bf16[4,64,512]{2,1,0:T(8,128)(2,1)S(1)} collective-permute-done((bf16[4,64,512]{2,1,0:T(8,128)(2,1)S(1)}, bf16[4,64,512]{2,1,0:T(8,128)(2,1)S(1)}, u32[]{:S(2)}, u32[]{:S(2)}) %collective-permute-start.2) | collective-permute-done | bytes 262176 | tf_op jit(solution)/shard_map/ppermute | solution.py:172
  142.0 1.8 shard_map.47.refs_0_
  143.8 3.7 %collective-permute-done.6.refs_2_ = bf16[4,64,512]{2,1,0:T(8,128)(2,1)S(1)} collective-permute-done((bf16[4,64,512]{2,1,0:T(8,128)(2,1)S(1)}, bf16[4,64,512]{2,1,0:T(8,128)(2,1)S(1)}, u32[]{:S(2)}, u32[]{:S(2)}) %collective-permute-start.6) | collective-permute-done | bytes 262176 | tf_op jit(solution)/shard_map/ppermute | solution.py:172
  147.6 1.6 shard_map.48
  150.7 3.9 %collective-permute-start.27 = (f32[16,8,64]{2,1,0:T(8,128)S(1)}, f32[16,8,64]{2,1,0:T(8,128)S(1)}, u32[]{:S(2)}, u32[]{:S(2)}) collective-permute-start(f32[16,8,64]{2,1,0:T(8,128)S(1)} %get-tuple-element.29), channel_id=1, source_target_pairs={{0,4},{1,5},{2,6},{3,7},{4,0},{5,1},{6,2},{7,3},{8,12},{9,13},{10,... | collective-permute-start | bytes 98312 | tf_op jit(solution)/shard_map/ppermute | solution.py:172
  155.0 3.8 %collective-permute-start.25 = (f32[16,8,64]{2,1,0:T(8,128)S(1)}, f32[16,8,64]{2,1,0:T(8,128)S(1)}, u32[]{:S(2)}, u32[]{:S(2)}) collective-permute-start(f32[16,8,64]{2,1,0:T(8,128)S(1)} %get-tuple-element.28), channel_id=1, source_target_pairs={{0,2},{1,3},{2,4},{3,5},{4,6},{5,7},{6,0},{7,1},{8,10},{9,11},{10,... | collective-permute-start | bytes 98312 | tf_op jit(solution)/shard_map/ppermute | solution.py:172
  158.8 2.4 %collective-permute-start.11 = (f32[8,8,64]{2,1,0:T(8,128)S(1)}, f32[8,8,64]{2,1,0:T(8,128)S(1)}, u32[]{:S(2)}, u32[]{:S(2)}) collective-permute-start(f32[8,8,64]{2,1,0:T(8,128)S(1)} %get-tuple-element.32), channel_id=1, source_target_pairs={{0,4},{1,5},{2,6},{3,7},{4,0},{5,1},{6,2},{7,3},{8,12},{9,13},{10,... | collective-permute-start | bytes 49160 | tf_op jit(solution)/shard_map/ppermute | solution.py:172
  161.3 4.0 %collective-permute-start.9 = (f32[8,8,64]{2,1,0:T(8,128)S(1)}, f32[8,8,64]{2,1,0:T(8,128)S(1)}, u32[]{:S(2)}, u32[]{:S(2)}) collective-permute-start(f32[8,8,64]{2,1,0:T(8,128)S(1)} %get-tuple-element.31), channel_id=1, source_target_pairs={{0,2},{1,3},{2,4},{3,5},{4,6},{5,7},{6,0},{7,1},{8,10},{9,11},{10,... | collective-permute-start | bytes 49160 | tf_op jit(solution)/shard_map/ppermute | solution.py:172
  165.3 8.1 %collective-permute-start.29 = (f32[8,8,64]{2,1,0:T(8,128)S(1)}, f32[8,8,64]{2,1,0:T(8,128)S(1)}, u32[]{:S(2)}, u32[]{:S(2)}) collective-permute-start(f32[8,8,64]{2,1,0:T(8,128)S(1)} %get-tuple-element.35), channel_id=1, source_target_pairs={{0,248},{1,249},{2,250},{3,251},{4,252},{5,253},{6,254},{7,255},{8... | collective-permute-start | bytes 49160 | tf_op jit(solution)/shard_map/ppermute | solution.py:172
  173.5 1.6 collective-permute-done.29
  175.1 6.5 %collective-permute-done.28 = f32[8,8,64]{2,1,0:T(8,128)S(1)} collective-permute-done((f32[8,8,64]{2,1,0:T(8,128)S(1)}, f32[8,8,64]{2,1,0:T(8,128)S(1)}, u32[]{:S(2)}, u32[]{:S(2)}) %collective-permute-start.28) | collective-permute-done | bytes 16416 | tf_op jit(solution)/shard_map/ppermute | solution.py:172
  (54 shorter events, 5.6 us)
Async XLA Ops:
  0.0 2.2 %copy-start = (bf16[1,512,4096]{2,1,0:T(8,128)(2,1)S(1)}, bf16[1,512,4096]{2,1,0:T(8,128)(2,1)}, u32[]{:S(2)}) copy-start(bf16[1,512,4096]{2,1,0:T(8,128)(2,1)} %param.6) | copy-start | bytes 12582916
  4.9 12.8 %copy-start.2 = (bf16[24,64,512]{2,1,0:T(8,128)(2,1)S(1)}, bf16[24,64,512]{2,1,0:T(8,128)(2,1)}, u32[]{:S(2)}) copy-start(bf16[24,64,512]{2,1,0:T(8,128)(2,1)} %param.4) | copy-start | bytes 4718596
  4.9 125.2 %collective-permute-start.4 = (bf16[512,2048]{1,0:T(8,128)(2,1)S(1)}, bf16[512,2048]{1,0:T(8,128)(2,1)S(1)}, u32[]{:S(2)}, u32[]{:S(2)}) collective-permute-start(bf16[512,2048]{1,0:T(8,128)(2,1)S(1)} %get-tuple-element.14), channel_id=1, source_target_pairs={{0,1},{1,0},{2,3},{3,2},{4,5},{5,4},{6,7},{7,6},{8,9},{9,8},{10,11... | collective-permute-start | bytes 6291464 | tf_op jit(solution)/shard_map/ppermute | solution.py:172
  5.1 30.1 %collective-permute-start.12 = (bf16[8,64,512]{2,1,0:T(8,128)(2,1)S(1)}, bf16[8,64,512]{2,1,0:T(8,128)(2,1)S(1)}, u32[]{:S(2)}, u32[]{:S(2)}) collective-permute-start(bf16[8,64,512]{2,1,0:T(8,128)(2,1)S(1)} %get-tuple-element.27), channel_id=1, source_target_pairs={{0,248},{1,249},{2,250},{3,251},{4,252},{5,253},{6,254},{7,255},{8... | collective-permute-start | bytes 1572872 | tf_op jit(solution)/shard_map/ppermute | solution.py:172
  11.7 32.2 %collective-permute-start.13 = (bf16[8,64,512]{2,1,0:T(8,128)(2,1)S(1)}, bf16[8,64,512]{2,1,0:T(8,128)(2,1)S(1)}, u32[]{:S(2)}, u32[]{:S(2)}) collective-permute-start(bf16[8,64,512]{2,1,0:T(8,128)(2,1)S(1)} %get-tuple-element.27), channel_id=1, source_target_pairs={{0,254},{1,255},{2,248},{3,249},{4,250},{5,251},{6,252},{7,253},{8... | collective-permute-start | bytes 1572872 | tf_op jit(solution)/shard_map/ppermute | solution.py:172
  11.7 34.7 %collective-permute-start.15 = (bf16[8,64,512]{2,1,0:T(8,128)(2,1)S(1)}, bf16[8,64,512]{2,1,0:T(8,128)(2,1)S(1)}, u32[]{:S(2)}, u32[]{:S(2)}) collective-permute-start(bf16[8,64,512]{2,1,0:T(8,128)(2,1)S(1)} %get-tuple-element.26), channel_id=1, source_target_pairs={{0,8},{1,9},{2,10},{3,11},{4,12},{5,13},{6,14},{7,15},{8,16},{9,17... | collective-permute-start | bytes 1572872 | tf_op jit(solution)/shard_map/ppermute | solution.py:172
  16.8 57.4 %collective-permute-start.16 = (bf16[8,64,512]{2,1,0:T(8,128)(2,1)S(1)}, bf16[8,64,512]{2,1,0:T(8,128)(2,1)S(1)}, u32[]{:S(2)}, u32[]{:S(2)}) collective-permute-start(bf16[8,64,512]{2,1,0:T(8,128)(2,1)S(1)} %get-tuple-element.26), channel_id=1, source_target_pairs={{0,10},{1,11},{2,12},{3,13},{4,14},{5,15},{6,8},{7,9},{8,18},{9,19... | collective-permute-start | bytes 1572872 | tf_op jit(solution)/shard_map/ppermute | solution.py:172
  35.2 50.1 %collective-permute-start.20 = (bf16[8,64,512]{2,1,0:T(8,128)(2,1)S(1)}, bf16[8,64,512]{2,1,0:T(8,128)(2,1)S(1)}, u32[]{:S(2)}, u32[]{:S(2)}) collective-permute-start(bf16[8,64,512]{2,1,0:T(8,128)(2,1)S(1)} %get-tuple-element.23), channel_id=1, source_target_pairs={{0,248},{1,249},{2,250},{3,251},{4,252},{5,253},{6,254},{7,255},{8... | collective-permute-start | bytes 1572872 | tf_op jit(solution)/shard_map/ppermute | solution.py:172
  43.9 41.4 %collective-permute-start.22 = (bf16[8,64,512]{2,1,0:T(8,128)(2,1)S(1)}, bf16[8,64,512]{2,1,0:T(8,128)(2,1)S(1)}, u32[]{:S(2)}, u32[]{:S(2)}) collective-permute-start(bf16[8,64,512]{2,1,0:T(8,128)(2,1)S(1)} %get-tuple-element.22), channel_id=1, source_target_pairs={{0,8},{1,9},{2,10},{3,11},{4,12},{5,13},{6,14},{7,15},{8,16},{9,17... | collective-permute-start | bytes 1572872 | tf_op jit(solution)/shard_map/ppermute | solution.py:172
  46.4 41.8 %collective-permute-start.14 = (bf16[8,64,512]{2,1,0:T(8,128)(2,1)S(1)}, bf16[8,64,512]{2,1,0:T(8,128)(2,1)S(1)}, u32[]{:S(2)}, u32[]{:S(2)}) collective-permute-start(bf16[8,64,512]{2,1,0:T(8,128)(2,1)S(1)} %collective-permute-done.12.refs_0_), channel_id=1, source_target_pairs={{0,6},{1,7},{2,0},{3,1},{4,2},{5,3},{6,4},{7,5},{8,14},{9,15},{10,... | collective-permute-start | bytes 1572872 | tf_op jit(solution)/shard_map/ppermute | solution.py:172
  74.2 20.0 %collective-permute-start.17 = (bf16[8,64,512]{2,1,0:T(8,128)(2,1)S(1)}, bf16[8,64,512]{2,1,0:T(8,128)(2,1)S(1)}, u32[]{:S(2)}, u32[]{:S(2)}) collective-permute-start(bf16[8,64,512]{2,1,0:T(8,128)(2,1)S(1)} %collective-permute-done.15.refs_0_), channel_id=1, source_target_pairs={{0,6},{1,7},{2,0},{3,1},{4,2},{5,3},{6,4},{7,5},{8,14},{9,15},{10,... | collective-permute-start | bytes 1572872 | tf_op jit(solution)/shard_map/ppermute | solution.py:172
  85.3 9.0 %collective-permute-start = (bf16[4,64,512]{2,1,0:T(8,128)(2,1)S(1)}, bf16[4,64,512]{2,1,0:T(8,128)(2,1)S(1)}, u32[]{:S(2)}, u32[]{:S(2)}) collective-permute-start(bf16[4,64,512]{2,1,0:T(8,128)(2,1)S(1)} %get-tuple-element.25.refs_0_), channel_id=1, source_target_pairs={{0,2},{1,3},{2,4},{3,5},{4,6},{5,7},{6,0},{7,1},{8,10},{9,11},{10,... | collective-permute-start | bytes 786440 | tf_op jit(solution)/shard_map/ppermute | solution.py:172
  85.3 15.6 %collective-permute-start.3 = (bf16[4,64,512]{2,1,0:T(8,128)(2,1)S(1)}, bf16[4,64,512]{2,1,0:T(8,128)(2,1)S(1)}, u32[]{:S(2)}, u32[]{:S(2)}) collective-permute-start(bf16[4,64,512]{2,1,0:T(8,128)(2,1)S(1)} %get-tuple-element.24.refs_1_), channel_id=1, source_target_pairs={{0,6},{1,7},{2,0},{3,1},{4,2},{5,3},{6,4},{7,5},{8,14},{9,15},{10,... | collective-permute-start | bytes 786440 | tf_op jit(solution)/shard_map/ppermute | solution.py:172
  88.2 13.0 %collective-permute-start.21 = (bf16[8,64,512]{2,1,0:T(8,128)(2,1)S(1)}, bf16[8,64,512]{2,1,0:T(8,128)(2,1)S(1)}, u32[]{:S(2)}, u32[]{:S(2)}) collective-permute-start(bf16[8,64,512]{2,1,0:T(8,128)(2,1)S(1)} %collective-permute-done.20.refs_6_), channel_id=1, source_target_pairs={{0,1},{1,0},{2,3},{3,2},{4,5},{5,4},{6,7},{7,6},{8,9},{9,8},{10,11... | collective-permute-start | bytes 1572872 | tf_op jit(solution)/shard_map/ppermute | solution.py:172
  94.2 7.1 %collective-permute-start.23 = (bf16[8,64,512]{2,1,0:T(8,128)(2,1)S(1)}, bf16[8,64,512]{2,1,0:T(8,128)(2,1)S(1)}, u32[]{:S(2)}, u32[]{:S(2)}) collective-permute-start(bf16[8,64,512]{2,1,0:T(8,128)(2,1)S(1)} %collective-permute-done.22.refs_8_), channel_id=1, source_target_pairs={{0,1},{1,0},{2,3},{3,2},{4,5},{5,4},{6,7},{7,6},{8,9},{9,8},{10,11... | collective-permute-start | bytes 1572872 | tf_op jit(solution)/shard_map/ppermute | solution.py:172
  94.3 31.7 %collective-permute-start.18 = (bf16[8,64,512]{2,1,0:T(8,128)(2,1)S(1)}, bf16[8,64,512]{2,1,0:T(8,128)(2,1)S(1)}, u32[]{:S(2)}, u32[]{:S(2)}) collective-permute-start(bf16[8,64,512]{2,1,0:T(8,128)(2,1)S(1)} %get-tuple-element.17), channel_id=1, source_target_pairs={{0,2},{1,3},{2,4},{3,5},{4,6},{5,7},{6,0},{7,1},{8,10},{9,11},{10,... | collective-permute-start | bytes 1572872 | tf_op jit(solution)/shard_map/ppermute | solution.py:172
  100.9 28.9 %collective-permute-start.19 = (bf16[8,64,512]{2,1,0:T(8,128)(2,1)S(1)}, bf16[8,64,512]{2,1,0:T(8,128)(2,1)S(1)}, u32[]{:S(2)}, u32[]{:S(2)}) collective-permute-start(bf16[8,64,512]{2,1,0:T(8,128)(2,1)S(1)} %get-tuple-element.18), channel_id=1, source_target_pairs={{0,6},{1,7},{2,0},{3,1},{4,2},{5,3},{6,4},{7,5},{8,14},{9,15},{10,... | collective-permute-start | bytes 1572872 | tf_op jit(solution)/shard_map/ppermute | solution.py:172
  101.3 46.3 %collective-permute-start.7 = (bf16[8,64,512]{2,1,0:T(8,128)(2,1)S(1)}, bf16[8,64,512]{2,1,0:T(8,128)(2,1)S(1)}, u32[]{:S(2)}, u32[]{:S(2)}) collective-permute-start(bf16[8,64,512]{2,1,0:T(8,128)(2,1)S(1)} %get-tuple-element.21.refs_5_), channel_id=1, source_target_pairs={{0,1},{1,0},{2,3},{3,2},{4,5},{5,4},{6,7},{7,6},{8,9},{9,8},{10,11... | collective-permute-start | bytes 1572872 | tf_op jit(solution)/shard_map/ppermute | solution.py:172
  101.3 38.0 %collective-permute-start.1 = (bf16[4,64,512]{2,1,0:T(8,128)(2,1)S(1)}, bf16[4,64,512]{2,1,0:T(8,128)(2,1)S(1)}, u32[]{:S(2)}, u32[]{:S(2)}) collective-permute-start(bf16[4,64,512]{2,1,0:T(8,128)(2,1)S(1)} %get-tuple-element.24.refs_1_), channel_id=1, source_target_pairs={{0,2},{1,3},{2,4},{3,5},{4,6},{5,7},{6,0},{7,1},{8,10},{9,11},{10,... | collective-permute-start | bytes 786440 | tf_op jit(solution)/shard_map/ppermute | solution.py:172
  126.0 16.0 %collective-permute-start.2 = (bf16[4,64,512]{2,1,0:T(8,128)(2,1)S(1)}, bf16[4,64,512]{2,1,0:T(8,128)(2,1)S(1)}, u32[]{:S(2)}, u32[]{:S(2)}) collective-permute-start(bf16[4,64,512]{2,1,0:T(8,128)(2,1)S(1)} %get-tuple-element.25.refs_0_), channel_id=1, source_target_pairs={{0,6},{1,7},{2,0},{3,1},{4,2},{5,3},{6,4},{7,5},{8,14},{9,15},{10,... | collective-permute-start | bytes 786440 | tf_op jit(solution)/shard_map/ppermute | solution.py:172
  129.7 14.1 %collective-permute-start.5 = (bf16[4,64,512]{2,1,0:T(8,128)(2,1)S(1)}, bf16[4,64,512]{2,1,0:T(8,128)(2,1)S(1)}, u32[]{:S(2)}, u32[]{:S(2)}) collective-permute-start(bf16[4,64,512]{2,1,0:T(8,128)(2,1)S(1)} %collective-permute-done.refs_2_), channel_id=1, source_target_pairs={{0,2},{1,3},{2,4},{3,5},{4,6},{5,7},{6,0},{7,1},{8,10},{9,11},{10,... | collective-permute-start | bytes 786440 | tf_op jit(solution)/shard_map/ppermute | solution.py:172
  130.1 17.5 %collective-permute-start.6 = (bf16[4,64,512]{2,1,0:T(8,128)(2,1)S(1)}, bf16[4,64,512]{2,1,0:T(8,128)(2,1)S(1)}, u32[]{:S(2)}, u32[]{:S(2)}) collective-permute-start(bf16[4,64,512]{2,1,0:T(8,128)(2,1)S(1)} %collective-permute-done.3.refs_5_), channel_id=1, source_target_pairs={{0,6},{1,7},{2,0},{3,1},{4,2},{5,3},{6,4},{7,5},{8,14},{9,15},{10,... | collective-permute-start | bytes 786440 | tf_op jit(solution)/shard_map/ppermute | solution.py:172
  139.3 11.3 %collective-permute-start.24 = (f32[4,16,8,64]{3,2,1,0:T(8,128)S(1)}, f32[4,16,8,64]{3,2,1,0:T(8,128)S(1)}, u32[]{:S(2)}, u32[]{:S(2)}) collective-permute-start(f32[4,16,8,64]{3,2,1,0:T(8,128)S(1)} %get-tuple-element.20), channel_id=1, source_target_pairs={{0,1},{1,0},{2,3},{3,2},{4,5},{5,4},{6,7},{7,6},{8,9},{9,8},{10,11... | collective-permute-start | bytes 393224 | tf_op jit(solution)/shard_map/ppermute | solution.py:172
  149.2 1.4 collective-permute-start.8
  150.7 10.6 %collective-permute-start.27 = (f32[16,8,64]{2,1,0:T(8,128)S(1)}, f32[16,8,64]{2,1,0:T(8,128)S(1)}, u32[]{:S(2)}, u32[]{:S(2)}) collective-permute-start(f32[16,8,64]{2,1,0:T(8,128)S(1)} %get-tuple-element.29), channel_id=1, source_target_pairs={{0,4},{1,5},{2,6},{3,7},{4,0},{5,1},{6,2},{7,3},{8,12},{9,13},{10,... | collective-permute-start | bytes 98312 | tf_op jit(solution)/shard_map/ppermute | solution.py:172
  154.6 10.7 %collective-permute-start.26 = (f32[16,8,64]{2,1,0:T(8,128)S(1)}, f32[16,8,64]{2,1,0:T(8,128)S(1)}, u32[]{:S(2)}, u32[]{:S(2)}) collective-permute-start(f32[16,8,64]{2,1,0:T(8,128)S(1)} %get-tuple-element.30), channel_id=1, source_target_pairs={{0,6},{1,7},{2,0},{3,1},{4,2},{5,3},{6,4},{7,5},{8,14},{9,15},{10,... | collective-permute-start | bytes 98312 | tf_op jit(solution)/shard_map/ppermute | solution.py:172
  155.0 10.3 %collective-permute-start.25 = (f32[16,8,64]{2,1,0:T(8,128)S(1)}, f32[16,8,64]{2,1,0:T(8,128)S(1)}, u32[]{:S(2)}, u32[]{:S(2)}) collective-permute-start(f32[16,8,64]{2,1,0:T(8,128)S(1)} %get-tuple-element.28), channel_id=1, source_target_pairs={{0,2},{1,3},{2,4},{3,5},{4,6},{5,7},{6,0},{7,1},{8,10},{9,11},{10,... | collective-permute-start | bytes 98312 | tf_op jit(solution)/shard_map/ppermute | solution.py:172
  158.8 14.7 %collective-permute-start.11 = (f32[8,8,64]{2,1,0:T(8,128)S(1)}, f32[8,8,64]{2,1,0:T(8,128)S(1)}, u32[]{:S(2)}, u32[]{:S(2)}) collective-permute-start(f32[8,8,64]{2,1,0:T(8,128)S(1)} %get-tuple-element.32), channel_id=1, source_target_pairs={{0,4},{1,5},{2,6},{3,7},{4,0},{5,1},{6,2},{7,3},{8,12},{9,13},{10,... | collective-permute-start | bytes 49160 | tf_op jit(solution)/shard_map/ppermute | solution.py:172
  161.2 12.3 %collective-permute-start.10 = (f32[8,8,64]{2,1,0:T(8,128)S(1)}, f32[8,8,64]{2,1,0:T(8,128)S(1)}, u32[]{:S(2)}, u32[]{:S(2)}) collective-permute-start(f32[8,8,64]{2,1,0:T(8,128)S(1)} %get-tuple-element.33), channel_id=1, source_target_pairs={{0,6},{1,7},{2,0},{3,1},{4,2},{5,3},{6,4},{7,5},{8,14},{9,15},{10,... | collective-permute-start | bytes 49160 | tf_op jit(solution)/shard_map/ppermute | solution.py:172
  161.3 12.2 %collective-permute-start.9 = (f32[8,8,64]{2,1,0:T(8,128)S(1)}, f32[8,8,64]{2,1,0:T(8,128)S(1)}, u32[]{:S(2)}, u32[]{:S(2)}) collective-permute-start(f32[8,8,64]{2,1,0:T(8,128)S(1)} %get-tuple-element.31), channel_id=1, source_target_pairs={{0,2},{1,3},{2,4},{3,5},{4,6},{5,7},{6,0},{7,1},{8,10},{9,11},{10,... | collective-permute-start | bytes 49160 | tf_op jit(solution)/shard_map/ppermute | solution.py:172
  165.3 9.7 %collective-permute-start.29 = (f32[8,8,64]{2,1,0:T(8,128)S(1)}, f32[8,8,64]{2,1,0:T(8,128)S(1)}, u32[]{:S(2)}, u32[]{:S(2)}) collective-permute-start(f32[8,8,64]{2,1,0:T(8,128)S(1)} %get-tuple-element.35), channel_id=1, source_target_pairs={{0,248},{1,249},{2,250},{3,251},{4,252},{5,253},{6,254},{7,255},{8... | collective-permute-start | bytes 49160 | tf_op jit(solution)/shard_map/ppermute | solution.py:172
  173.5 8.1 %collective-permute-start.28 = (f32[8,8,64]{2,1,0:T(8,128)S(1)}, f32[8,8,64]{2,1,0:T(8,128)S(1)}, u32[]{:S(2)}, u32[]{:S(2)}) collective-permute-start(f32[8,8,64]{2,1,0:T(8,128)S(1)} %get-tuple-element.34), channel_id=1, source_target_pairs={{0,8},{1,9},{2,10},{3,11},{4,12},{5,13},{6,14},{7,15},{8,16},{9,17... | collective-permute-start | bytes 49160 | tf_op jit(solution)/shard_map/ppermute | solution.py:172
  (2 other events, 2.8 us)

commit v3 on v2

--- a/solution.py
+++ b/solution.py
@@ -157,6 +157,20 @@
                     give_ref[d, q] = jnp.where(even, part[j, 1], part[j, 0])
 
 
+def merge_kernel(keep0, got0, keep, got, *out):
+    size = keep0.shape[1]
+    for d, ref in enumerate(out):
+        ref[:size] = keep0[d] + got0[d]
+        ref[size:] = keep[d] + got[d]
+
+
+def total_kernel(a, b, c, d, *out):
+    size = out[0].shape[0]
+    for g, ref in enumerate(out):
+        span = slice(g * size, (g + 1) * size)
+        ref[...] = a[span] + b[span] + c[span] + d[span]
+
+
 def shards(pair_conduction, pair_valence, screened, sphere_sizes):
     owners = lax.axis_size("kr")
     quarters = lax.axis_size("kc") // 2
@@ -257,22 +271,19 @@
             (*accs, *far, w0, w1, *conduction),
         )
 
-    def exchange(keep, give):
-        keep = keep + swap(give)
-        parts = [send(keep[d], lambda i, k, c: (i, k + d, c)) for d in (1, 3, 2)]
-        return keep[0] + parts[0] + parts[1] + parts[2]
-
     accs = [first(g, 1, (own[g], ahead[g], behind[g])) for g in (1, 2)]
-    both = exchange(*last((1, 2), accs, far))
-    results = [
-        send(
-            both[(g - 1) * group_size : g * group_size],
-            lambda i, k, c: (i - shift[g], k, c),
-        )
-        for g in (1, 2)
-    ]
+    keep, give = last((1, 2), accs, far)
+    got = swap(give)
     acc = first(0, 2, (*v0, *up, *down))
-    results.insert(0, exchange(*last((0,), [acc], far0)))
+    keep0, give0 = last((0,), [acc], far0)
+    got0 = swap(give0)
+    block_shape = jax.ShapeDtypeStruct((3 * group_size, *keep.shape[2:]), jnp.float32)
+    blocks = call(merge_kernel, [block_shape] * quarters, (keep0, got0, keep, got))
+    others = [send(blocks[d], lambda i, k, c: (i, k + d, c)) for d in (1, 3, 2)]
+    group_shape = jax.ShapeDtypeStruct((group_size, *keep.shape[2:]), jnp.float32)
+    results = list(call(total_kernel, [group_shape] * 3, (blocks[0], *others)))
+    for g in (1, 2):
+        results[g] = send(results[g], lambda i, k, c: (i - shift[g], k, c))
     return jnp.concatenate(results, 0)
 
 

time: 182 us -> 189 us (1.038)
  the two profiles are of different devices: /device:TPU:64 before, /device:TPU:30 now
where the time goes in v3:
time: 189 us
  starting transfers between devices  94.9 us (50%)
  waiting for transfers between devices  78.3 us (41%)
  Pallas kernels  12.2 us (6%)
  local copies, waits for them, and re-layouts  3.12 us (2%)
    ppermute x27, starting transfers between devices, send(): return lax.ppermute(x, AXES, moves(owners, quarters, target))  94.9 us
    ppermute x27, waiting for transfers between devices, send(): return lax.ppermute(x, AXES, moves(owners, quarters, target))  78.3 us
    pallas_call x9, Pallas kernels, call(): pl.pallas_call(body, in_specs=in_specs or [VMEM] * len(operands), out_spe...  12.2 us
  transfers between devices with their start and end apart: 27, of which 11 were waited for; matrix products, arithmetic and copies ran while one was open for 0% of the time, Pallas kernels for 5%

profile of v3, /device:TPU:30, one launch (start us, length us, event | category | flops | bytes accessed | tf_op | source)
XLA Modules:
  0.0 189.4 jit_solution(7841539062863410524)
XLA Ops:
  0.0 2.2 %copy-done = bf16[1,512,4096]{2,1,0:T(8,128)(2,1)S(1)} copy-done((bf16[1,512,4096]{2,1,0:T(8,128)(2,1)S(1)}, bf16[1,512,4096]{2,1,0:T(8,128)(2,1)}, u32[]{:S(2)}) %copy-start) | copy-done | bytes 4194328
  2.8 2.0 %shard_map.46 = (bf16[512,2048]{1,0:T(8,128)(2,1)S(1)}, bf16[512,2048]{1,0:T(8,128)(2,1)S(1)}) custom-call(s32[32]{0:T(128)S(1)} %copy-done.1, bf16[512,4096]{1,0:T(8,128)(2,1)S(1)} %bitcast.1), custom_call_target="tpu_custom_call" | custom-call | tf_op jit(solution)/shard_map/pallas_call | solution.py:193
  5.1 1.6 collective-permute-start.12
  6.7 5.5 %collective-permute-start.13 = (bf16[8,64,512]{2,1,0:T(8,128)(2,1)S(1)}, bf16[8,64,512]{2,1,0:T(8,128)(2,1)S(1)}, u32[]{:S(2)}, u32[]{:S(2)}) collective-permute-start(bf16[8,64,512]{2,1,0:T(8,128)(2,1)S(1)} %get-tuple-element.38), channel_id=1, source_target_pairs={{0,10},{1,11},{2,12},{3,13},{4,14},{5,15},{6,8},{7,9},{8,18},{9,19... | collective-permute-start | bytes 1572872 | tf_op jit(solution)/shard_map/ppermute | solution.py:186
  12.2 3.7 %collective-permute-start.10 = (bf16[8,64,512]{2,1,0:T(8,128)(2,1)S(1)}, bf16[8,64,512]{2,1,0:T(8,128)(2,1)S(1)}, u32[]{:S(2)}, u32[]{:S(2)}) collective-permute-start(bf16[8,64,512]{2,1,0:T(8,128)(2,1)S(1)} %get-tuple-element.39), channel_id=1, source_target_pairs={{0,254},{1,255},{2,248},{3,249},{4,250},{5,251},{6,252},{7,253},{8... | collective-permute-start | bytes 1572872 | tf_op jit(solution)/shard_map/ppermute | solution.py:186
  16.0 14.7 %collective-permute-done.12.refs_0_ = bf16[8,64,512]{2,1,0:T(8,128)(2,1)S(1)} collective-permute-done((bf16[8,64,512]{2,1,0:T(8,128)(2,1)S(1)}, bf16[8,64,512]{2,1,0:T(8,128)(2,1)S(1)}, u32[]{:S(2)}, u32[]{:S(2)}) %collective-permute-start.12) | collective-permute-done | bytes 524320 | tf_op jit(solution)/shard_map/ppermute | solution.py:186
  31.5 5.5 %collective-permute-start.19 = (bf16[8,64,512]{2,1,0:T(8,128)(2,1)S(1)}, bf16[8,64,512]{2,1,0:T(8,128)(2,1)S(1)}, u32[]{:S(2)}, u32[]{:S(2)}) collective-permute-start(bf16[8,64,512]{2,1,0:T(8,128)(2,1)S(1)} %get-tuple-element.35), channel_id=1, source_target_pairs={{0,8},{1,9},{2,10},{3,11},{4,12},{5,13},{6,14},{7,15},{8,16},{9,17... | collective-permute-start | bytes 1572872 | tf_op jit(solution)/shard_map/ppermute | solution.py:186
  37.0 11.2 %collective-permute-done.9.refs_0_ = bf16[8,64,512]{2,1,0:T(8,128)(2,1)S(1)} collective-permute-done((bf16[8,64,512]{2,1,0:T(8,128)(2,1)S(1)}, bf16[8,64,512]{2,1,0:T(8,128)(2,1)S(1)}, u32[]{:S(2)}, u32[]{:S(2)}) %collective-permute-start.9) | collective-permute-done | bytes 524320 | tf_op jit(solution)/shard_map/ppermute | solution.py:186
  48.2 2.7 %collective-permute-start.14 = (bf16[8,64,512]{2,1,0:T(8,128)(2,1)S(1)}, bf16[8,64,512]{2,1,0:T(8,128)(2,1)S(1)}, u32[]{:S(2)}, u32[]{:S(2)}) collective-permute-start(bf16[8,64,512]{2,1,0:T(8,128)(2,1)S(1)} %collective-permute-done.12.refs_0_), channel_id=1, source_target_pairs={{0,6},{1,7},{2,0},{3,1},{4,2},{5,3},{6,4},{7,5},{8,14},{9,15},{10,... | collective-permute-start | bytes 1572872 | tf_op jit(solution)/shard_map/ppermute | solution.py:186
  50.9 2.4 %collective-permute-start.11 = (bf16[8,64,512]{2,1,0:T(8,128)(2,1)S(1)}, bf16[8,64,512]{2,1,0:T(8,128)(2,1)S(1)}, u32[]{:S(2)}, u32[]{:S(2)}) collective-permute-start(bf16[8,64,512]{2,1,0:T(8,128)(2,1)S(1)} %collective-permute-done.9.refs_0_), channel_id=1, source_target_pairs={{0,6},{1,7},{2,0},{3,1},{4,2},{5,3},{6,4},{7,5},{8,14},{9,15},{10,... | collective-permute-start | bytes 1572872 | tf_op jit(solution)/shard_map/ppermute | solution.py:186
  53.3 16.5 %collective-permute-done.17.refs_6_ = bf16[8,64,512]{2,1,0:T(8,128)(2,1)S(1)} collective-permute-done((bf16[8,64,512]{2,1,0:T(8,128)(2,1)S(1)}, bf16[8,64,512]{2,1,0:T(8,128)(2,1)S(1)}, u32[]{:S(2)}, u32[]{:S(2)}) %collective-permute-start.17) | collective-permute-done | bytes 524320 | tf_op jit(solution)/shard_map/ppermute | solution.py:186
  69.9 13.9 %collective-permute-start.3 = (bf16[4,64,512]{2,1,0:T(8,128)(2,1)S(1)}, bf16[4,64,512]{2,1,0:T(8,128)(2,1)S(1)}, u32[]{:S(2)}, u32[]{:S(2)}) collective-permute-start(bf16[4,64,512]{2,1,0:T(8,128)(2,1)S(1)} %get-tuple-element.40.refs_1_), channel_id=1, source_target_pairs={{0,6},{1,7},{2,0},{3,1},{4,2},{5,3},{6,4},{7,5},{8,14},{9,15},{10,... | collective-permute-start | bytes 786440 | tf_op jit(solution)/shard_map/ppermute | solution.py:186
  84.4 5.3 %collective-permute-done.refs_2_ = bf16[4,64,512]{2,1,0:T(8,128)(2,1)S(1)} collective-permute-done((bf16[4,64,512]{2,1,0:T(8,128)(2,1)S(1)}, bf16[4,64,512]{2,1,0:T(8,128)(2,1)S(1)}, u32[]{:S(2)}, u32[]{:S(2)}) %collective-permute-start) | collective-permute-done | bytes 262176 | tf_op jit(solution)/shard_map/ppermute | solution.py:186
  89.7 13.9 %collective-permute-start.15 = (bf16[8,64,512]{2,1,0:T(8,128)(2,1)S(1)}, bf16[8,64,512]{2,1,0:T(8,128)(2,1)S(1)}, u32[]{:S(2)}, u32[]{:S(2)}) collective-permute-start(bf16[8,64,512]{2,1,0:T(8,128)(2,1)S(1)} %get-tuple-element.24), channel_id=1, source_target_pairs={{0,2},{1,3},{2,4},{3,5},{4,6},{5,7},{6,0},{7,1},{8,10},{9,11},{10,... | collective-permute-start | bytes 1572872 | tf_op jit(solution)/shard_map/ppermute | solution.py:186
  103.6 27.0 %collective-permute-start.16 = (bf16[8,64,512]{2,1,0:T(8,128)(2,1)S(1)}, bf16[8,64,512]{2,1,0:T(8,128)(2,1)S(1)}, u32[]{:S(2)}, u32[]{:S(2)}) collective-permute-start(bf16[8,64,512]{2,1,0:T(8,128)(2,1)S(1)} %get-tuple-element.25), channel_id=1, source_target_pairs={{0,6},{1,7},{2,0},{3,1},{4,2},{5,3},{6,4},{7,5},{8,14},{9,15},{10,... | collective-permute-start | bytes 1572872 | tf_op jit(solution)/shard_map/ppermute | solution.py:186
  130.8 12.6 %collective-permute-done.15.refs_2_ = bf16[8,64,512]{2,1,0:T(8,128)(2,1)S(1)} collective-permute-done((bf16[8,64,512]{2,1,0:T(8,128)(2,1)S(1)}, bf16[8,64,512]{2,1,0:T(8,128)(2,1)S(1)}, u32[]{:S(2)}, u32[]{:S(2)}) %collective-permute-start.15) | collective-permute-done | bytes 524320 | tf_op jit(solution)/shard_map/ppermute | solution.py:186
  143.4 4.9 %collective-permute-start.2 = (bf16[4,64,512]{2,1,0:T(8,128)(2,1)S(1)}, bf16[4,64,512]{2,1,0:T(8,128)(2,1)S(1)}, u32[]{:S(2)}, u32[]{:S(2)}) collective-permute-start(bf16[4,64,512]{2,1,0:T(8,128)(2,1)S(1)} %get-tuple-element.41.refs_0_), channel_id=1, source_target_pairs={{0,6},{1,7},{2,0},{3,1},{4,2},{5,3},{6,4},{7,5},{8,14},{9,15},{10,... | collective-permute-start | bytes 786440 | tf_op jit(solution)/shard_map/ppermute | solution.py:186
  148.4 4.1 %collective-permute-start.6 = (bf16[4,64,512]{2,1,0:T(8,128)(2,1)S(1)}, bf16[4,64,512]{2,1,0:T(8,128)(2,1)S(1)}, u32[]{:S(2)}, u32[]{:S(2)}) collective-permute-start(bf16[4,64,512]{2,1,0:T(8,128)(2,1)S(1)} %collective-permute-done.3.refs_5_), channel_id=1, source_target_pairs={{0,6},{1,7},{2,0},{3,1},{4,2},{5,3},{6,4},{7,5},{8,14},{9,15},{10,... | collective-permute-start | bytes 786440 | tf_op jit(solution)/shard_map/ppermute | solution.py:186
  152.5 1.8 shard_map.50.refs_1_
  154.3 1.8 shard_map.49.refs_0_
  156.2 2.9 %shard_map.52 = (f32[4,16,8,64]{3,2,1,0:T(8,128)S(1)}, f32[4,16,8,64]{3,2,1,0:T(8,128)S(1)}) custom-call(f32[2,512,512]{2,1,0:T(8,128)S(1)} %shard_map.49.refs_0_, f32[2,512,512]{2,1,0:T(8,128)S(1)} %shard_map.50.refs_1_, bf16[8,64,512]{2,1,0:T(8,128)(2,1)S(1)} %collective-permute-done.15.refs_2_, bf16[8,64,512]{2,1,0:T(8,128)(2,1)S(1)} %collective-permute-done.16.refs_3_, ...), custom_call_target="tpu_custom_call" | custom-call | tf_op jit(solution)/shard_map/pallas_call | solution.py:193
  159.3 1.8 shard_map.47.refs_0_
  161.1 1.7 collective-permute-done.6.refs_2_
  162.9 1.6 shard_map.48
  164.6 1.3 collective-permute-done.8.got0
  166.2 4.1 %collective-permute-start.23 = (f32[24,8,64]{2,1,0:T(8,128)S(1)}, f32[24,8,64]{2,1,0:T(8,128)S(1)}, u32[]{:S(2)}, u32[]{:S(2)}) collective-permute-start(f32[24,8,64]{2,1,0:T(8,128)S(1)} %get-tuple-element.30), channel_id=1, source_target_pairs={{0,6},{1,7},{2,0},{3,1},{4,2},{5,3},{6,4},{7,5},{8,14},{9,15},{10,... | collective-permute-start | bytes 147464 | tf_op jit(solution)/shard_map/ppermute | solution.py:186
  170.4 1.4 collective-permute-start.24
  171.8 1.4 collective-permute-done.22.b
  173.2 7.2 %collective-permute-done.24.d = f32[24,8,64]{2,1,0:T(8,128)S(1)} collective-permute-done((f32[24,8,64]{2,1,0:T(8,128)S(1)}, f32[24,8,64]{2,1,0:T(8,128)S(1)}, u32[]{:S(2)}, u32[]{:S(2)}) %collective-permute-start.24) | collective-permute-done | bytes 49184 | tf_op jit(solution)/shard_map/ppermute | solution.py:186
  180.5 2.0 %collective-permute-start.26 = (f32[8,8,64]{2,1,0:T(8,128)S(1)}, f32[8,8,64]{2,1,0:T(8,128)S(1)}, u32[]{:S(2)}, u32[]{:S(2)}) collective-permute-start(f32[8,8,64]{2,1,0:T(8,128)S(1)} %get-tuple-element.34), channel_id=1, source_target_pairs={{0,248},{1,249},{2,250},{3,251},{4,252},{5,253},{6,254},{7,255},{8... | collective-permute-start | bytes 49160 | tf_op jit(solution)/shard_map/ppermute | solution.py:186
  182.5 1.9 collective-permute-done.25
  184.4 4.3 %collective-permute-done.26 = f32[8,8,64]{2,1,0:T(8,128)S(1)} collective-permute-done((f32[8,8,64]{2,1,0:T(8,128)S(1)}, f32[8,8,64]{2,1,0:T(8,128)S(1)}, u32[]{:S(2)}, u32[]{:S(2)}) %collective-permute-start.26) | collective-permute-done | bytes 16416 | tf_op jit(solution)/shard_map/ppermute | solution.py:186
  (43 shorter events, 3.9 us)
Async XLA Ops:
  0.0 2.2 %copy-start = (bf16[1,512,4096]{2,1,0:T(8,128)(2,1)S(1)}, bf16[1,512,4096]{2,1,0:T(8,128)(2,1)}, u32[]{:S(2)}) copy-start(bf16[1,512,4096]{2,1,0:T(8,128)(2,1)} %param.6) | copy-start | bytes 12582916
  2.2 0.7 copy-start.1
  2.8 2.1 %copy-start.3 = (bf16[24,64,512]{2,1,0:T(8,128)(2,1)S(1)}, bf16[24,64,512]{2,1,0:T(8,128)(2,1)}, u32[]{:S(2)}) copy-start(bf16[24,64,512]{2,1,0:T(8,128)(2,1)} %param.5) | copy-start | bytes 4718596
  4.9 11.0 %copy-start.2 = (bf16[24,64,512]{2,1,0:T(8,128)(2,1)S(1)}, bf16[24,64,512]{2,1,0:T(8,128)(2,1)}, u32[]{:S(2)}) copy-start(bf16[24,64,512]{2,1,0:T(8,128)(2,1)} %param.4) | copy-start | bytes 4718596
  4.9 143.5 %collective-permute-start.4 = (bf16[512,2048]{1,0:T(8,128)(2,1)S(1)}, bf16[512,2048]{1,0:T(8,128)(2,1)S(1)}, u32[]{:S(2)}, u32[]{:S(2)}) collective-permute-start(bf16[512,2048]{1,0:T(8,128)(2,1)S(1)} %get-tuple-element.21), channel_id=1, source_target_pairs={{0,1},{1,0},{2,3},{3,2},{4,5},{5,4},{6,7},{7,6},{8,9},{9,8},{10,11... | collective-permute-start | bytes 6291464 | tf_op jit(solution)/shard_map/ppermute | solution.py:186
  5.1 25.6 %collective-permute-start.12 = (bf16[8,64,512]{2,1,0:T(8,128)(2,1)S(1)}, bf16[8,64,512]{2,1,0:T(8,128)(2,1)S(1)}, u32[]{:S(2)}, u32[]{:S(2)}) collective-permute-start(bf16[8,64,512]{2,1,0:T(8,128)(2,1)S(1)} %get-tuple-element.38), channel_id=1, source_target_pairs={{0,8},{1,9},{2,10},{3,11},{4,12},{5,13},{6,14},{7,15},{8,16},{9,17... | collective-permute-start | bytes 1572872 | tf_op jit(solution)/shard_map/ppermute | solution.py:186
  6.7 24.8 %collective-permute-start.13 = (bf16[8,64,512]{2,1,0:T(8,128)(2,1)S(1)}, bf16[8,64,512]{2,1,0:T(8,128)(2,1)S(1)}, u32[]{:S(2)}, u32[]{:S(2)}) collective-permute-start(bf16[8,64,512]{2,1,0:T(8,128)(2,1)S(1)} %get-tuple-element.38), channel_id=1, source_target_pairs={{0,10},{1,11},{2,12},{3,13},{4,14},{5,15},{6,8},{7,9},{8,18},{9,19... | collective-permute-start | bytes 1572872 | tf_op jit(solution)/shard_map/ppermute | solution.py:186
  12.2 36.0 %collective-permute-start.9 = (bf16[8,64,512]{2,1,0:T(8,128)(2,1)S(1)}, bf16[8,64,512]{2,1,0:T(8,128)(2,1)S(1)}, u32[]{:S(2)}, u32[]{:S(2)}) collective-permute-start(bf16[8,64,512]{2,1,0:T(8,128)(2,1)S(1)} %get-tuple-element.39), channel_id=1, source_target_pairs={{0,248},{1,249},{2,250},{3,251},{4,252},{5,253},{6,254},{7,255},{8... | collective-permute-start | bytes 1572872 | tf_op jit(solution)/shard_map/ppermute | solution.py:186
  12.2 38.7 %collective-permute-start.10 = (bf16[8,64,512]{2,1,0:T(8,128)(2,1)S(1)}, bf16[8,64,512]{2,1,0:T(8,128)(2,1)S(1)}, u32[]{:S(2)}, u32[]{:S(2)}) collective-permute-start(bf16[8,64,512]{2,1,0:T(8,128)(2,1)S(1)} %get-tuple-element.39), channel_id=1, source_target_pairs={{0,254},{1,255},{2,248},{3,249},{4,250},{5,251},{6,252},{7,253},{8... | collective-permute-start | bytes 1572872 | tf_op jit(solution)/shard_map/ppermute | solution.py:186
  30.7 39.1 %collective-permute-start.17 = (bf16[8,64,512]{2,1,0:T(8,128)(2,1)S(1)}, bf16[8,64,512]{2,1,0:T(8,128)(2,1)S(1)}, u32[]{:S(2)}, u32[]{:S(2)}) collective-permute-start(bf16[8,64,512]{2,1,0:T(8,128)(2,1)S(1)} %get-tuple-element.37), channel_id=1, source_target_pairs={{0,248},{1,249},{2,250},{3,251},{4,252},{5,253},{6,254},{7,255},{8... | collective-permute-start | bytes 1572872 | tf_op jit(solution)/shard_map/ppermute | solution.py:186
  31.5 38.4 %collective-permute-start.19 = (bf16[8,64,512]{2,1,0:T(8,128)(2,1)S(1)}, bf16[8,64,512]{2,1,0:T(8,128)(2,1)S(1)}, u32[]{:S(2)}, u32[]{:S(2)}) collective-permute-start(bf16[8,64,512]{2,1,0:T(8,128)(2,1)S(1)} %get-tuple-element.35), channel_id=1, source_target_pairs={{0,8},{1,9},{2,10},{3,11},{4,12},{5,13},{6,14},{7,15},{8,16},{9,17... | collective-permute-start | bytes 1572872 | tf_op jit(solution)/shard_map/ppermute | solution.py:186
  48.2 35.6 %collective-permute-start.14 = (bf16[8,64,512]{2,1,0:T(8,128)(2,1)S(1)}, bf16[8,64,512]{2,1,0:T(8,128)(2,1)S(1)}, u32[]{:S(2)}, u32[]{:S(2)}) collective-permute-start(bf16[8,64,512]{2,1,0:T(8,128)(2,1)S(1)} %collective-permute-done.12.refs_0_), channel_id=1, source_target_pairs={{0,6},{1,7},{2,0},{3,1},{4,2},{5,3},{6,4},{7,5},{8,14},{9,15},{10,... | collective-permute-start | bytes 1572872 | tf_op jit(solution)/shard_map/ppermute | solution.py:186
  50.9 32.9 %collective-permute-start.11 = (bf16[8,64,512]{2,1,0:T(8,128)(2,1)S(1)}, bf16[8,64,512]{2,1,0:T(8,128)(2,1)S(1)}, u32[]{:S(2)}, u32[]{:S(2)}) collective-permute-start(bf16[8,64,512]{2,1,0:T(8,128)(2,1)S(1)} %collective-permute-done.9.refs_0_), channel_id=1, source_target_pairs={{0,6},{1,7},{2,0},{3,1},{4,2},{5,3},{6,4},{7,5},{8,14},{9,15},{10,... | collective-permute-start | bytes 1572872 | tf_op jit(solution)/shard_map/ppermute | solution.py:186
  69.8 19.8 %collective-permute-start = (bf16[4,64,512]{2,1,0:T(8,128)(2,1)S(1)}, bf16[4,64,512]{2,1,0:T(8,128)(2,1)S(1)}, u32[]{:S(2)}, u32[]{:S(2)}) collective-permute-start(bf16[4,64,512]{2,1,0:T(8,128)(2,1)S(1)} %get-tuple-element.41.refs_0_), channel_id=1, source_target_pairs={{0,2},{1,3},{2,4},{3,5},{4,6},{5,7},{6,0},{7,1},{8,10},{9,11},{10,... | collective-permute-start | bytes 786440 | tf_op jit(solution)/shard_map/ppermute | solution.py:186
  69.9 33.7 %collective-permute-start.3 = (bf16[4,64,512]{2,1,0:T(8,128)(2,1)S(1)}, bf16[4,64,512]{2,1,0:T(8,128)(2,1)S(1)}, u32[]{:S(2)}, u32[]{:S(2)}) collective-permute-start(bf16[4,64,512]{2,1,0:T(8,128)(2,1)S(1)} %get-tuple-element.40.refs_1_), channel_id=1, source_target_pairs={{0,6},{1,7},{2,0},{3,1},{4,2},{5,3},{6,4},{7,5},{8,14},{9,15},{10,... | collective-permute-start | bytes 786440 | tf_op jit(solution)/shard_map/ppermute | solution.py:186
  83.8 46.8 %collective-permute-start.18 = (bf16[8,64,512]{2,1,0:T(8,128)(2,1)S(1)}, bf16[8,64,512]{2,1,0:T(8,128)(2,1)S(1)}, u32[]{:S(2)}, u32[]{:S(2)}) collective-permute-start(bf16[8,64,512]{2,1,0:T(8,128)(2,1)S(1)} %collective-permute-done.17.refs_6_), channel_id=1, source_target_pairs={{0,1},{1,0},{2,3},{3,2},{4,5},{5,4},{6,7},{7,6},{8,9},{9,8},{10,11... | collective-permute-start | bytes 1572872 | tf_op jit(solution)/shard_map/ppermute | solution.py:186
  83.8 46.8 %collective-permute-start.20 = (bf16[8,64,512]{2,1,0:T(8,128)(2,1)S(1)}, bf16[8,64,512]{2,1,0:T(8,128)(2,1)S(1)}, u32[]{:S(2)}, u32[]{:S(2)}) collective-permute-start(bf16[8,64,512]{2,1,0:T(8,128)(2,1)S(1)} %collective-permute-done.19.refs_8_), channel_id=1, source_target_pairs={{0,1},{1,0},{2,3},{3,2},{4,5},{5,4},{6,7},{7,6},{8,9},{9,8},{10,11... | collective-permute-start | bytes 1572872 | tf_op jit(solution)/shard_map/ppermute | solution.py:186
  89.7 53.8 %collective-permute-start.15 = (bf16[8,64,512]{2,1,0:T(8,128)(2,1)S(1)}, bf16[8,64,512]{2,1,0:T(8,128)(2,1)S(1)}, u32[]{:S(2)}, u32[]{:S(2)}) collective-permute-start(bf16[8,64,512]{2,1,0:T(8,128)(2,1)S(1)} %get-tuple-element.24), channel_id=1, source_target_pairs={{0,2},{1,3},{2,4},{3,5},{4,6},{5,7},{6,0},{7,1},{8,10},{9,11},{10,... | collective-permute-start | bytes 1572872 | tf_op jit(solution)/shard_map/ppermute | solution.py:186
  103.6 44.8 %collective-permute-start.16 = (bf16[8,64,512]{2,1,0:T(8,128)(2,1)S(1)}, bf16[8,64,512]{2,1,0:T(8,128)(2,1)S(1)}, u32[]{:S(2)}, u32[]{:S(2)}) collective-permute-start(bf16[8,64,512]{2,1,0:T(8,128)(2,1)S(1)} %get-tuple-element.25), channel_id=1, source_target_pairs={{0,6},{1,7},{2,0},{3,1},{4,2},{5,3},{6,4},{7,5},{8,14},{9,15},{10,... | collective-permute-start | bytes 1572872 | tf_op jit(solution)/shard_map/ppermute | solution.py:186
  130.5 32.3 %collective-permute-start.7 = (bf16[8,64,512]{2,1,0:T(8,128)(2,1)S(1)}, bf16[8,64,512]{2,1,0:T(8,128)(2,1)S(1)}, u32[]{:S(2)}, u32[]{:S(2)}) collective-permute-start(bf16[8,64,512]{2,1,0:T(8,128)(2,1)S(1)} %get-tuple-element.36.refs_5_), channel_id=1, source_target_pairs={{0,1},{1,0},{2,3},{3,2},{4,5},{5,4},{6,7},{7,6},{8,9},{9,8},{10,11... | collective-permute-start | bytes 1572872 | tf_op jit(solution)/shard_map/ppermute | solution.py:186
  130.6 28.6 %collective-permute-start.1 = (bf16[4,64,512]{2,1,0:T(8,128)(2,1)S(1)}, bf16[4,64,512]{2,1,0:T(8,128)(2,1)S(1)}, u32[]{:S(2)}, u32[]{:S(2)}) collective-permute-start(bf16[4,64,512]{2,1,0:T(8,128)(2,1)S(1)} %get-tuple-element.40.refs_1_), channel_id=1, source_target_pairs={{0,2},{1,3},{2,4},{3,5},{4,6},{5,7},{6,0},{7,1},{8,10},{9,11},{10,... | collective-permute-start | bytes 786440 | tf_op jit(solution)/shard_map/ppermute | solution.py:186
  143.4 15.8 %collective-permute-start.2 = (bf16[4,64,512]{2,1,0:T(8,128)(2,1)S(1)}, bf16[4,64,512]{2,1,0:T(8,128)(2,1)S(1)}, u32[]{:S(2)}, u32[]{:S(2)}) collective-permute-start(bf16[4,64,512]{2,1,0:T(8,128)(2,1)S(1)} %get-tuple-element.41.refs_0_), channel_id=1, source_target_pairs={{0,6},{1,7},{2,0},{3,1},{4,2},{5,3},{6,4},{7,5},{8,14},{9,15},{10,... | collective-permute-start | bytes 786440 | tf_op jit(solution)/shard_map/ppermute | solution.py:186
  148.4 12.7 %collective-permute-start.5 = (bf16[4,64,512]{2,1,0:T(8,128)(2,1)S(1)}, bf16[4,64,512]{2,1,0:T(8,128)(2,1)S(1)}, u32[]{:S(2)}, u32[]{:S(2)}) collective-permute-start(bf16[4,64,512]{2,1,0:T(8,128)(2,1)S(1)} %collective-permute-done.refs_2_), channel_id=1, source_target_pairs={{0,2},{1,3},{2,4},{3,5},{4,6},{5,7},{6,0},{7,1},{8,10},{9,11},{10,... | collective-permute-start | bytes 786440 | tf_op jit(solution)/shard_map/ppermute | solution.py:186
  148.4 14.5 %collective-permute-start.6 = (bf16[4,64,512]{2,1,0:T(8,128)(2,1)S(1)}, bf16[4,64,512]{2,1,0:T(8,128)(2,1)S(1)}, u32[]{:S(2)}, u32[]{:S(2)}) collective-permute-start(bf16[4,64,512]{2,1,0:T(8,128)(2,1)S(1)} %collective-permute-done.3.refs_5_), channel_id=1, source_target_pairs={{0,6},{1,7},{2,0},{3,1},{4,2},{5,3},{6,4},{7,5},{8,14},{9,15},{10,... | collective-permute-start | bytes 786440 | tf_op jit(solution)/shard_map/ppermute | solution.py:186
  159.1 6.7 %collective-permute-start.21 = (f32[4,16,8,64]{3,2,1,0:T(8,128)S(1)}, f32[4,16,8,64]{3,2,1,0:T(8,128)S(1)}, u32[]{:S(2)}, u32[]{:S(2)}) collective-permute-start(f32[4,16,8,64]{3,2,1,0:T(8,128)S(1)} %get-tuple-element.27), channel_id=1, source_target_pairs={{0,1},{1,0},{2,3},{3,2},{4,5},{5,4},{6,7},{7,6},{8,9},{9,8},{10,11... | collective-permute-start | bytes 393224 | tf_op jit(solution)/shard_map/ppermute | solution.py:186
  164.4 1.4 collective-permute-start.8
  165.9 7.3 %collective-permute-start.22 = (f32[24,8,64]{2,1,0:T(8,128)S(1)}, f32[24,8,64]{2,1,0:T(8,128)S(1)}, u32[]{:S(2)}, u32[]{:S(2)}) collective-permute-start(f32[24,8,64]{2,1,0:T(8,128)S(1)} %get-tuple-element.29), channel_id=1, source_target_pairs={{0,2},{1,3},{2,4},{3,5},{4,6},{5,7},{6,0},{7,1},{8,10},{9,11},{10,... | collective-permute-start | bytes 147464 | tf_op jit(solution)/shard_map/ppermute | solution.py:186
  166.2 6.9 %collective-permute-start.23 = (f32[24,8,64]{2,1,0:T(8,128)S(1)}, f32[24,8,64]{2,1,0:T(8,128)S(1)}, u32[]{:S(2)}, u32[]{:S(2)}) collective-permute-start(f32[24,8,64]{2,1,0:T(8,128)S(1)} %get-tuple-element.30), channel_id=1, source_target_pairs={{0,6},{1,7},{2,0},{3,1},{4,2},{5,3},{6,4},{7,5},{8,14},{9,15},{10,... | collective-permute-start | bytes 147464 | tf_op jit(solution)/shard_map/ppermute | solution.py:186
  170.4 10.0 %collective-permute-start.24 = (f32[24,8,64]{2,1,0:T(8,128)S(1)}, f32[24,8,64]{2,1,0:T(8,128)S(1)}, u32[]{:S(2)}, u32[]{:S(2)}) collective-permute-start(f32[24,8,64]{2,1,0:T(8,128)S(1)} %get-tuple-element.31), channel_id=1, source_target_pairs={{0,4},{1,5},{2,6},{3,7},{4,0},{5,1},{6,2},{7,3},{8,12},{9,13},{10,... | collective-permute-start | bytes 147464 | tf_op jit(solution)/shard_map/ppermute | solution.py:186
  180.4 4.0 %collective-permute-start.25 = (f32[8,8,64]{2,1,0:T(8,128)S(1)}, f32[8,8,64]{2,1,0:T(8,128)S(1)}, u32[]{:S(2)}, u32[]{:S(2)}) collective-permute-start(f32[8,8,64]{2,1,0:T(8,128)S(1)} %get-tuple-element.33), channel_id=1, source_target_pairs={{0,8},{1,9},{2,10},{3,11},{4,12},{5,13},{6,14},{7,15},{8,16},{9,17... | collective-permute-start | bytes 49160 | tf_op jit(solution)/shard_map/ppermute | solution.py:186
  180.5 8.2 %collective-permute-start.26 = (f32[8,8,64]{2,1,0:T(8,128)S(1)}, f32[8,8,64]{2,1,0:T(8,128)S(1)}, u32[]{:S(2)}, u32[]{:S(2)}) collective-permute-start(f32[8,8,64]{2,1,0:T(8,128)S(1)} %get-tuple-element.34), channel_id=1, source_target_pairs={{0,248},{1,249},{2,250},{3,251},{4,252},{5,253},{6,254},{7,255},{8... | collective-permute-start | bytes 49160 | tf_op jit(solution)/shard_map/ppermute | solution.py:186

commit v4 on v3

--- a/solution.py
+++ b/solution.py
@@ -20,7 +20,10 @@
     for i in range(owners):
         for k in range(quarters):
             for c in range(2):
-                ti, tk, tc = target(i, k, c)
+                to = target(i, k, c)
+                if to is None:
+                    continue
+                ti, tk, tc = to
                 pairs.append(
                     (
                         (i * quarters + k) * 2 + c,
@@ -32,6 +35,17 @@
 
 def turn(group, q, owners):
     return 1 if group == 0 or q < owners // 2 else -1
+
+
+def crossing(owners):
+    split = owners // 2
+    low, high = (0, 1, split - 4, 4), (split - 1, split - 2, 3, split - 5)
+    return {
+        0: (1, owners - 1, low),
+        split: (1, split - 1, tuple(split + m for m in low)),
+        split - 1: (2, split, high),
+        owners - 1: (2, 0, tuple(split + m for m in high)),
+    }
 
 
 def where_am_i():
@@ -78,6 +92,36 @@
         def _():
             up_ref[n * half : (n + 1) * half] = b[:half]
             down_ref[n * half : (n + 1) * half] = a[half:]
+
+
+def pick_kernel(owners, c1, c2, *out):
+    owner, _, _ = where_am_i()
+    group1 = lax.rem(owner, owners // 2) == 0
+    for c, flag in ((c1, group1), (c2, jnp.logical_not(group1))):
+
+        @pl.when(flag)
+        def _():
+            for p, ref in enumerate(out):
+                size = ref.shape[0]
+                ref[...] = c[p * size : (p + 1) * size]
+
+
+def place_kernel(owners, c1, c2, *refs):
+    parts, out = refs[:-2], refs[-2:]
+    owner, _, _ = where_am_i()
+    split = owners // 2
+    for c, ref, edge in ((c1, out[0], split - 1), (c2, out[1], 0)):
+        crossed = lax.rem(owner, split) == edge
+
+        @pl.when(crossed)
+        def _():
+            for p, part in enumerate(parts):
+                size = part.shape[0]
+                ref[p * size : (p + 1) * size] = part[...]
+
+        @pl.when(jnp.logical_not(crossed))
+        def _():
+            ref[...] = c[...]
 
 
 def flat(x):
@@ -214,9 +258,37 @@
                 c,
             ),
         )
+    edges = crossing(owners)
+    straight = {}
+    for g in (1, 2):
+        straight[g] = send(
+            cond[g],
+            lambda i, k, c: (
+                None if i in edges and edges[i][0] == g else (i + shift[g], k, c)
+            ),
+        )
+    count = len(edges[0][2])
+    part = jax.ShapeDtypeStruct((group_size // count, *cond[0].shape[1:]), cond[0].dtype)
+    parts = list(
+        call(functools.partial(pick_kernel, owners), [part] * count, (cond[1], cond[2]))
+    )
+    for p in range(count):
+        relays = {i: e[2][p] for i, e in edges.items()}
+        if any(i != m for i, m in relays.items()):
+            parts[p] = send(
+                parts[p], lambda i, k, c: (relays[i], k, c) if i in relays else None
+            )
+        ends = {e[2][p]: e[1] for e in edges.values()}
+        parts[p] = send(
+            parts[p], lambda i, k, c: (ends[i], k, c) if i in ends else None
+        )
+    whole = jax.ShapeDtypeStruct(cond[0].shape, cond[0].dtype)
     c_own = {0: cond[0]}
-    for g in (1, 2):
-        c_own[g] = send(cond[g], lambda i, k, c: (i + shift[g], k, c))
+    c_own[1], c_own[2] = call(
+        functools.partial(place_kernel, owners),
+        [whole] * 2,
+        (straight[1], straight[2], *parts),
+    )
     for g in (1, 2):
         behind[g] = send(own[g], lambda i, k, c: (i, k - turn(g, i, owners), c))
     v0 = [v[0][:half], v[0][half:]]

time: 189 us -> 194 us (1.026)
  the two profiles are of different devices: /device:TPU:30 before, /device:TPU:32 now
where the time goes in v4:
time: 194 us
  starting transfers between devices  93.9 us (48%)
  waiting for transfers between devices  84.9 us (44%)
  Pallas kernels  12.3 us (6%)
    ppermute x34, starting transfers between devices, send(): return lax.ppermute(x, AXES, moves(owners, quarters, target))  93.9 us
    ppermute x34, waiting for transfers between devices, send(): return lax.ppermute(x, AXES, moves(owners, quarters, target))  84.9 us
    pallas_call x11, Pallas kernels, call(): pl.pallas_call(body, in_specs=in_specs or [VMEM] * len(operands), out_spe...  12.3 us
  transfers between devices with their start and end apart: 34, of which 15 were waited for; matrix products, arithmetic and copies ran while one was open for 0% of the time, Pallas kernels for 6%

profile of v4, /device:TPU:32, one launch (start us, length us, event | category | flops | bytes accessed | tf_op | source)
XLA Modules:
  0.0 193.9 jit_solution(13462918510257816879)
XLA Ops:
  1.7 3.6 %collective-permute-start.20 = (bf16[2,64,512]{2,1,0:T(8,128)(2,1)S(1)}, bf16[2,64,512]{2,1,0:T(8,128)(2,1)S(1)}, u32[]{:S(2)}, u32[]{:S(2)}) collective-permute-start(bf16[2,64,512]{2,1,0:T(8,128)(2,1)S(1)} %get-tuple-element.33), channel_id=1, source_target_pairs={{0,8},{1,9},{2,10},{3,11},{4,12},{5,13},{6,14},{7,15},{120,112},{1... | collective-permute-start | bytes 393224 | tf_op jit(solution)/shard_map/ppermute | solution.py:230
  5.3 1.9 collective-permute-start.22
  7.2 2.0 %shard_map.46 = (bf16[512,2048]{1,0:T(8,128)(2,1)S(1)}, bf16[512,2048]{1,0:T(8,128)(2,1)S(1)}) custom-call(s32[32]{0:T(128)S(1)} %copy-done.1, bf16[512,4096]{1,0:T(8,128)(2,1)S(1)} %bitcast.1), custom_call_target="tpu_custom_call" | custom-call | tf_op jit(solution)/shard_map/pallas_call | solution.py:237
  9.4 5.3 %collective-permute-start.19 = (bf16[2,64,512]{2,1,0:T(8,128)(2,1)S(1)}, bf16[2,64,512]{2,1,0:T(8,128)(2,1)S(1)}, u32[]{:S(2)}, u32[]{:S(2)}) collective-permute-start(bf16[2,64,512]{2,1,0:T(8,128)(2,1)S(1)} %get-tuple-element.32), channel_id=1, source_target_pairs={{0,248},{1,249},{2,250},{3,251},{4,252},{5,253},{6,254},{7,255},{1... | collective-permute-start | bytes 393224 | tf_op jit(solution)/shard_map/ppermute | solution.py:230
  18.7 2.7 %collective-permute-done.19.refs_0_ = bf16[2,64,512]{2,1,0:T(8,128)(2,1)S(1)} collective-permute-done((bf16[2,64,512]{2,1,0:T(8,128)(2,1)S(1)}, bf16[2,64,512]{2,1,0:T(8,128)(2,1)S(1)}, u32[]{:S(2)}, u32[]{:S(2)}) %collective-permute-start.19) | collective-permute-done | bytes 131104 | tf_op jit(solution)/shard_map/ppermute | solution.py:230
  21.4 3.4 %collective-permute-start.9 = (bf16[8,64,512]{2,1,0:T(8,128)(2,1)S(1)}, bf16[8,64,512]{2,1,0:T(8,128)(2,1)S(1)}, u32[]{:S(2)}, u32[]{:S(2)}) collective-permute-start(bf16[8,64,512]{2,1,0:T(8,128)(2,1)S(1)} %get-tuple-element.51), channel_id=1, source_target_pairs={{0,248},{1,249},{2,250},{3,251},{4,252},{5,253},{6,254},{7,255},{8... | collective-permute-start | bytes 1572872 | tf_op jit(solution)/shard_map/ppermute | solution.py:230
  24.8 2.9 %collective-permute-start.10 = (bf16[8,64,512]{2,1,0:T(8,128)(2,1)S(1)}, bf16[8,64,512]{2,1,0:T(8,128)(2,1)S(1)}, u32[]{:S(2)}, u32[]{:S(2)}) collective-permute-start(bf16[8,64,512]{2,1,0:T(8,128)(2,1)S(1)} %get-tuple-element.51), channel_id=1, source_target_pairs={{0,254},{1,255},{2,248},{3,249},{4,250},{5,251},{6,252},{7,253},{8... | collective-permute-start | bytes 1572872 | tf_op jit(solution)/shard_map/ppermute | solution.py:230
  27.7 2.0 %collective-permute-done.21.refs_1_ = bf16[2,64,512]{2,1,0:T(8,128)(2,1)S(1)} collective-permute-done((bf16[2,64,512]{2,1,0:T(8,128)(2,1)S(1)}, bf16[2,64,512]{2,1,0:T(8,128)(2,1)S(1)}, u32[]{:S(2)}, u32[]{:S(2)}) %collective-permute-start.21) | collective-permute-done | bytes 131104 | tf_op jit(solution)/shard_map/ppermute | solution.py:230
  29.7 2.8 %collective-permute-start.12 = (bf16[8,64,512]{2,1,0:T(8,128)(2,1)S(1)}, bf16[8,64,512]{2,1,0:T(8,128)(2,1)S(1)}, u32[]{:S(2)}, u32[]{:S(2)}) collective-permute-start(bf16[8,64,512]{2,1,0:T(8,128)(2,1)S(1)} %get-tuple-element.50), channel_id=1, source_target_pairs={{0,8},{1,9},{2,10},{3,11},{4,12},{5,13},{6,14},{7,15},{8,16},{9,17... | collective-permute-start | bytes 1572872 | tf_op jit(solution)/shard_map/ppermute | solution.py:230
  33.8 12.4 %collective-permute-done.25.refs_3_ = bf16[2,64,512]{2,1,0:T(8,128)(2,1)S(1)} collective-permute-done((bf16[2,64,512]{2,1,0:T(8,128)(2,1)S(1)}, bf16[2,64,512]{2,1,0:T(8,128)(2,1)S(1)}, u32[]{:S(2)}, u32[]{:S(2)}) %collective-permute-start.25) | collective-permute-done | bytes 131104 | tf_op jit(solution)/shard_map/ppermute | solution.py:230
  46.2 3.0 %collective-permute-done.9.refs_0_ = bf16[8,64,512]{2,1,0:T(8,128)(2,1)S(1)} collective-permute-done((bf16[8,64,512]{2,1,0:T(8,128)(2,1)S(1)}, bf16[8,64,512]{2,1,0:T(8,128)(2,1)S(1)}, u32[]{:S(2)}, u32[]{:S(2)}) %collective-permute-start.9) | collective-permute-done | bytes 524320 | tf_op jit(solution)/shard_map/ppermute | solution.py:230
  50.5 10.0 %collective-permute-done.10.refs_1_.a1 = bf16[8,64,512]{2,1,0:T(8,128)(2,1)S(1)} collective-permute-done((bf16[8,64,512]{2,1,0:T(8,128)(2,1)S(1)}, bf16[8,64,512]{2,1,0:T(8,128)(2,1)S(1)}, u32[]{:S(2)}, u32[]{:S(2)}) %collective-permute-start.10) | collective-permute-done | bytes 524320 | tf_op jit(solution)/shard_map/ppermute | solution.py:230
  62.0 3.2 %collective-permute-done.13.refs_1_.a2 = bf16[8,64,512]{2,1,0:T(8,128)(2,1)S(1)} collective-permute-done((bf16[8,64,512]{2,1,0:T(8,128)(2,1)S(1)}, bf16[8,64,512]{2,1,0:T(8,128)(2,1)S(1)}, u32[]{:S(2)}, u32[]{:S(2)}) %collective-permute-start.13) | collective-permute-done | bytes 524320 | tf_op jit(solution)/shard_map/ppermute | solution.py:230
  65.2 4.3 %collective-permute-start.14 = (bf16[8,64,512]{2,1,0:T(8,128)(2,1)S(1)}, bf16[8,64,512]{2,1,0:T(8,128)(2,1)S(1)}, u32[]{:S(2)}, u32[]{:S(2)}) collective-permute-start(bf16[8,64,512]{2,1,0:T(8,128)(2,1)S(1)} %collective-permute-done.12.refs_0_), channel_id=1, source_target_pairs={{0,6},{1,7},{2,0},{3,1},{4,2},{5,3},{6,4},{7,5},{8,14},{9,15},{10,... | collective-permute-start | bytes 1572872 | tf_op jit(solution)/shard_map/ppermute | solution.py:230
  69.5 27.4 %collective-permute-start = (bf16[4,64,512]{2,1,0:T(8,128)(2,1)S(1)}, bf16[4,64,512]{2,1,0:T(8,128)(2,1)S(1)}, u32[]{:S(2)}, u32[]{:S(2)}) collective-permute-start(bf16[4,64,512]{2,1,0:T(8,128)(2,1)S(1)} %get-tuple-element.53.refs_0_), channel_id=1, source_target_pairs={{0,2},{1,3},{2,4},{3,5},{4,6},{5,7},{6,0},{7,1},{8,10},{9,11},{10,... | collective-permute-start | bytes 786440 | tf_op jit(solution)/shard_map/ppermute | solution.py:230
  97.1 19.5 %collective-permute-done.14.refs_2_.b2 = bf16[8,64,512]{2,1,0:T(8,128)(2,1)S(1)} collective-permute-done((bf16[8,64,512]{2,1,0:T(8,128)(2,1)S(1)}, bf16[8,64,512]{2,1,0:T(8,128)(2,1)S(1)}, u32[]{:S(2)}, u32[]{:S(2)}) %collective-permute-start.14) | collective-permute-done | bytes 524320 | tf_op jit(solution)/shard_map/ppermute | solution.py:230
  116.7 5.6 %collective-permute-done.refs_2_ = bf16[4,64,512]{2,1,0:T(8,128)(2,1)S(1)} collective-permute-done((bf16[4,64,512]{2,1,0:T(8,128)(2,1)S(1)}, bf16[4,64,512]{2,1,0:T(8,128)(2,1)S(1)}, u32[]{:S(2)}, u32[]{:S(2)}) %collective-permute-start) | collective-permute-done | bytes 262176 | tf_op jit(solution)/shard_map/ppermute | solution.py:230
  122.4 6.1 %collective-permute-start.15 = (bf16[8,64,512]{2,1,0:T(8,128)(2,1)S(1)}, bf16[8,64,512]{2,1,0:T(8,128)(2,1)S(1)}, u32[]{:S(2)}, u32[]{:S(2)}) collective-permute-start(bf16[8,64,512]{2,1,0:T(8,128)(2,1)S(1)} %get-tuple-element.30), channel_id=1, source_target_pairs={{0,2},{1,3},{2,4},{3,5},{4,6},{5,7},{6,0},{7,1},{8,10},{9,11},{10,... | collective-permute-start | bytes 1572872 | tf_op jit(solution)/shard_map/ppermute | solution.py:230
  129.3 4.1 %collective-permute-start.1 = (bf16[4,64,512]{2,1,0:T(8,128)(2,1)S(1)}, bf16[4,64,512]{2,1,0:T(8,128)(2,1)S(1)}, u32[]{:S(2)}, u32[]{:S(2)}) collective-permute-start(bf16[4,64,512]{2,1,0:T(8,128)(2,1)S(1)} %get-tuple-element.52.refs_1_), channel_id=1, source_target_pairs={{0,2},{1,3},{2,4},{3,5},{4,6},{5,7},{6,0},{7,1},{8,10},{9,11},{10,... | collective-permute-start | bytes 786440 | tf_op jit(solution)/shard_map/ppermute | solution.py:230
  133.5 8.7 %collective-permute-done.15.refs_2_ = bf16[8,64,512]{2,1,0:T(8,128)(2,1)S(1)} collective-permute-done((bf16[8,64,512]{2,1,0:T(8,128)(2,1)S(1)}, bf16[8,64,512]{2,1,0:T(8,128)(2,1)S(1)}, u32[]{:S(2)}, u32[]{:S(2)}) %collective-permute-start.15) | collective-permute-done | bytes 524320 | tf_op jit(solution)/shard_map/ppermute | solution.py:230
  142.2 3.8 %collective-permute-start.2 = (bf16[4,64,512]{2,1,0:T(8,128)(2,1)S(1)}, bf16[4,64,512]{2,1,0:T(8,128)(2,1)S(1)}, u32[]{:S(2)}, u32[]{:S(2)}) collective-permute-start(bf16[4,64,512]{2,1,0:T(8,128)(2,1)S(1)} %get-tuple-element.53.refs_0_), channel_id=1, source_target_pairs={{0,6},{1,7},{2,0},{3,1},{4,2},{5,3},{6,4},{7,5},{8,14},{9,15},{10,... | collective-permute-start | bytes 786440 | tf_op jit(solution)/shard_map/ppermute | solution.py:230
  147.5 3.1 %collective-permute-start.5 = (bf16[4,64,512]{2,1,0:T(8,128)(2,1)S(1)}, bf16[4,64,512]{2,1,0:T(8,128)(2,1)S(1)}, u32[]{:S(2)}, u32[]{:S(2)}) collective-permute-start(bf16[4,64,512]{2,1,0:T(8,128)(2,1)S(1)} %collective-permute-done.refs_2_), channel_id=1, source_target_pairs={{0,2},{1,3},{2,4},{3,5},{4,6},{5,7},{6,0},{7,1},{8,10},{9,11},{10,... | collective-permute-start | bytes 786440 | tf_op jit(solution)/shard_map/ppermute | solution.py:230
  151.7 1.8 shard_map.49.refs_0_
  153.5 1.8 shard_map.50.refs_1_
  155.3 2.9 %shard_map.54 = (f32[4,16,8,64]{3,2,1,0:T(8,128)S(1)}, f32[4,16,8,64]{3,2,1,0:T(8,128)S(1)}) custom-call(f32[2,512,512]{2,1,0:T(8,128)S(1)} %shard_map.49.refs_0_, f32[2,512,512]{2,1,0:T(8,128)S(1)} %shard_map.50.refs_1_, bf16[8,64,512]{2,1,0:T(8,128)(2,1)S(1)} %collective-permute-done.15.refs_2_, bf16[8,64,512]{2,1,0:T(8,128)(2,1)S(1)} %collective-permute-done.16.refs_3_, ...), custom_call_target="tpu_custom_call" | custom-call | tf_op jit(solution)/shard_map/pallas_call | solution.py:237
  158.4 1.8 shard_map.47.refs_0_
  163.5 2.0 %collective-permute-start.29 = (f32[24,8,64]{2,1,0:T(8,128)S(1)}, f32[24,8,64]{2,1,0:T(8,128)S(1)}, u32[]{:S(2)}, u32[]{:S(2)}) collective-permute-start(f32[24,8,64]{2,1,0:T(8,128)S(1)} %get-tuple-element.41), channel_id=1, source_target_pairs={{0,2},{1,3},{2,4},{3,5},{4,6},{5,7},{6,0},{7,1},{8,10},{9,11},{10,... | collective-permute-start | bytes 147464 | tf_op jit(solution)/shard_map/ppermute | solution.py:230
  165.4 2.2 %collective-permute-start.30 = (f32[24,8,64]{2,1,0:T(8,128)S(1)}, f32[24,8,64]{2,1,0:T(8,128)S(1)}, u32[]{:S(2)}, u32[]{:S(2)}) collective-permute-start(f32[24,8,64]{2,1,0:T(8,128)S(1)} %get-tuple-element.42), channel_id=1, source_target_pairs={{0,6},{1,7},{2,0},{3,1},{4,2},{5,3},{6,4},{7,5},{8,14},{9,15},{10,... | collective-permute-start | bytes 147464 | tf_op jit(solution)/shard_map/ppermute | solution.py:230
  167.7 3.5 %collective-permute-start.31 = (f32[24,8,64]{2,1,0:T(8,128)S(1)}, f32[24,8,64]{2,1,0:T(8,128)S(1)}, u32[]{:S(2)}, u32[]{:S(2)}) collective-permute-start(f32[24,8,64]{2,1,0:T(8,128)S(1)} %get-tuple-element.43), channel_id=1, source_target_pairs={{0,4},{1,5},{2,6},{3,7},{4,0},{5,1},{6,2},{7,3},{8,12},{9,13},{10,... | collective-permute-start | bytes 147464 | tf_op jit(solution)/shard_map/ppermute | solution.py:230
  171.5 6.7 %collective-permute-done.31.d = f32[24,8,64]{2,1,0:T(8,128)S(1)} collective-permute-done((f32[24,8,64]{2,1,0:T(8,128)S(1)}, f32[24,8,64]{2,1,0:T(8,128)S(1)}, u32[]{:S(2)}, u32[]{:S(2)}) %collective-permute-start.31) | collective-permute-done | bytes 49184 | tf_op jit(solution)/shard_map/ppermute | solution.py:230
  178.2 6.9 %collective-permute-start.33 = (f32[8,8,64]{2,1,0:T(8,128)S(1)}, f32[8,8,64]{2,1,0:T(8,128)S(1)}, u32[]{:S(2)}, u32[]{:S(2)}) collective-permute-start(f32[8,8,64]{2,1,0:T(8,128)S(1)} %get-tuple-element.46), channel_id=1, source_target_pairs={{0,248},{1,249},{2,250},{3,251},{4,252},{5,253},{6,254},{7,255},{8... | collective-permute-start | bytes 49160 | tf_op jit(solution)/shard_map/ppermute | solution.py:230
  186.7 6.5 %collective-permute-done.32 = f32[8,8,64]{2,1,0:T(8,128)S(1)} collective-permute-done((f32[8,8,64]{2,1,0:T(8,128)S(1)}, f32[8,8,64]{2,1,0:T(8,128)S(1)}, u32[]{:S(2)}, u32[]{:S(2)}) %collective-permute-start.32) | collective-permute-done | bytes 16416 | tf_op jit(solution)/shard_map/ppermute | solution.py:230
  (57 shorter events, 19.3 us)
Async XLA Ops:
  1.7 14.3 %collective-permute-start.20 = (bf16[2,64,512]{2,1,0:T(8,128)(2,1)S(1)}, bf16[2,64,512]{2,1,0:T(8,128)(2,1)S(1)}, u32[]{:S(2)}, u32[]{:S(2)}) collective-permute-start(bf16[2,64,512]{2,1,0:T(8,128)(2,1)S(1)} %get-tuple-element.33), channel_id=1, source_target_pairs={{0,8},{1,9},{2,10},{3,11},{4,12},{5,13},{6,14},{7,15},{120,112},{1... | collective-permute-start | bytes 393224 | tf_op jit(solution)/shard_map/ppermute | solution.py:230
  5.3 11.9 %collective-permute-start.22 = (bf16[2,64,512]{2,1,0:T(8,128)(2,1)S(1)}, bf16[2,64,512]{2,1,0:T(8,128)(2,1)S(1)}, u32[]{:S(2)}, u32[]{:S(2)}) collective-permute-start(bf16[2,64,512]{2,1,0:T(8,128)(2,1)S(1)} %get-tuple-element.34), channel_id=1, source_target_pairs={{0,96},{1,97},{2,98},{3,99},{4,100},{5,101},{6,102},{7,103},{120,2... | collective-permute-start | bytes 393224 | tf_op jit(solution)/shard_map/ppermute | solution.py:230
  9.3 141.3 %collective-permute-start.4 = (bf16[512,2048]{1,0:T(8,128)(2,1)S(1)}, bf16[512,2048]{1,0:T(8,128)(2,1)S(1)}, u32[]{:S(2)}, u32[]{:S(2)}) collective-permute-start(bf16[512,2048]{1,0:T(8,128)(2,1)S(1)} %get-tuple-element.27), channel_id=1, source_target_pairs={{0,1},{1,0},{2,3},{3,2},{4,5},{5,4},{6,7},{7,6},{8,9},{9,8},{10,11... | collective-permute-start | bytes 6291464 | tf_op jit(solution)/shard_map/ppermute | solution.py:230
  9.4 12.0 %collective-permute-start.19 = (bf16[2,64,512]{2,1,0:T(8,128)(2,1)S(1)}, bf16[2,64,512]{2,1,0:T(8,128)(2,1)S(1)}, u32[]{:S(2)}, u32[]{:S(2)}) collective-permute-start(bf16[2,64,512]{2,1,0:T(8,128)(2,1)S(1)} %get-tuple-element.32), channel_id=1, source_target_pairs={{0,248},{1,249},{2,250},{3,251},{4,252},{5,253},{6,254},{7,255},{1... | collective-permute-start | bytes 393224 | tf_op jit(solution)/shard_map/ppermute | solution.py:230
  14.7 10.1 %collective-permute-start.24 = (bf16[2,64,512]{2,1,0:T(8,128)(2,1)S(1)}, bf16[2,64,512]{2,1,0:T(8,128)(2,1)S(1)}, u32[]{:S(2)}, u32[]{:S(2)}) collective-permute-start(bf16[2,64,512]{2,1,0:T(8,128)(2,1)S(1)} %get-tuple-element.35), channel_id=1, source_target_pairs={{0,32},{1,33},{2,34},{3,35},{4,36},{5,37},{6,38},{7,39},{120,88},{... | collective-permute-start | bytes 393224 | tf_op jit(solution)/shard_map/ppermute | solution.py:230
  16.0 13.7 %collective-permute-start.21 = (bf16[2,64,512]{2,1,0:T(8,128)(2,1)S(1)}, bf16[2,64,512]{2,1,0:T(8,128)(2,1)S(1)}, u32[]{:S(2)}, u32[]{:S(2)}) collective-permute-start(bf16[2,64,512]{2,1,0:T(8,128)(2,1)S(1)} %collective-permute-done.20), channel_id=1, source_target_pairs={{8,248},{9,249},{10,250},{11,251},{12,252},{13,253},{14,254},{15,2... | collective-permute-start | bytes 393224 | tf_op jit(solution)/shard_map/ppermute | solution.py:230
  17.3 15.2 %collective-permute-start.23 = (bf16[2,64,512]{2,1,0:T(8,128)(2,1)S(1)}, bf16[2,64,512]{2,1,0:T(8,128)(2,1)S(1)}, u32[]{:S(2)}, u32[]{:S(2)}) collective-permute-start(bf16[2,64,512]{2,1,0:T(8,128)(2,1)S(1)} %collective-permute-done.22), channel_id=1, source_target_pairs={{24,128},{25,129},{26,130},{27,131},{28,132},{29,133},{30,134},{31... | collective-permute-start | bytes 393224 | tf_op jit(solution)/shard_map/ppermute | solution.py:230
  21.4 27.9 %collective-permute-start.9 = (bf16[8,64,512]{2,1,0:T(8,128)(2,1)S(1)}, bf16[8,64,512]{2,1,0:T(8,128)(2,1)S(1)}, u32[]{:S(2)}, u32[]{:S(2)}) collective-permute-start(bf16[8,64,512]{2,1,0:T(8,128)(2,1)S(1)} %get-tuple-element.51), channel_id=1, source_target_pairs={{0,248},{1,249},{2,250},{3,251},{4,252},{5,253},{6,254},{7,255},{8... | collective-permute-start | bytes 1572872 | tf_op jit(solution)/shard_map/ppermute | solution.py:230
  24.8 35.8 %collective-permute-start.10 = (bf16[8,64,512]{2,1,0:T(8,128)(2,1)S(1)}, bf16[8,64,512]{2,1,0:T(8,128)(2,1)S(1)}, u32[]{:S(2)}, u32[]{:S(2)}) collective-permute-start(bf16[8,64,512]{2,1,0:T(8,128)(2,1)S(1)} %get-tuple-element.51), channel_id=1, source_target_pairs={{0,254},{1,255},{2,248},{3,249},{4,250},{5,251},{6,252},{7,253},{8... | collective-permute-start | bytes 1572872 | tf_op jit(solution)/shard_map/ppermute | solution.py:230
  29.7 32.2 %collective-permute-start.12 = (bf16[8,64,512]{2,1,0:T(8,128)(2,1)S(1)}, bf16[8,64,512]{2,1,0:T(8,128)(2,1)S(1)}, u32[]{:S(2)}, u32[]{:S(2)}) collective-permute-start(bf16[8,64,512]{2,1,0:T(8,128)(2,1)S(1)} %get-tuple-element.50), channel_id=1, source_target_pairs={{0,8},{1,9},{2,10},{3,11},{4,12},{5,13},{6,14},{7,15},{8,16},{9,17... | collective-permute-start | bytes 1572872 | tf_op jit(solution)/shard_map/ppermute | solution.py:230
  32.5 13.7 %collective-permute-start.25 = (bf16[2,64,512]{2,1,0:T(8,128)(2,1)S(1)}, bf16[2,64,512]{2,1,0:T(8,128)(2,1)S(1)}, u32[]{:S(2)}, u32[]{:S(2)}) collective-permute-start(bf16[2,64,512]{2,1,0:T(8,128)(2,1)S(1)} %collective-permute-done.24), channel_id=1, source_target_pairs={{32,248},{33,249},{34,250},{35,251},{36,252},{37,253},{38,254},{39... | collective-permute-start | bytes 393224 | tf_op jit(solution)/shard_map/ppermute | solution.py:230
  46.2 19.0 %collective-permute-start.13 = (bf16[8,64,512]{2,1,0:T(8,128)(2,1)S(1)}, bf16[8,64,512]{2,1,0:T(8,128)(2,1)S(1)}, u32[]{:S(2)}, u32[]{:S(2)}) collective-permute-start(bf16[8,64,512]{2,1,0:T(8,128)(2,1)S(1)} %get-tuple-element.50), channel_id=1, source_target_pairs={{0,10},{1,11},{2,12},{3,13},{4,14},{5,15},{6,8},{7,9},{8,18},{9,19... | collective-permute-start | bytes 1572872 | tf_op jit(solution)/shard_map/ppermute | solution.py:230
  49.2 20.2 %collective-permute-start.17 = (bf16[8,64,512]{2,1,0:T(8,128)(2,1)S(1)}, bf16[8,64,512]{2,1,0:T(8,128)(2,1)S(1)}, u32[]{:S(2)}, u32[]{:S(2)}) collective-permute-start(bf16[8,64,512]{2,1,0:T(8,128)(2,1)S(1)} %get-tuple-element.49.c1), channel_id=1, source_target_pairs={{8,0},{9,1},{10,2},{11,3},{12,4},{13,5},{14,6},{15,7},{16,8},{17,9... | collective-permute-start | bytes 1572872 | tf_op jit(solution)/shard_map/ppermute | solution.py:230
  60.6 36.3 %collective-permute-start.18 = (bf16[8,64,512]{2,1,0:T(8,128)(2,1)S(1)}, bf16[8,64,512]{2,1,0:T(8,128)(2,1)S(1)}, u32[]{:S(2)}, u32[]{:S(2)}) collective-permute-start(bf16[8,64,512]{2,1,0:T(8,128)(2,1)S(1)} %get-tuple-element.47.c2), channel_id=1, source_target_pairs={{0,8},{1,9},{2,10},{3,11},{4,12},{5,13},{6,14},{7,15},{8,16},{9,17... | collective-permute-start | bytes 1572872 | tf_op jit(solution)/shard_map/ppermute | solution.py:230
  61.9 35.1 %collective-permute-start.11 = (bf16[8,64,512]{2,1,0:T(8,128)(2,1)S(1)}, bf16[8,64,512]{2,1,0:T(8,128)(2,1)S(1)}, u32[]{:S(2)}, u32[]{:S(2)}) collective-permute-start(bf16[8,64,512]{2,1,0:T(8,128)(2,1)S(1)} %collective-permute-done.9.refs_0_), channel_id=1, source_target_pairs={{0,6},{1,7},{2,0},{3,1},{4,2},{5,3},{6,4},{7,5},{8,14},{9,15},{10,... | collective-permute-start | bytes 1572872 | tf_op jit(solution)/shard_map/ppermute | solution.py:230
  65.2 51.5 %collective-permute-start.14 = (bf16[8,64,512]{2,1,0:T(8,128)(2,1)S(1)}, bf16[8,64,512]{2,1,0:T(8,128)(2,1)S(1)}, u32[]{:S(2)}, u32[]{:S(2)}) collective-permute-start(bf16[8,64,512]{2,1,0:T(8,128)(2,1)S(1)} %collective-permute-done.12.refs_0_), channel_id=1, source_target_pairs={{0,6},{1,7},{2,0},{3,1},{4,2},{5,3},{6,4},{7,5},{8,14},{9,15},{10,... | collective-permute-start | bytes 1572872 | tf_op jit(solution)/shard_map/ppermute | solution.py:230
  69.5 52.9 %collective-permute-start = (bf16[4,64,512]{2,1,0:T(8,128)(2,1)S(1)}, bf16[4,64,512]{2,1,0:T(8,128)(2,1)S(1)}, u32[]{:S(2)}, u32[]{:S(2)}) collective-permute-start(bf16[4,64,512]{2,1,0:T(8,128)(2,1)S(1)} %get-tuple-element.53.refs_0_), channel_id=1, source_target_pairs={{0,2},{1,3},{2,4},{3,5},{4,6},{5,7},{6,0},{7,1},{8,10},{9,11},{10,... | collective-permute-start | bytes 786440 | tf_op jit(solution)/shard_map/ppermute | solution.py:230
  96.9 31.6 %collective-permute-start.3 = (bf16[4,64,512]{2,1,0:T(8,128)(2,1)S(1)}, bf16[4,64,512]{2,1,0:T(8,128)(2,1)S(1)}, u32[]{:S(2)}, u32[]{:S(2)}) collective-permute-start(bf16[4,64,512]{2,1,0:T(8,128)(2,1)S(1)} %get-tuple-element.52.refs_1_), channel_id=1, source_target_pairs={{0,6},{1,7},{2,0},{3,1},{4,2},{5,3},{6,4},{7,5},{8,14},{9,15},{10,... | collective-permute-start | bytes 786440 | tf_op jit(solution)/shard_map/ppermute | solution.py:230
  97.0 32.3 %collective-permute-start.26 = (bf16[8,64,512]{2,1,0:T(8,128)(2,1)S(1)}, bf16[8,64,512]{2,1,0:T(8,128)(2,1)S(1)}, u32[]{:S(2)}, u32[]{:S(2)}) collective-permute-start(bf16[8,64,512]{2,1,0:T(8,128)(2,1)S(1)} %get-tuple-element.36.refs_6_), channel_id=1, source_target_pairs={{0,1},{1,0},{2,3},{3,2},{4,5},{5,4},{6,7},{7,6},{8,9},{9,8},{10,11... | collective-permute-start | bytes 1572872 | tf_op jit(solution)/shard_map/ppermute | solution.py:230
  116.6 12.7 %collective-permute-start.27 = (bf16[8,64,512]{2,1,0:T(8,128)(2,1)S(1)}, bf16[8,64,512]{2,1,0:T(8,128)(2,1)S(1)}, u32[]{:S(2)}, u32[]{:S(2)}) collective-permute-start(bf16[8,64,512]{2,1,0:T(8,128)(2,1)S(1)} %get-tuple-element.37.refs_8_), channel_id=1, source_target_pairs={{0,1},{1,0},{2,3},{3,2},{4,5},{5,4},{6,7},{7,6},{8,9},{9,8},{10,11... | collective-permute-start | bytes 1572872 | tf_op jit(solution)/shard_map/ppermute | solution.py:230
  122.4 19.8 %collective-permute-start.15 = (bf16[8,64,512]{2,1,0:T(8,128)(2,1)S(1)}, bf16[8,64,512]{2,1,0:T(8,128)(2,1)S(1)}, u32[]{:S(2)}, u32[]{:S(2)}) collective-permute-start(bf16[8,64,512]{2,1,0:T(8,128)(2,1)S(1)} %get-tuple-element.30), channel_id=1, source_target_pairs={{0,2},{1,3},{2,4},{3,5},{4,6},{5,7},{6,0},{7,1},{8,10},{9,11},{10,... | collective-permute-start | bytes 1572872 | tf_op jit(solution)/shard_map/ppermute | solution.py:230
  128.5 19.0 %collective-permute-start.16 = (bf16[8,64,512]{2,1,0:T(8,128)(2,1)S(1)}, bf16[8,64,512]{2,1,0:T(8,128)(2,1)S(1)}, u32[]{:S(2)}, u32[]{:S(2)}) collective-permute-start(bf16[8,64,512]{2,1,0:T(8,128)(2,1)S(1)} %get-tuple-element.31), channel_id=1, source_target_pairs={{0,6},{1,7},{2,0},{3,1},{4,2},{5,3},{6,4},{7,5},{8,14},{9,15},{10,... | collective-permute-start | bytes 1572872 | tf_op jit(solution)/shard_map/ppermute | solution.py:230
  129.3 30.9 %collective-permute-start.7 = (bf16[8,64,512]{2,1,0:T(8,128)(2,1)S(1)}, bf16[8,64,512]{2,1,0:T(8,128)(2,1)S(1)}, u32[]{:S(2)}, u32[]{:S(2)}) collective-permute-start(bf16[8,64,512]{2,1,0:T(8,128)(2,1)S(1)} %get-tuple-element.48.refs_5_), channel_id=1, source_target_pairs={{0,1},{1,0},{2,3},{3,2},{4,5},{5,4},{6,7},{7,6},{8,9},{9,8},{10,11... | collective-permute-start | bytes 1572872 | tf_op jit(solution)/shard_map/ppermute | solution.py:230
  129.3 28.9 %collective-permute-start.1 = (bf16[4,64,512]{2,1,0:T(8,128)(2,1)S(1)}, bf16[4,64,512]{2,1,0:T(8,128)(2,1)S(1)}, u32[]{:S(2)}, u32[]{:S(2)}) collective-permute-start(bf16[4,64,512]{2,1,0:T(8,128)(2,1)S(1)} %get-tuple-element.52.refs_1_), channel_id=1, source_target_pairs={{0,2},{1,3},{2,4},{3,5},{4,6},{5,7},{6,0},{7,1},{8,10},{9,11},{10,... | collective-permute-start | bytes 786440 | tf_op jit(solution)/shard_map/ppermute | solution.py:230
  142.2 16.2 %collective-permute-start.2 = (bf16[4,64,512]{2,1,0:T(8,128)(2,1)S(1)}, bf16[4,64,512]{2,1,0:T(8,128)(2,1)S(1)}, u32[]{:S(2)}, u32[]{:S(2)}) collective-permute-start(bf16[4,64,512]{2,1,0:T(8,128)(2,1)S(1)} %get-tuple-element.53.refs_0_), channel_id=1, source_target_pairs={{0,6},{1,7},{2,0},{3,1},{4,2},{5,3},{6,4},{7,5},{8,14},{9,15},{10,... | collective-permute-start | bytes 786440 | tf_op jit(solution)/shard_map/ppermute | solution.py:230
  147.5 12.7 %collective-permute-start.5 = (bf16[4,64,512]{2,1,0:T(8,128)(2,1)S(1)}, bf16[4,64,512]{2,1,0:T(8,128)(2,1)S(1)}, u32[]{:S(2)}, u32[]{:S(2)}) collective-permute-start(bf16[4,64,512]{2,1,0:T(8,128)(2,1)S(1)} %collective-permute-done.refs_2_), channel_id=1, source_target_pairs={{0,2},{1,3},{2,4},{3,5},{4,6},{5,7},{6,0},{7,1},{8,10},{9,11},{10,... | collective-permute-start | bytes 786440 | tf_op jit(solution)/shard_map/ppermute | solution.py:230
  150.6 9.6 %collective-permute-start.6 = (bf16[4,64,512]{2,1,0:T(8,128)(2,1)S(1)}, bf16[4,64,512]{2,1,0:T(8,128)(2,1)S(1)}, u32[]{:S(2)}, u32[]{:S(2)}) collective-permute-start(bf16[4,64,512]{2,1,0:T(8,128)(2,1)S(1)} %collective-permute-done.3.refs_5_), channel_id=1, source_target_pairs={{0,6},{1,7},{2,0},{3,1},{4,2},{5,3},{6,4},{7,5},{8,14},{9,15},{10,... | collective-permute-start | bytes 786440 | tf_op jit(solution)/shard_map/ppermute | solution.py:230
  163.5 7.8 %collective-permute-start.29 = (f32[24,8,64]{2,1,0:T(8,128)S(1)}, f32[24,8,64]{2,1,0:T(8,128)S(1)}, u32[]{:S(2)}, u32[]{:S(2)}) collective-permute-start(f32[24,8,64]{2,1,0:T(8,128)S(1)} %get-tuple-element.41), channel_id=1, source_target_pairs={{0,2},{1,3},{2,4},{3,5},{4,6},{5,7},{6,0},{7,1},{8,10},{9,11},{10,... | collective-permute-start | bytes 147464 | tf_op jit(solution)/shard_map/ppermute | solution.py:230
  165.4 6.1 %collective-permute-start.30 = (f32[24,8,64]{2,1,0:T(8,128)S(1)}, f32[24,8,64]{2,1,0:T(8,128)S(1)}, u32[]{:S(2)}, u32[]{:S(2)}) collective-permute-start(f32[24,8,64]{2,1,0:T(8,128)S(1)} %get-tuple-element.42), channel_id=1, source_target_pairs={{0,6},{1,7},{2,0},{3,1},{4,2},{5,3},{6,4},{7,5},{8,14},{9,15},{10,... | collective-permute-start | bytes 147464 | tf_op jit(solution)/shard_map/ppermute | solution.py:230
  167.7 10.5 %collective-permute-start.31 = (f32[24,8,64]{2,1,0:T(8,128)S(1)}, f32[24,8,64]{2,1,0:T(8,128)S(1)}, u32[]{:S(2)}, u32[]{:S(2)}) collective-permute-start(f32[24,8,64]{2,1,0:T(8,128)S(1)} %get-tuple-element.43), channel_id=1, source_target_pairs={{0,4},{1,5},{2,6},{3,7},{4,0},{5,1},{6,2},{7,3},{8,12},{9,13},{10,... | collective-permute-start | bytes 147464 | tf_op jit(solution)/shard_map/ppermute | solution.py:230
  178.2 8.5 %collective-permute-start.33 = (f32[8,8,64]{2,1,0:T(8,128)S(1)}, f32[8,8,64]{2,1,0:T(8,128)S(1)}, u32[]{:S(2)}, u32[]{:S(2)}) collective-permute-start(f32[8,8,64]{2,1,0:T(8,128)S(1)} %get-tuple-element.46), channel_id=1, source_target_pairs={{0,248},{1,249},{2,250},{3,251},{4,252},{5,253},{6,254},{7,255},{8... | collective-permute-start | bytes 49160 | tf_op jit(solution)/shard_map/ppermute | solution.py:230
  185.1 8.1 %collective-permute-start.32 = (f32[8,8,64]{2,1,0:T(8,128)S(1)}, f32[8,8,64]{2,1,0:T(8,128)S(1)}, u32[]{:S(2)}, u32[]{:S(2)}) collective-permute-start(f32[8,8,64]{2,1,0:T(8,128)S(1)} %get-tuple-element.45), channel_id=1, source_target_pairs={{0,8},{1,9},{2,10},{3,11},{4,12},{5,13},{6,14},{7,15},{8,16},{9,17... | collective-permute-start | bytes 49160 | tf_op jit(solution)/shard_map/ppermute | solution.py:230
  (5 other events, 32.5 us)

commit v5 on v4

--- a/solution.py
+++ b/solution.py
@@ -129,32 +129,27 @@
     return x.reshape(x.shape[0] * x.shape[1], x.shape[2])
 
 
-def first_kernel(group, owners, quarters, counts, *refs):
-    blocks, (w0, w1, acc) = refs[:-3], refs[-3:]
+def first_kernel(group, owners, quarters, own, ahead, behind, w0, w1, acc):
     owner, quarter, _ = where_am_i()
     rows = acc.shape[2]
     sigma = heading(group, owner, owners)
-    columns = (
-        quarter,
-        lax.rem(quarter - sigma + quarters, quarters),
-        lax.rem(quarter + sigma + quarters, quarters),
+    blocks = (
+        (own, quarter),
+        (ahead, lax.rem(quarter - sigma + quarters, quarters)),
+        (behind, lax.rem(quarter + sigma + quarters, quarters)),
     )
     for s, w in enumerate((w0, w1)):
-        base, size = 0, acc.shape[1]
-        for h in range(counts):
-            total = None
-            for n in range(3):
-                pieces = blocks[n * counts : (n + 1) * counts]
-                at = pl.multiple_of(columns[n] * rows, rows)
-                y = lax.dot_general(
-                    flat(pieces[h]),
-                    w[:, pl.ds(at, rows)],
-                    CONTRACT_LAST,
-                    preferred_element_type=jnp.float32,
-                )
-                total = y if total is None else total + y
-            acc[s, base : base + size // counts] = total
-            base += size // counts
+        total = None
+        for x, column in blocks:
+            at = pl.multiple_of(column * rows, rows)
+            y = lax.dot_general(
+                flat(x),
+                w[:, pl.ds(at, rows)],
+                CONTRACT_LAST,
+                preferred_element_type=jnp.float32,
+            )
+            total = y if total is None else total + y
+        acc[s] = total
 
 
 def last_kernel(groups, quarters, half, *refs):
@@ -196,23 +191,33 @@
                 part = part.reshape(quarters, 2, -1, bands)
                 for j in range(quarters):
                     d = lax.rem(j - quarter + quarters, quarters)
-                    q = g * 2 * half + p
-                    keep_ref[d, q] = jnp.where(even, part[j, 0], part[j, 1])
-                    give_ref[d, q] = jnp.where(even, part[j, 1], part[j, 0])
-
-
-def merge_kernel(keep0, got0, keep, got, *out):
+                    m, lane = g * half + p // 2, (p % 2) * bands
+                    span = slice(lane, lane + bands)
+                    keep_ref[d, m, :, span] = jnp.where(even, part[j, 0], part[j, 1])
+                    give_ref[d, m, :, span] = jnp.where(even, part[j, 1], part[j, 0])
+
+
+def add_kernel(keep, got, *out):
+    size = out[0].shape[1]
+    for g, ref in enumerate(out):
+        span = slice(g * size, (g + 1) * size)
+        ref[...] = keep[:, span] + got[:, span]
+
+
+def merge_kernel(keep0, got0, back1, back2, *out):
     size = keep0.shape[1]
     for d, ref in enumerate(out):
         ref[:size] = keep0[d] + got0[d]
-        ref[size:] = keep[d] + got[d]
-
-
-def total_kernel(a, b, c, d, *out):
-    size = out[0].shape[0]
-    for g, ref in enumerate(out):
-        span = slice(g * size, (g + 1) * size)
-        ref[...] = a[span] + b[span] + c[span] + d[span]
+        ref[size : 2 * size] = back1[d]
+        ref[2 * size :] = back2[d]
+
+
+def total_kernel(a, b, c, d, out):
+    bands = out.shape[2]
+    for m in range(a.shape[0]):
+        x = a[m] + b[m] + c[m] + d[m]
+        out[2 * m] = x[:, :bands]
+        out[2 * m + 1] = x[:, bands:]
 
 
 def shards(pair_conduction, pair_valence, screened, sphere_sizes):
@@ -291,11 +296,9 @@
     )
     for g in (1, 2):
         behind[g] = send(own[g], lambda i, k, c: (i, k - turn(g, i, owners), c))
-    v0 = [v[0][:half], v[0][half:]]
-    up, down = [None, None], [None, None]
-    for n in range(2):
-        up[n] = send(v0[n], lambda i, k, c: (i, k + 1, c))
-        down[1 - n] = send(v0[1 - n], lambda i, k, c: (i, k - 1, c))
+    own[0] = v[0]
+    ahead[0] = send(v[0], lambda i, k, c: (i, k + 1, c))
+    behind[0] = send(v[0], lambda i, k, c: (i, k - 1, c))
     going_up, going_down = call(
         functools.partial(forward_kernel, owners, half),
         [jax.ShapeDtypeStruct(v[0].shape, v[0].dtype)] * 2,
@@ -306,8 +309,8 @@
         send(going_down, lambda i, k, c: (i, k - 1, c)),
     )
     far0 = (
-        send(up[0], lambda i, k, c: (i, k + 1, c)),
-        send(down[1], lambda i, k, c: (i, k - 1, c)),
+        send(ahead[0][:half], lambda i, k, c: (i, k + 1, c)),
+        send(behind[0][half:], lambda i, k, c: (i, k - 1, c)),
     )
 
     block = rows // 4
@@ -322,19 +325,19 @@
     w1 = swap(give)
     c_par = {g: swap(c_own[g]) for g in range(3)}
 
-    def first(g, counts, blocks):
+    def first(g):
         return call(
-            functools.partial(first_kernel, g, owners, quarters, counts),
+            functools.partial(first_kernel, g, owners, quarters),
             jax.ShapeDtypeStruct((2, group_size * bands, rows), jnp.float32),
-            (*blocks, w0, w1),
+            (own[g], ahead[g], behind[g], w0, w1),
         )
 
     def last(groups, accs, far):
         shape = (
             quarters,
-            len(groups) * group_size,
+            len(groups) * half,
             cbands // quarters // 2,
-            bands,
+            2 * bands,
         )
         conduction = [x[g] for g in groups for x in (c_own, c_par)]
         return call(
@@ -343,20 +346,31 @@
             (*accs, *far, w0, w1, *conduction),
         )
 
-    accs = [first(g, 1, (own[g], ahead[g], behind[g])) for g in (1, 2)]
+    accs = [first(g) for g in (1, 2)]
     keep, give = last((1, 2), accs, far)
-    got = swap(give)
-    acc = first(0, 2, (*v0, *up, *down))
+    packed = (quarters, half, *keep.shape[2:])
+    back = list(
+        call(
+            add_kernel,
+            [jax.ShapeDtypeStruct(packed, jnp.float32)] * 2,
+            (keep, swap(give)),
+        )
+    )
+    for g in (1, 2):
+        back[g - 1] = send(back[g - 1], lambda i, k, c: (i - shift[g], k, c))
+    acc = first(0)
     keep0, give0 = last((0,), [acc], far0)
-    got0 = swap(give0)
-    block_shape = jax.ShapeDtypeStruct((3 * group_size, *keep.shape[2:]), jnp.float32)
-    blocks = call(merge_kernel, [block_shape] * quarters, (keep0, got0, keep, got))
+    blocks = call(
+        merge_kernel,
+        [jax.ShapeDtypeStruct((3 * half, *packed[2:]), jnp.float32)] * quarters,
+        (keep0, swap(give0), *back),
+    )
     others = [send(blocks[d], lambda i, k, c: (i, k + d, c)) for d in (1, 3, 2)]
-    group_shape = jax.ShapeDtypeStruct((group_size, *keep.shape[2:]), jnp.float32)
-    results = list(call(total_kernel, [group_shape] * 3, (blocks[0], *others)))
-    for g in (1, 2):
-        results[g] = send(results[g], lambda i, k, c: (i - shift[g], k, c))
-    return jnp.concatenate(results, 0)
+    return call(
+        total_kernel,
+        jax.ShapeDtypeStruct((3 * group_size, packed[2], bands), jnp.float32),
+        (blocks[0], *others),
+    )
 
 
 def solution(mesh):

time: 194 us -> 185 us (0.954)
  the two profiles are of different devices: /device:TPU:32 before, /device:TPU:62 now
where the time goes in v5:
time: 185 us
  starting transfers between devices  122 us (66%)
  waiting for transfers between devices  45.9 us (25%)
  Pallas kernels  13.1 us (7%)
  local copies, waits for them, and re-layouts  3.18 us (2%)
    ppermute x32, starting transfers between devices, send(): return lax.ppermute(x, AXES, moves(owners, quarters, target))  122 us
    ppermute x32, waiting for transfers between devices, send(): return lax.ppermute(x, AXES, moves(owners, quarters, target))  45.9 us
    pallas_call x12, Pallas kernels, call(): pl.pallas_call(body, in_specs=in_specs or [VMEM] * len(operands), out_spe...  13.1 us
  transfers between devices with their start and end apart: 32, of which 10 were waited for; matrix products, arithmetic and copies ran while one was open for 0% of the time, Pallas kernels for 6%

profile of v5, /device:TPU:62, one launch (start us, length us, event | category | flops | bytes accessed | tf_op | source)
XLA Modules:
  0.0 184.7 jit_solution(846854531906931057)
XLA Ops:
  0.0 2.2 %copy-done = bf16[1,512,4096]{2,1,0:T(8,128)(2,1)S(1)} copy-done((bf16[1,512,4096]{2,1,0:T(8,128)(2,1)S(1)}, bf16[1,512,4096]{2,1,0:T(8,128)(2,1)}, u32[]{:S(2)}) %copy-start) | copy-done | bytes 4194328
  2.8 2.0 %shard_map.46 = (bf16[512,2048]{1,0:T(8,128)(2,1)S(1)}, bf16[512,2048]{1,0:T(8,128)(2,1)S(1)}) custom-call(s32[32]{0:T(128)S(1)} %copy-done.1, bf16[512,4096]{1,0:T(8,128)(2,1)S(1)} %bitcast.1), custom_call_target="tpu_custom_call" | custom-call | tf_op jit(solution)/shard_map/pallas_call | solution.py:242
  5.2 3.4 %collective-permute-start.17 = (bf16[2,64,512]{2,1,0:T(8,128)(2,1)S(1)}, bf16[2,64,512]{2,1,0:T(8,128)(2,1)S(1)}, u32[]{:S(2)}, u32[]{:S(2)}) collective-permute-start(bf16[2,64,512]{2,1,0:T(8,128)(2,1)S(1)} %get-tuple-element.31), channel_id=1, source_target_pairs={{0,248},{1,249},{2,250},{3,251},{4,252},{5,253},{6,254},{7,255},{1... | collective-permute-start | bytes 393224 | tf_op jit(solution)/shard_map/ppermute | solution.py:235
  8.7 1.3 collective-permute-start.18
  10.0 1.3 collective-permute-start.20
  11.3 1.3 collective-permute-start.22
  14.5 2.8 %collective-permute-done.17.refs_0_ = bf16[2,64,512]{2,1,0:T(8,128)(2,1)S(1)} collective-permute-done((bf16[2,64,512]{2,1,0:T(8,128)(2,1)S(1)}, bf16[2,64,512]{2,1,0:T(8,128)(2,1)S(1)}, u32[]{:S(2)}, u32[]{:S(2)}) %collective-permute-start.17) | collective-permute-done | bytes 131104 | tf_op jit(solution)/shard_map/ppermute | solution.py:235
  17.3 3.6 %collective-permute-start.7 = (bf16[8,64,512]{2,1,0:T(8,128)(2,1)S(1)}, bf16[8,64,512]{2,1,0:T(8,128)(2,1)S(1)}, u32[]{:S(2)}, u32[]{:S(2)}) collective-permute-start(bf16[8,64,512]{2,1,0:T(8,128)(2,1)S(1)} %get-tuple-element.50), channel_id=1, source_target_pairs={{0,248},{1,249},{2,250},{3,251},{4,252},{5,253},{6,254},{7,255},{8... | collective-permute-start | bytes 1572872 | tf_op jit(solution)/shard_map/ppermute | solution.py:235
  20.9 4.9 %collective-permute-start.8 = (bf16[8,64,512]{2,1,0:T(8,128)(2,1)S(1)}, bf16[8,64,512]{2,1,0:T(8,128)(2,1)S(1)}, u32[]{:S(2)}, u32[]{:S(2)}) collective-permute-start(bf16[8,64,512]{2,1,0:T(8,128)(2,1)S(1)} %get-tuple-element.50), channel_id=1, source_target_pairs={{0,254},{1,255},{2,248},{3,249},{4,250},{5,251},{6,252},{7,253},{8... | collective-permute-start | bytes 1572872 | tf_op jit(solution)/shard_map/ppermute | solution.py:235
  27.2 5.3 %collective-permute-start.10 = (bf16[8,64,512]{2,1,0:T(8,128)(2,1)S(1)}, bf16[8,64,512]{2,1,0:T(8,128)(2,1)S(1)}, u32[]{:S(2)}, u32[]{:S(2)}) collective-permute-start(bf16[8,64,512]{2,1,0:T(8,128)(2,1)S(1)} %get-tuple-element.48), channel_id=1, source_target_pairs={{0,8},{1,9},{2,10},{3,11},{4,12},{5,13},{6,14},{7,15},{8,16},{9,17... | collective-permute-start | bytes 1572872 | tf_op jit(solution)/shard_map/ppermute | solution.py:235
  32.5 7.8 %collective-permute-done.21.refs_2_ = bf16[2,64,512]{2,1,0:T(8,128)(2,1)S(1)} collective-permute-done((bf16[2,64,512]{2,1,0:T(8,128)(2,1)S(1)}, bf16[2,64,512]{2,1,0:T(8,128)(2,1)S(1)}, u32[]{:S(2)}, u32[]{:S(2)}) %collective-permute-start.21) | collective-permute-done | bytes 131104 | tf_op jit(solution)/shard_map/ppermute | solution.py:235
  41.5 11.5 %collective-permute-done.23.refs_3_ = bf16[2,64,512]{2,1,0:T(8,128)(2,1)S(1)} collective-permute-done((bf16[2,64,512]{2,1,0:T(8,128)(2,1)S(1)}, bf16[2,64,512]{2,1,0:T(8,128)(2,1)S(1)}, u32[]{:S(2)}, u32[]{:S(2)}) %collective-permute-start.23) | collective-permute-done | bytes 131104 | tf_op jit(solution)/shard_map/ppermute | solution.py:235
  53.2 10.6 %collective-permute-start.15 = (bf16[8,64,512]{2,1,0:T(8,128)(2,1)S(1)}, bf16[8,64,512]{2,1,0:T(8,128)(2,1)S(1)}, u32[]{:S(2)}, u32[]{:S(2)}) collective-permute-start(bf16[8,64,512]{2,1,0:T(8,128)(2,1)S(1)} %get-tuple-element.47.c1), channel_id=1, source_target_pairs={{8,0},{9,1},{10,2},{11,3},{12,4},{13,5},{14,6},{15,7},{16,8},{17,9... | collective-permute-start | bytes 1572872 | tf_op jit(solution)/shard_map/ppermute | solution.py:235
  63.8 1.3 collective-permute-start.16
  65.2 39.6 %collective-permute-start.12 = (bf16[8,64,512]{2,1,0:T(8,128)(2,1)S(1)}, bf16[8,64,512]{2,1,0:T(8,128)(2,1)S(1)}, u32[]{:S(2)}, u32[]{:S(2)}) collective-permute-start(bf16[8,64,512]{2,1,0:T(8,128)(2,1)S(1)} %collective-permute-done.10.own), channel_id=1, source_target_pairs={{0,6},{1,7},{2,0},{3,1},{4,2},{5,3},{6,4},{7,5},{8,14},{9,15},{10,... | collective-permute-start | bytes 1572872 | tf_op jit(solution)/shard_map/ppermute | solution.py:235
  104.8 2.5 %collective-permute-start = (bf16[8,64,512]{2,1,0:T(8,128)(2,1)S(1)}, bf16[8,64,512]{2,1,0:T(8,128)(2,1)S(1)}, u32[]{:S(2)}, u32[]{:S(2)}) collective-permute-start(bf16[8,64,512]{2,1,0:T(8,128)(2,1)S(1)} %get-tuple-element.49.own), channel_id=1, source_target_pairs={{0,2},{1,3},{2,4},{3,5},{4,6},{5,7},{6,0},{7,1},{8,10},{9,11},{10,... | collective-permute-start | bytes 1572872 | tf_op jit(solution)/shard_map/ppermute | solution.py:235
  107.4 21.6 %collective-permute-start.1 = (bf16[8,64,512]{2,1,0:T(8,128)(2,1)S(1)}, bf16[8,64,512]{2,1,0:T(8,128)(2,1)S(1)}, u32[]{:S(2)}, u32[]{:S(2)}) collective-permute-start(bf16[8,64,512]{2,1,0:T(8,128)(2,1)S(1)} %get-tuple-element.49.own), channel_id=1, source_target_pairs={{0,6},{1,7},{2,0},{3,1},{4,2},{5,3},{6,4},{7,5},{8,14},{9,15},{10,... | collective-permute-start | bytes 1572872 | tf_op jit(solution)/shard_map/ppermute | solution.py:235
  129.2 6.9 %collective-permute-done.12.behind.b2 = bf16[8,64,512]{2,1,0:T(8,128)(2,1)S(1)} collective-permute-done((bf16[8,64,512]{2,1,0:T(8,128)(2,1)S(1)}, bf16[8,64,512]{2,1,0:T(8,128)(2,1)S(1)}, u32[]{:S(2)}, u32[]{:S(2)}) %collective-permute-start.12) | collective-permute-done | bytes 524320 | tf_op jit(solution)/shard_map/ppermute | solution.py:235
  136.1 5.8 %collective-permute-done.ahead = bf16[8,64,512]{2,1,0:T(8,128)(2,1)S(1)} collective-permute-done((bf16[8,64,512]{2,1,0:T(8,128)(2,1)S(1)}, bf16[8,64,512]{2,1,0:T(8,128)(2,1)S(1)}, u32[]{:S(2)}, u32[]{:S(2)}) %collective-permute-start) | collective-permute-done | bytes 524320 | tf_op jit(solution)/shard_map/ppermute | solution.py:235
  141.9 4.1 %collective-permute-start.14 = (bf16[8,64,512]{2,1,0:T(8,128)(2,1)S(1)}, bf16[8,64,512]{2,1,0:T(8,128)(2,1)S(1)}, u32[]{:S(2)}, u32[]{:S(2)}) collective-permute-start(bf16[8,64,512]{2,1,0:T(8,128)(2,1)S(1)} %get-tuple-element.30), channel_id=1, source_target_pairs={{0,6},{1,7},{2,0},{3,1},{4,2},{5,3},{6,4},{7,5},{8,14},{9,15},{10,... | collective-permute-start | bytes 1572872 | tf_op jit(solution)/shard_map/ppermute | solution.py:235
  146.4 4.1 %collective-permute-start.4 = (bf16[4,64,512]{2,1,0:T(8,128)(2,1)S(1)}, bf16[4,64,512]{2,1,0:T(8,128)(2,1)S(1)}, u32[]{:S(2)}, u32[]{:S(2)}) collective-permute-start(bf16[4,64,512]{2,1,0:T(8,128)(2,1)S(1)} %slice.33), channel_id=1, source_target_pairs={{0,6},{1,7},{2,0},{3,1},{4,2},{5,3},{6,4},{7,5},{8,14},{9,15},{10,... | collective-permute-start | bytes 786440 | tf_op jit(solution)/shard_map/ppermute | solution.py:235
  150.5 1.8 shard_map.49.refs_0_
  152.3 1.8 shard_map.50.refs_1_
  154.9 3.0 %shard_map.54 = (f32[4,8,8,128]{3,2,1,0:T(8,128)S(1)}, f32[4,8,8,128]{3,2,1,0:T(8,128)S(1)}) custom-call(f32[2,512,512]{2,1,0:T(8,128)S(1)} %shard_map.49.refs_0_, f32[2,512,512]{2,1,0:T(8,128)S(1)} %shard_map.50.refs_1_, bf16[8,64,512]{2,1,0:T(8,128)(2,1)S(1)} %collective-permute-done.13.refs_2_, bf16[8,64,512]{2,1,0:T(8,128)(2,1)S(1)} %collective-permute-done.14.refs_3_, ...), custom_call_target="tpu_custom_call" | custom-call | tf_op jit(solution)/shard_map/pallas_call | solution.py:242
  158.0 1.8 shard_map.47.refs_0_
  159.8 1.7 shard_map.48
  162.1 2.0 %collective-permute-start.28 = (f32[4,4,8,128]{3,2,1,0:T(8,128)S(1)}, f32[4,4,8,128]{3,2,1,0:T(8,128)S(1)}, u32[]{:S(2)}, u32[]{:S(2)}) collective-permute-start(f32[4,4,8,128]{3,2,1,0:T(8,128)S(1)} %get-tuple-element.40), channel_id=1, source_target_pairs={{0,248},{1,249},{2,250},{3,251},{4,252},{5,253},{6,254},{7,255},{8... | collective-permute-start | bytes 196616 | tf_op jit(solution)/shard_map/ppermute | solution.py:235
  164.2 2.2 %collective-permute-done.27.back1 = f32[4,4,8,128]{3,2,1,0:T(8,128)S(1)} collective-permute-done((f32[4,4,8,128]{3,2,1,0:T(8,128)S(1)}, f32[4,4,8,128]{3,2,1,0:T(8,128)S(1)}, u32[]{:S(2)}, u32[]{:S(2)}) %collective-permute-start.27) | collective-permute-done | bytes 65568 | tf_op jit(solution)/shard_map/ppermute | solution.py:235
  166.4 5.1 %collective-permute-done.28.back2 = f32[4,4,8,128]{3,2,1,0:T(8,128)S(1)} collective-permute-done((f32[4,4,8,128]{3,2,1,0:T(8,128)S(1)}, f32[4,4,8,128]{3,2,1,0:T(8,128)S(1)}, u32[]{:S(2)}, u32[]{:S(2)}) %collective-permute-start.28) | collective-permute-done | bytes 65568 | tf_op jit(solution)/shard_map/ppermute | solution.py:235
  171.5 3.2 %collective-permute-start.29 = (f32[12,8,128]{2,1,0:T(8,128)S(1)}, f32[12,8,128]{2,1,0:T(8,128)S(1)}, u32[]{:S(2)}, u32[]{:S(2)}) collective-permute-start(f32[12,8,128]{2,1,0:T(8,128)S(1)} %get-tuple-element.42), channel_id=1, source_target_pairs={{0,2},{1,3},{2,4},{3,5},{4,6},{5,7},{6,0},{7,1},{8,10},{9,11},{10,... | collective-permute-start | bytes 147464 | tf_op jit(solution)/shard_map/ppermute | solution.py:235
  175.8 5.6 %collective-permute-start.31 = (f32[12,8,128]{2,1,0:T(8,128)S(1)}, f32[12,8,128]{2,1,0:T(8,128)S(1)}, u32[]{:S(2)}, u32[]{:S(2)}) collective-permute-start(f32[12,8,128]{2,1,0:T(8,128)S(1)} %get-tuple-element.44), channel_id=1, source_target_pairs={{0,4},{1,5},{2,6},{3,7},{4,0},{5,1},{6,2},{7,3},{8,12},{9,13},{10,... | collective-permute-start | bytes 147464 | tf_op jit(solution)/shard_map/ppermute | solution.py:235
  181.3 2.6 %collective-permute-done.31.d = f32[12,8,128]{2,1,0:T(8,128)S(1)} collective-permute-done((f32[12,8,128]{2,1,0:T(8,128)S(1)}, f32[12,8,128]{2,1,0:T(8,128)S(1)}, u32[]{:S(2)}, u32[]{:S(2)}) %collective-permute-start.31) | collective-permute-done | bytes 49184 | tf_op jit(solution)/shard_map/ppermute | solution.py:235
  (56 shorter events, 9.5 us)
Async XLA Ops:
  4.9 141.5 %collective-permute-start.2 = (bf16[512,2048]{1,0:T(8,128)(2,1)S(1)}, bf16[512,2048]{1,0:T(8,128)(2,1)S(1)}, u32[]{:S(2)}, u32[]{:S(2)}) collective-permute-start(bf16[512,2048]{1,0:T(8,128)(2,1)S(1)} %get-tuple-element.26), channel_id=1, source_target_pairs={{0,1},{1,0},{2,3},{3,2},{4,5},{5,4},{6,7},{7,6},{8,9},{9,8},{10,11... | collective-permute-start | bytes 6291464 | tf_op jit(solution)/shard_map/ppermute | solution.py:235
  5.2 12.1 %collective-permute-start.17 = (bf16[2,64,512]{2,1,0:T(8,128)(2,1)S(1)}, bf16[2,64,512]{2,1,0:T(8,128)(2,1)S(1)}, u32[]{:S(2)}, u32[]{:S(2)}) collective-permute-start(bf16[2,64,512]{2,1,0:T(8,128)(2,1)S(1)} %get-tuple-element.31), channel_id=1, source_target_pairs={{0,248},{1,249},{2,250},{3,251},{4,252},{5,253},{6,254},{7,255},{1... | collective-permute-start | bytes 393224 | tf_op jit(solution)/shard_map/ppermute | solution.py:235
  8.7 4.6 %collective-permute-start.18 = (bf16[2,64,512]{2,1,0:T(8,128)(2,1)S(1)}, bf16[2,64,512]{2,1,0:T(8,128)(2,1)S(1)}, u32[]{:S(2)}, u32[]{:S(2)}) collective-permute-start(bf16[2,64,512]{2,1,0:T(8,128)(2,1)S(1)} %get-tuple-element.32), channel_id=1, source_target_pairs={{0,8},{1,9},{2,10},{3,11},{4,12},{5,13},{6,14},{7,15},{120,112},{1... | collective-permute-start | bytes 393224 | tf_op jit(solution)/shard_map/ppermute | solution.py:235
  10.0 11.0 %collective-permute-start.20 = (bf16[2,64,512]{2,1,0:T(8,128)(2,1)S(1)}, bf16[2,64,512]{2,1,0:T(8,128)(2,1)S(1)}, u32[]{:S(2)}, u32[]{:S(2)}) collective-permute-start(bf16[2,64,512]{2,1,0:T(8,128)(2,1)S(1)} %get-tuple-element.33), channel_id=1, source_target_pairs={{0,96},{1,97},{2,98},{3,99},{4,100},{5,101},{6,102},{7,103},{120,2... | collective-permute-start | bytes 393224 | tf_op jit(solution)/shard_map/ppermute | solution.py:235
  11.3 14.6 %collective-permute-start.22 = (bf16[2,64,512]{2,1,0:T(8,128)(2,1)S(1)}, bf16[2,64,512]{2,1,0:T(8,128)(2,1)S(1)}, u32[]{:S(2)}, u32[]{:S(2)}) collective-permute-start(bf16[2,64,512]{2,1,0:T(8,128)(2,1)S(1)} %get-tuple-element.34), channel_id=1, source_target_pairs={{0,32},{1,33},{2,34},{3,35},{4,36},{5,37},{6,38},{7,39},{120,88},{... | collective-permute-start | bytes 393224 | tf_op jit(solution)/shard_map/ppermute | solution.py:235
  13.2 13.9 %collective-permute-start.19 = (bf16[2,64,512]{2,1,0:T(8,128)(2,1)S(1)}, bf16[2,64,512]{2,1,0:T(8,128)(2,1)S(1)}, u32[]{:S(2)}, u32[]{:S(2)}) collective-permute-start(bf16[2,64,512]{2,1,0:T(8,128)(2,1)S(1)} %collective-permute-done.18), channel_id=1, source_target_pairs={{8,248},{9,249},{10,250},{11,251},{12,252},{13,253},{14,254},{15,2... | collective-permute-start | bytes 393224 | tf_op jit(solution)/shard_map/ppermute | solution.py:235
  17.3 35.9 %collective-permute-start.7 = (bf16[8,64,512]{2,1,0:T(8,128)(2,1)S(1)}, bf16[8,64,512]{2,1,0:T(8,128)(2,1)S(1)}, u32[]{:S(2)}, u32[]{:S(2)}) collective-permute-start(bf16[8,64,512]{2,1,0:T(8,128)(2,1)S(1)} %get-tuple-element.50), channel_id=1, source_target_pairs={{0,248},{1,249},{2,250},{3,251},{4,252},{5,253},{6,254},{7,255},{8... | collective-permute-start | bytes 1572872 | tf_op jit(solution)/shard_map/ppermute | solution.py:235
  20.9 42.9 %collective-permute-start.8 = (bf16[8,64,512]{2,1,0:T(8,128)(2,1)S(1)}, bf16[8,64,512]{2,1,0:T(8,128)(2,1)S(1)}, u32[]{:S(2)}, u32[]{:S(2)}) collective-permute-start(bf16[8,64,512]{2,1,0:T(8,128)(2,1)S(1)} %get-tuple-element.50), channel_id=1, source_target_pairs={{0,254},{1,255},{2,248},{3,249},{4,250},{5,251},{6,252},{7,253},{8... | collective-permute-start | bytes 1572872 | tf_op jit(solution)/shard_map/ppermute | solution.py:235
  25.9 14.4 %collective-permute-start.21 = (bf16[2,64,512]{2,1,0:T(8,128)(2,1)S(1)}, bf16[2,64,512]{2,1,0:T(8,128)(2,1)S(1)}, u32[]{:S(2)}, u32[]{:S(2)}) collective-permute-start(bf16[2,64,512]{2,1,0:T(8,128)(2,1)S(1)} %collective-permute-done.20), channel_id=1, source_target_pairs={{24,128},{25,129},{26,130},{27,131},{28,132},{29,133},{30,134},{31... | collective-permute-start | bytes 393224 | tf_op jit(solution)/shard_map/ppermute | solution.py:235
  27.2 38.0 %collective-permute-start.10 = (bf16[8,64,512]{2,1,0:T(8,128)(2,1)S(1)}, bf16[8,64,512]{2,1,0:T(8,128)(2,1)S(1)}, u32[]{:S(2)}, u32[]{:S(2)}) collective-permute-start(bf16[8,64,512]{2,1,0:T(8,128)(2,1)S(1)} %get-tuple-element.48), channel_id=1, source_target_pairs={{0,8},{1,9},{2,10},{3,11},{4,12},{5,13},{6,14},{7,15},{8,16},{9,17... | collective-permute-start | bytes 1572872 | tf_op jit(solution)/shard_map/ppermute | solution.py:235
  40.3 12.8 %collective-permute-start.23 = (bf16[2,64,512]{2,1,0:T(8,128)(2,1)S(1)}, bf16[2,64,512]{2,1,0:T(8,128)(2,1)S(1)}, u32[]{:S(2)}, u32[]{:S(2)}) collective-permute-start(bf16[2,64,512]{2,1,0:T(8,128)(2,1)S(1)} %collective-permute-done.22), channel_id=1, source_target_pairs={{32,248},{33,249},{34,250},{35,251},{36,252},{37,253},{38,254},{39... | collective-permute-start | bytes 393224 | tf_op jit(solution)/shard_map/ppermute | solution.py:235
  53.0 12.2 %collective-permute-start.11 = (bf16[8,64,512]{2,1,0:T(8,128)(2,1)S(1)}, bf16[8,64,512]{2,1,0:T(8,128)(2,1)S(1)}, u32[]{:S(2)}, u32[]{:S(2)}) collective-permute-start(bf16[8,64,512]{2,1,0:T(8,128)(2,1)S(1)} %get-tuple-element.48), channel_id=1, source_target_pairs={{0,10},{1,11},{2,12},{3,13},{4,14},{5,15},{6,8},{7,9},{8,18},{9,19... | collective-permute-start | bytes 1572872 | tf_op jit(solution)/shard_map/ppermute | solution.py:235
  53.2 51.7 %collective-permute-start.15 = (bf16[8,64,512]{2,1,0:T(8,128)(2,1)S(1)}, bf16[8,64,512]{2,1,0:T(8,128)(2,1)S(1)}, u32[]{:S(2)}, u32[]{:S(2)}) collective-permute-start(bf16[8,64,512]{2,1,0:T(8,128)(2,1)S(1)} %get-tuple-element.47.c1), channel_id=1, source_target_pairs={{8,0},{9,1},{10,2},{11,3},{12,4},{13,5},{14,6},{15,7},{16,8},{17,9... | collective-permute-start | bytes 1572872 | tf_op jit(solution)/shard_map/ppermute | solution.py:235
  63.8 43.5 %collective-permute-start.16 = (bf16[8,64,512]{2,1,0:T(8,128)(2,1)S(1)}, bf16[8,64,512]{2,1,0:T(8,128)(2,1)S(1)}, u32[]{:S(2)}, u32[]{:S(2)}) collective-permute-start(bf16[8,64,512]{2,1,0:T(8,128)(2,1)S(1)} %get-tuple-element.45.c2), channel_id=1, source_target_pairs={{0,8},{1,9},{2,10},{3,11},{4,12},{5,13},{6,14},{7,15},{8,16},{9,17... | collective-permute-start | bytes 1572872 | tf_op jit(solution)/shard_map/ppermute | solution.py:235
  65.1 64.0 %collective-permute-start.9 = (bf16[8,64,512]{2,1,0:T(8,128)(2,1)S(1)}, bf16[8,64,512]{2,1,0:T(8,128)(2,1)S(1)}, u32[]{:S(2)}, u32[]{:S(2)}) collective-permute-start(bf16[8,64,512]{2,1,0:T(8,128)(2,1)S(1)} %collective-permute-done.7.own), channel_id=1, source_target_pairs={{0,6},{1,7},{2,0},{3,1},{4,2},{5,3},{6,4},{7,5},{8,14},{9,15},{10,... | collective-permute-start | bytes 1572872 | tf_op jit(solution)/shard_map/ppermute | solution.py:235
  65.2 70.8 %collective-permute-start.12 = (bf16[8,64,512]{2,1,0:T(8,128)(2,1)S(1)}, bf16[8,64,512]{2,1,0:T(8,128)(2,1)S(1)}, u32[]{:S(2)}, u32[]{:S(2)}) collective-permute-start(bf16[8,64,512]{2,1,0:T(8,128)(2,1)S(1)} %collective-permute-done.10.own), channel_id=1, source_target_pairs={{0,6},{1,7},{2,0},{3,1},{4,2},{5,3},{6,4},{7,5},{8,14},{9,15},{10,... | collective-permute-start | bytes 1572872 | tf_op jit(solution)/shard_map/ppermute | solution.py:235
  104.8 37.1 %collective-permute-start = (bf16[8,64,512]{2,1,0:T(8,128)(2,1)S(1)}, bf16[8,64,512]{2,1,0:T(8,128)(2,1)S(1)}, u32[]{:S(2)}, u32[]{:S(2)}) collective-permute-start(bf16[8,64,512]{2,1,0:T(8,128)(2,1)S(1)} %get-tuple-element.49.own), channel_id=1, source_target_pairs={{0,2},{1,3},{2,4},{3,5},{4,6},{5,7},{6,0},{7,1},{8,10},{9,11},{10,... | collective-permute-start | bytes 1572872 | tf_op jit(solution)/shard_map/ppermute | solution.py:235
  107.4 34.6 %collective-permute-start.1 = (bf16[8,64,512]{2,1,0:T(8,128)(2,1)S(1)}, bf16[8,64,512]{2,1,0:T(8,128)(2,1)S(1)}, u32[]{:S(2)}, u32[]{:S(2)}) collective-permute-start(bf16[8,64,512]{2,1,0:T(8,128)(2,1)S(1)} %get-tuple-element.49.own), channel_id=1, source_target_pairs={{0,6},{1,7},{2,0},{3,1},{4,2},{5,3},{6,4},{7,5},{8,14},{9,15},{10,... | collective-permute-start | bytes 1572872 | tf_op jit(solution)/shard_map/ppermute | solution.py:235
  129.1 17.0 %collective-permute-start.24 = (bf16[8,64,512]{2,1,0:T(8,128)(2,1)S(1)}, bf16[8,64,512]{2,1,0:T(8,128)(2,1)S(1)}, u32[]{:S(2)}, u32[]{:S(2)}) collective-permute-start(bf16[8,64,512]{2,1,0:T(8,128)(2,1)S(1)} %get-tuple-element.35.refs_6_), channel_id=1, source_target_pairs={{0,1},{1,0},{2,3},{3,2},{4,5},{5,4},{6,7},{7,6},{8,9},{9,8},{10,11... | collective-permute-start | bytes 1572872 | tf_op jit(solution)/shard_map/ppermute | solution.py:235
  136.1 10.1 %collective-permute-start.25 = (bf16[8,64,512]{2,1,0:T(8,128)(2,1)S(1)}, bf16[8,64,512]{2,1,0:T(8,128)(2,1)S(1)}, u32[]{:S(2)}, u32[]{:S(2)}) collective-permute-start(bf16[8,64,512]{2,1,0:T(8,128)(2,1)S(1)} %get-tuple-element.36.refs_8_), channel_id=1, source_target_pairs={{0,1},{1,0},{2,3},{3,2},{4,5},{5,4},{6,7},{7,6},{8,9},{9,8},{10,11... | collective-permute-start | bytes 1572872 | tf_op jit(solution)/shard_map/ppermute | solution.py:235
  141.9 13.0 %collective-permute-start.13 = (bf16[8,64,512]{2,1,0:T(8,128)(2,1)S(1)}, bf16[8,64,512]{2,1,0:T(8,128)(2,1)S(1)}, u32[]{:S(2)}, u32[]{:S(2)}) collective-permute-start(bf16[8,64,512]{2,1,0:T(8,128)(2,1)S(1)} %get-tuple-element.29), channel_id=1, source_target_pairs={{0,2},{1,3},{2,4},{3,5},{4,6},{5,7},{6,0},{7,1},{8,10},{9,11},{10,... | collective-permute-start | bytes 1572872 | tf_op jit(solution)/shard_map/ppermute | solution.py:235
  141.9 13.0 %collective-permute-start.14 = (bf16[8,64,512]{2,1,0:T(8,128)(2,1)S(1)}, bf16[8,64,512]{2,1,0:T(8,128)(2,1)S(1)}, u32[]{:S(2)}, u32[]{:S(2)}) collective-permute-start(bf16[8,64,512]{2,1,0:T(8,128)(2,1)S(1)} %get-tuple-element.30), channel_id=1, source_target_pairs={{0,6},{1,7},{2,0},{3,1},{4,2},{5,3},{6,4},{7,5},{8,14},{9,15},{10,... | collective-permute-start | bytes 1572872 | tf_op jit(solution)/shard_map/ppermute | solution.py:235
  146.1 13.7 %collective-permute-start.5 = (bf16[8,64,512]{2,1,0:T(8,128)(2,1)S(1)}, bf16[8,64,512]{2,1,0:T(8,128)(2,1)S(1)}, u32[]{:S(2)}, u32[]{:S(2)}) collective-permute-start(bf16[8,64,512]{2,1,0:T(8,128)(2,1)S(1)} %get-tuple-element.46.refs_5_), channel_id=1, source_target_pairs={{0,1},{1,0},{2,3},{3,2},{4,5},{5,4},{6,7},{7,6},{8,9},{9,8},{10,11... | collective-permute-start | bytes 1572872 | tf_op jit(solution)/shard_map/ppermute | solution.py:235
  146.1 13.7 %collective-permute-start.3 = (bf16[4,64,512]{2,1,0:T(8,128)(2,1)S(1)}, bf16[4,64,512]{2,1,0:T(8,128)(2,1)S(1)}, u32[]{:S(2)}, u32[]{:S(2)}) collective-permute-start(bf16[4,64,512]{2,1,0:T(8,128)(2,1)S(1)} %slice.32), channel_id=1, source_target_pairs={{0,2},{1,3},{2,4},{3,5},{4,6},{5,7},{6,0},{7,1},{8,10},{9,11},{10,... | collective-permute-start | bytes 786440 | tf_op jit(solution)/shard_map/ppermute | solution.py:235
  146.4 13.4 %collective-permute-start.4 = (bf16[4,64,512]{2,1,0:T(8,128)(2,1)S(1)}, bf16[4,64,512]{2,1,0:T(8,128)(2,1)S(1)}, u32[]{:S(2)}, u32[]{:S(2)}) collective-permute-start(bf16[4,64,512]{2,1,0:T(8,128)(2,1)S(1)} %slice.33), channel_id=1, source_target_pairs={{0,6},{1,7},{2,0},{3,1},{4,2},{5,3},{6,4},{7,5},{8,14},{9,15},{10,... | collective-permute-start | bytes 786440 | tf_op jit(solution)/shard_map/ppermute | solution.py:235
  157.9 4.1 %collective-permute-start.26 = (f32[4,8,8,128]{3,2,1,0:T(8,128)S(1)}, f32[4,8,8,128]{3,2,1,0:T(8,128)S(1)}, u32[]{:S(2)}, u32[]{:S(2)}) collective-permute-start(f32[4,8,8,128]{3,2,1,0:T(8,128)S(1)} %get-tuple-element.38), channel_id=1, source_target_pairs={{0,1},{1,0},{2,3},{3,2},{4,5},{5,4},{6,7},{7,6},{8,9},{9,8},{10,11... | collective-permute-start | bytes 393224 | tf_op jit(solution)/shard_map/ppermute | solution.py:235
  161.5 2.7 %collective-permute-start.6 = (f32[4,4,8,128]{3,2,1,0:T(8,128)S(1)}, f32[4,4,8,128]{3,2,1,0:T(8,128)S(1)}, u32[]{:S(2)}, u32[]{:S(2)}) collective-permute-start(f32[4,4,8,128]{3,2,1,0:T(8,128)S(1)} %get-tuple-element.28), channel_id=1, source_target_pairs={{0,1},{1,0},{2,3},{3,2},{4,5},{5,4},{6,7},{7,6},{8,9},{9,8},{10,11... | collective-permute-start | bytes 196616 | tf_op jit(solution)/shard_map/ppermute | solution.py:235
  162.0 4.3 %collective-permute-start.27 = (f32[4,4,8,128]{3,2,1,0:T(8,128)S(1)}, f32[4,4,8,128]{3,2,1,0:T(8,128)S(1)}, u32[]{:S(2)}, u32[]{:S(2)}) collective-permute-start(f32[4,4,8,128]{3,2,1,0:T(8,128)S(1)} %get-tuple-element.39), channel_id=1, source_target_pairs={{0,8},{1,9},{2,10},{3,11},{4,12},{5,13},{6,14},{7,15},{8,16},{9,17... | collective-permute-start | bytes 196616 | tf_op jit(solution)/shard_map/ppermute | solution.py:235
  162.1 9.4 %collective-permute-start.28 = (f32[4,4,8,128]{3,2,1,0:T(8,128)S(1)}, f32[4,4,8,128]{3,2,1,0:T(8,128)S(1)}, u32[]{:S(2)}, u32[]{:S(2)}) collective-permute-start(f32[4,4,8,128]{3,2,1,0:T(8,128)S(1)} %get-tuple-element.40), channel_id=1, source_target_pairs={{0,248},{1,249},{2,250},{3,251},{4,252},{5,253},{6,254},{7,255},{8... | collective-permute-start | bytes 196616 | tf_op jit(solution)/shard_map/ppermute | solution.py:235
  171.5 9.8 %collective-permute-start.29 = (f32[12,8,128]{2,1,0:T(8,128)S(1)}, f32[12,8,128]{2,1,0:T(8,128)S(1)}, u32[]{:S(2)}, u32[]{:S(2)}) collective-permute-start(f32[12,8,128]{2,1,0:T(8,128)S(1)} %get-tuple-element.42), channel_id=1, source_target_pairs={{0,2},{1,3},{2,4},{3,5},{4,6},{5,7},{6,0},{7,1},{8,10},{9,11},{10,... | collective-permute-start | bytes 147464 | tf_op jit(solution)/shard_map/ppermute | solution.py:235
  174.7 6.7 %collective-permute-start.30 = (f32[12,8,128]{2,1,0:T(8,128)S(1)}, f32[12,8,128]{2,1,0:T(8,128)S(1)}, u32[]{:S(2)}, u32[]{:S(2)}) collective-permute-start(f32[12,8,128]{2,1,0:T(8,128)S(1)} %get-tuple-element.43), channel_id=1, source_target_pairs={{0,6},{1,7},{2,0},{3,1},{4,2},{5,3},{6,4},{7,5},{8,14},{9,15},{10,... | collective-permute-start | bytes 147464 | tf_op jit(solution)/shard_map/ppermute | solution.py:235
  175.8 8.2 %collective-permute-start.31 = (f32[12,8,128]{2,1,0:T(8,128)S(1)}, f32[12,8,128]{2,1,0:T(8,128)S(1)}, u32[]{:S(2)}, u32[]{:S(2)}) collective-permute-start(f32[12,8,128]{2,1,0:T(8,128)S(1)} %get-tuple-element.44), channel_id=1, source_target_pairs={{0,4},{1,5},{2,6},{3,7},{4,0},{5,1},{6,2},{7,3},{8,12},{9,13},{10,... | collective-permute-start | bytes 147464 | tf_op jit(solution)/shard_map/ppermute | solution.py:235
  (4 other events, 12.7 us)

commit v6 on v5

--- a/solution.py
+++ b/solution.py
@@ -78,20 +78,20 @@
         give_ref[:, span] = jnp.where(even, kept[1], kept[0]).astype(give_ref.dtype)
 
 
-def forward_kernel(owners, half, a1, b1, a2, b2, up_ref, down_ref):
+def forward_kernel(group, owners, a, b, up_ref, down_ref):
     owner, _, _ = where_am_i()
-    for n, (a, b) in enumerate(((a1, b1), (a2, b2))):
-        ahead_up = heading(n + 1, owner, owners) > 0
-
-        @pl.when(ahead_up)
-        def _():
-            up_ref[n * half : (n + 1) * half] = a[:half]
-            down_ref[n * half : (n + 1) * half] = b[half:]
-
-        @pl.when(jnp.logical_not(ahead_up))
-        def _():
-            up_ref[n * half : (n + 1) * half] = b[:half]
-            down_ref[n * half : (n + 1) * half] = a[half:]
+    half = up_ref.shape[0]
+    ahead_up = heading(group, owner, owners) > 0
+
+    @pl.when(ahead_up)
+    def _():
+        up_ref[...] = a[:half]
+        down_ref[...] = b[half:]
+
+    @pl.when(jnp.logical_not(ahead_up))
+    def _():
+        up_ref[...] = b[:half]
+        down_ref[...] = a[half:]
 
 
 def pick_kernel(owners, c1, c2, *out):
@@ -154,19 +154,20 @@
 
 def last_kernel(groups, quarters, half, *refs):
     accs, refs = refs[:groups], refs[groups:]
-    far, (w0, w1), refs = refs[:2], refs[2:4], refs[4:]
+    fars, refs = refs[: 2 * groups], refs[2 * groups :]
+    (w0, w1), refs = refs[:2], refs[2:]
     conduction, (keep_ref, give_ref) = refs[:-2], refs[-2:]
     _, quarter, core = where_am_i()
-    bands, rows = far[0].shape[1:]
+    bands, rows = fars[0].shape[1:]
     at = pl.multiple_of(lax.rem(quarter + 2, quarters) * rows, rows)
     even = core == 0
     for g in range(groups):
-        for h, x in enumerate(far):
+        for h, x in enumerate(fars[2 * g : 2 * g + 2]):
             base = h * half * bands
             both = []
             for s, w in enumerate((w0, w1)):
                 y = accs[g][s, base : base + half * bands] + lax.dot_general(
-                    x[g * half : (g + 1) * half].reshape(half * bands, rows),
+                    flat(x),
                     w[:, pl.ds(at, rows)],
                     CONTRACT_LAST,
                     preferred_element_type=jnp.float32,
@@ -299,19 +300,20 @@
     own[0] = v[0]
     ahead[0] = send(v[0], lambda i, k, c: (i, k + 1, c))
     behind[0] = send(v[0], lambda i, k, c: (i, k - 1, c))
-    going_up, going_down = call(
-        functools.partial(forward_kernel, owners, half),
-        [jax.ShapeDtypeStruct(v[0].shape, v[0].dtype)] * 2,
-        (ahead[1], behind[1], ahead[2], behind[2]),
-    )
-    far = (
-        send(going_up, lambda i, k, c: (i, k + 1, c)),
-        send(going_down, lambda i, k, c: (i, k - 1, c)),
-    )
-    far0 = (
-        send(ahead[0][:half], lambda i, k, c: (i, k + 1, c)),
-        send(behind[0][half:], lambda i, k, c: (i, k - 1, c)),
-    )
+    far = {}
+    for g in (1, 2):
+        going_up, going_down = call(
+            functools.partial(forward_kernel, g, owners),
+            [jax.ShapeDtypeStruct((half, *v[0].shape[1:]), v[0].dtype)] * 2,
+            (ahead[g], behind[g]),
+        )
+        far[g] = (going_up, going_down)
+    far[0] = (ahead[0][:half], behind[0][half:])
+    for g in (1, 2, 0):
+        far[g] = (
+            send(far[g][0], lambda i, k, c: (i, k + 1, c)),
+            send(far[g][1], lambda i, k, c: (i, k - 1, c)),
+        )
 
     block = rows // 4
     w0, give = call(
@@ -347,7 +349,7 @@
         )
 
     accs = [first(g) for g in (1, 2)]
-    keep, give = last((1, 2), accs, far)
+    keep, give = last((1, 2), accs, far[1] + far[2])
     packed = (quarters, half, *keep.shape[2:])
     back = list(
         call(
@@ -359,7 +361,7 @@
     for g in (1, 2):
         back[g - 1] = send(back[g - 1], lambda i, k, c: (i - shift[g], k, c))
     acc = first(0)
-    keep0, give0 = last((0,), [acc], far0)
+    keep0, give0 = last((0,), [acc], far[0])
     blocks = call(
         merge_kernel,
         [jax.ShapeDtypeStruct((3 * half, *packed[2:]), jnp.float32)] * quarters,

time: 185 us -> 179 us (0.968)
  the two profiles are of different devices: /device:TPU:62 before, /device:TPU:30 now
where the time goes in v6:
time: 179 us
  waiting for transfers between devices  96.8 us (54%)
  starting transfers between devices  67.3 us (38%)
  Pallas kernels  13.1 us (7%)
  local copies, waits for them, and re-layouts  1.8 us (1%)
    ppermute x34, waiting for transfers between devices, send(): return lax.ppermute(x, AXES, moves(owners, quarters, target))  96.8 us
    ppermute x34, starting transfers between devices, send(): return lax.ppermute(x, AXES, moves(owners, quarters, target))  67.3 us
    pallas_call x13, Pallas kernels, call(): pl.pallas_call(body, in_specs=in_specs or [VMEM] * len(operands), out_spe...  13.1 us
  transfers between devices with their start and end apart: 34, of which 17 were waited for; matrix products, arithmetic and copies ran while one was open for 0% of the time, Pallas kernels for 7%

profile of v6, /device:TPU:30, one launch (start us, length us, event | category | flops | bytes accessed | tf_op | source)
XLA Modules:
  0.0 179.3 jit_solution(9534208228378892914)
XLA Ops:
  0.0 1.6 fusion
  1.7 2.8 %collective-permute-start.20 = (bf16[2,64,512]{2,1,0:T(8,128)(2,1)S(1)}, bf16[2,64,512]{2,1,0:T(8,128)(2,1)S(1)}, u32[]{:S(2)}, u32[]{:S(2)}) collective-permute-start(bf16[2,64,512]{2,1,0:T(8,128)(2,1)S(1)} %get-tuple-element.36), channel_id=1, source_target_pairs={{0,8},{1,9},{2,10},{3,11},{4,12},{5,13},{6,14},{7,15},{120,112},{1... | collective-permute-start | bytes 393224 | tf_op jit(solution)/shard_map/ppermute | solution.py:236
  5.9 2.0 %shard_map.46 = (bf16[512,2048]{1,0:T(8,128)(2,1)S(1)}, bf16[512,2048]{1,0:T(8,128)(2,1)S(1)}) custom-call(s32[32]{0:T(128)S(1)} %copy-done.1, bf16[512,4096]{1,0:T(8,128)(2,1)S(1)} %bitcast.1), custom_call_target="tpu_custom_call" | custom-call | tf_op jit(solution)/shard_map/pallas_call | solution.py:243
  8.0 4.8 %collective-permute-start.19 = (bf16[2,64,512]{2,1,0:T(8,128)(2,1)S(1)}, bf16[2,64,512]{2,1,0:T(8,128)(2,1)S(1)}, u32[]{:S(2)}, u32[]{:S(2)}) collective-permute-start(bf16[2,64,512]{2,1,0:T(8,128)(2,1)S(1)} %get-tuple-element.35), channel_id=1, source_target_pairs={{0,248},{1,249},{2,250},{3,251},{4,252},{5,253},{6,254},{7,255},{1... | collective-permute-start | bytes 393224 | tf_op jit(solution)/shard_map/ppermute | solution.py:236
  16.8 3.2 %collective-permute-done.19.refs_0_ = bf16[2,64,512]{2,1,0:T(8,128)(2,1)S(1)} collective-permute-done((bf16[2,64,512]{2,1,0:T(8,128)(2,1)S(1)}, bf16[2,64,512]{2,1,0:T(8,128)(2,1)S(1)}, u32[]{:S(2)}, u32[]{:S(2)}) %collective-permute-start.19) | collective-permute-done | bytes 131104 | tf_op jit(solution)/shard_map/ppermute | solution.py:236
  20.0 3.3 %collective-permute-start = (bf16[8,64,512]{2,1,0:T(8,128)(2,1)S(1)}, bf16[8,64,512]{2,1,0:T(8,128)(2,1)S(1)}, u32[]{:S(2)}, u32[]{:S(2)}) collective-permute-start(bf16[8,64,512]{2,1,0:T(8,128)(2,1)S(1)} %get-tuple-element.53.own), channel_id=1, source_target_pairs={{0,2},{1,3},{2,4},{3,5},{4,6},{5,7},{6,0},{7,1},{8,10},{9,11},{10,... | collective-permute-start | bytes 1572872 | tf_op jit(solution)/shard_map/ppermute | solution.py:236
  23.3 3.0 %collective-permute-start.1 = (bf16[8,64,512]{2,1,0:T(8,128)(2,1)S(1)}, bf16[8,64,512]{2,1,0:T(8,128)(2,1)S(1)}, u32[]{:S(2)}, u32[]{:S(2)}) collective-permute-start(bf16[8,64,512]{2,1,0:T(8,128)(2,1)S(1)} %get-tuple-element.53.own), channel_id=1, source_target_pairs={{0,6},{1,7},{2,0},{3,1},{4,2},{5,3},{6,4},{7,5},{8,14},{9,15},{10,... | collective-permute-start | bytes 1572872 | tf_op jit(solution)/shard_map/ppermute | solution.py:236
  26.3 1.5 collective-permute-done.21.refs_1_
  29.2 27.0 %collective-permute-done.25.refs_3_ = bf16[2,64,512]{2,1,0:T(8,128)(2,1)S(1)} collective-permute-done((bf16[2,64,512]{2,1,0:T(8,128)(2,1)S(1)}, bf16[2,64,512]{2,1,0:T(8,128)(2,1)S(1)}, u32[]{:S(2)}, u32[]{:S(2)}) %collective-permute-start.25) | collective-permute-done | bytes 131104 | tf_op jit(solution)/shard_map/ppermute | solution.py:236
  59.0 5.4 %collective-permute-done.7.own = bf16[8,64,512]{2,1,0:T(8,128)(2,1)S(1)} collective-permute-done((bf16[8,64,512]{2,1,0:T(8,128)(2,1)S(1)}, bf16[8,64,512]{2,1,0:T(8,128)(2,1)S(1)}, u32[]{:S(2)}, u32[]{:S(2)}) %collective-permute-start.7) | collective-permute-done | bytes 524320 | tf_op jit(solution)/shard_map/ppermute | solution.py:236
  64.4 2.6 %collective-permute-done.17.c1 = bf16[8,64,512]{2,1,0:T(8,128)(2,1)S(1)} collective-permute-done((bf16[8,64,512]{2,1,0:T(8,128)(2,1)S(1)}, bf16[8,64,512]{2,1,0:T(8,128)(2,1)S(1)}, u32[]{:S(2)}, u32[]{:S(2)}) %collective-permute-start.17) | collective-permute-done | bytes 524320 | tf_op jit(solution)/shard_map/ppermute | solution.py:236
  68.1 6.2 %collective-permute-done.18.c2 = bf16[8,64,512]{2,1,0:T(8,128)(2,1)S(1)} collective-permute-done((bf16[8,64,512]{2,1,0:T(8,128)(2,1)S(1)}, bf16[8,64,512]{2,1,0:T(8,128)(2,1)S(1)}, u32[]{:S(2)}, u32[]{:S(2)}) %collective-permute-start.18) | collective-permute-done | bytes 524320 | tf_op jit(solution)/shard_map/ppermute | solution.py:236
  74.4 8.3 %collective-permute-done.10.own = bf16[8,64,512]{2,1,0:T(8,128)(2,1)S(1)} collective-permute-done((bf16[8,64,512]{2,1,0:T(8,128)(2,1)S(1)}, bf16[8,64,512]{2,1,0:T(8,128)(2,1)S(1)}, u32[]{:S(2)}, u32[]{:S(2)}) %collective-permute-start.10) | collective-permute-done | bytes 524320 | tf_op jit(solution)/shard_map/ppermute | solution.py:236
  84.0 7.1 %collective-permute-done.8.ahead.a = bf16[8,64,512]{2,1,0:T(8,128)(2,1)S(1)} collective-permute-done((bf16[8,64,512]{2,1,0:T(8,128)(2,1)S(1)}, bf16[8,64,512]{2,1,0:T(8,128)(2,1)S(1)}, u32[]{:S(2)}, u32[]{:S(2)}) %collective-permute-start.8) | collective-permute-done | bytes 524320 | tf_op jit(solution)/shard_map/ppermute | solution.py:236
  92.5 10.4 %collective-permute-done.11.ahead.a = bf16[8,64,512]{2,1,0:T(8,128)(2,1)S(1)} collective-permute-done((bf16[8,64,512]{2,1,0:T(8,128)(2,1)S(1)}, bf16[8,64,512]{2,1,0:T(8,128)(2,1)S(1)}, u32[]{:S(2)}, u32[]{:S(2)}) %collective-permute-start.11) | collective-permute-done | bytes 524320 | tf_op jit(solution)/shard_map/ppermute | solution.py:236
  103.2 8.1 %collective-permute-done.12.behind.b = bf16[8,64,512]{2,1,0:T(8,128)(2,1)S(1)} collective-permute-done((bf16[8,64,512]{2,1,0:T(8,128)(2,1)S(1)}, bf16[8,64,512]{2,1,0:T(8,128)(2,1)S(1)}, u32[]{:S(2)}, u32[]{:S(2)}) %collective-permute-start.12) | collective-permute-done | bytes 524320 | tf_op jit(solution)/shard_map/ppermute | solution.py:236
  111.3 3.8 %collective-permute-start.14 = (bf16[4,64,512]{2,1,0:T(8,128)(2,1)S(1)}, bf16[4,64,512]{2,1,0:T(8,128)(2,1)S(1)}, u32[]{:S(2)}, u32[]{:S(2)}) collective-permute-start(bf16[4,64,512]{2,1,0:T(8,128)(2,1)S(1)} %get-tuple-element.32), channel_id=1, source_target_pairs={{0,6},{1,7},{2,0},{3,1},{4,2},{5,3},{6,4},{7,5},{8,14},{9,15},{10,... | collective-permute-start | bytes 786440 | tf_op jit(solution)/shard_map/ppermute | solution.py:236
  115.4 4.1 %collective-permute-start.16 = (bf16[4,64,512]{2,1,0:T(8,128)(2,1)S(1)}, bf16[4,64,512]{2,1,0:T(8,128)(2,1)S(1)}, u32[]{:S(2)}, u32[]{:S(2)}) collective-permute-start(bf16[4,64,512]{2,1,0:T(8,128)(2,1)S(1)} %get-tuple-element.34), channel_id=1, source_target_pairs={{0,6},{1,7},{2,0},{3,1},{4,2},{5,3},{6,4},{7,5},{8,14},{9,15},{10,... | collective-permute-start | bytes 786440 | tf_op jit(solution)/shard_map/ppermute | solution.py:236
  119.6 1.5 collective-permute-start.3
  121.1 2.7 %collective-permute-start.4 = (bf16[4,64,512]{2,1,0:T(8,128)(2,1)S(1)}, bf16[4,64,512]{2,1,0:T(8,128)(2,1)S(1)}, u32[]{:S(2)}, u32[]{:S(2)}) collective-permute-start(bf16[4,64,512]{2,1,0:T(8,128)(2,1)S(1)} %slice.33), channel_id=1, source_target_pairs={{0,6},{1,7},{2,0},{3,1},{4,2},{5,3},{6,4},{7,5},{8,14},{9,15},{10,... | collective-permute-start | bytes 786440 | tf_op jit(solution)/shard_map/ppermute | solution.py:236
  123.8 1.8 %shard_map.49.refs_0_ = f32[2,512,512]{2,1,0:T(8,128)S(1)} custom-call(bf16[8,64,512]{2,1,0:T(8,128)(2,1)S(1)} %collective-permute-done.7.own, bf16[8,64,512]{2,1,0:T(8,128)(2,1)S(1)} %collective-permute-done.8.ahead.a, bf16[8,64,512]{2,1,0:T(8,128)(2,1)S(1)} %collective-permute-done.9.behind.b, bf16[512,2048]{1,0:T(8,128)(2,1)S(1)} %get-tuple-element.27.w0.refs_3_.refs_6_, ...), custom_call_target="tpu_custom_call" | custom-call | tf_op jit(solution)/shard_map/pallas_call | solution.py:243
  125.7 1.8 %shard_map.50.refs_1_ = f32[2,512,512]{2,1,0:T(8,128)S(1)} custom-call(bf16[8,64,512]{2,1,0:T(8,128)(2,1)S(1)} %collective-permute-done.10.own, bf16[8,64,512]{2,1,0:T(8,128)(2,1)S(1)} %collective-permute-done.11.ahead.a, bf16[8,64,512]{2,1,0:T(8,128)(2,1)S(1)} %collective-permute-done.12.behind.b, ...), custom_call_target="tpu_custom_call" | custom-call | tf_op jit(solution)/shard_map/pallas_call | solution.py:243
  127.5 3.8 %collective-permute-done.15.refs_4_ = bf16[4,64,512]{2,1,0:T(8,128)(2,1)S(1)} collective-permute-done((bf16[4,64,512]{2,1,0:T(8,128)(2,1)S(1)}, bf16[4,64,512]{2,1,0:T(8,128)(2,1)S(1)}, u32[]{:S(2)}, u32[]{:S(2)}) %collective-permute-start.15) | collective-permute-done | bytes 262176 | tf_op jit(solution)/shard_map/ppermute | solution.py:236
  131.3 3.0 %shard_map.55 = (f32[4,8,8,128]{3,2,1,0:T(8,128)S(1)}, f32[4,8,8,128]{3,2,1,0:T(8,128)S(1)}) custom-call(f32[2,512,512]{2,1,0:T(8,128)S(1)} %shard_map.49.refs_0_, f32[2,512,512]{2,1,0:T(8,128)S(1)} %shard_map.50.refs_1_, bf16[4,64,512]{2,1,0:T(8,128)(2,1)S(1)} %collective-permute-done.13.refs_2_, bf16[4,64,512]{2,1,0:T(8,128)(2,1)S(1)} %collective-permute-done.14.refs_3_, ...), custom_call_target="tpu_custom_call" | custom-call | tf_op jit(solution)/shard_map/pallas_call | solution.py:243
  134.4 1.8 %shard_map.47.refs_0_ = f32[2,512,512]{2,1,0:T(8,128)S(1)} custom-call(bf16[8,64,512]{2,1,0:T(8,128)(2,1)S(1)} %get-tuple-element.53.own, bf16[8,64,512]{2,1,0:T(8,128)(2,1)S(1)} %collective-permute-done.ahead, bf16[8,64,512]{2,1,0:T(8,128)(2,1)S(1)} %collective-permute-done.1.behind, bf16[512,2048]{1,0:T(8,128)(2,1)S(1)} %get-tuple-element.27.w0.refs_3_.refs_6_, ...), custom_call_target="tpu_custom_call" | custom-call | tf_op jit(solution)/shard_map/pallas_call | solution.py:243
  137.0 1.6 shard_map.48
  138.8 17.5 %collective-permute-start.29 = (f32[4,4,8,128]{3,2,1,0:T(8,128)S(1)}, f32[4,4,8,128]{3,2,1,0:T(8,128)S(1)}, u32[]{:S(2)}, u32[]{:S(2)}) collective-permute-start(f32[4,4,8,128]{3,2,1,0:T(8,128)S(1)} %get-tuple-element.43), channel_id=1, source_target_pairs={{0,8},{1,9},{2,10},{3,11},{4,12},{5,13},{6,14},{7,15},{8,16},{9,17... | collective-permute-start | bytes 196616 | tf_op jit(solution)/shard_map/ppermute | solution.py:236
  156.3 1.9 %collective-permute-done.29.back1 = f32[4,4,8,128]{3,2,1,0:T(8,128)S(1)} collective-permute-done((f32[4,4,8,128]{3,2,1,0:T(8,128)S(1)}, f32[4,4,8,128]{3,2,1,0:T(8,128)S(1)}, u32[]{:S(2)}, u32[]{:S(2)}) %collective-permute-start.29) | collective-permute-done | bytes 65568 | tf_op jit(solution)/shard_map/ppermute | solution.py:236
  158.2 6.6 %collective-permute-done.30.back2 = f32[4,4,8,128]{3,2,1,0:T(8,128)S(1)} collective-permute-done((f32[4,4,8,128]{3,2,1,0:T(8,128)S(1)}, f32[4,4,8,128]{3,2,1,0:T(8,128)S(1)}, u32[]{:S(2)}, u32[]{:S(2)}) %collective-permute-start.30) | collective-permute-done | bytes 65568 | tf_op jit(solution)/shard_map/ppermute | solution.py:236
  165.7 3.3 %collective-permute-start.32 = (f32[12,8,128]{2,1,0:T(8,128)S(1)}, f32[12,8,128]{2,1,0:T(8,128)S(1)}, u32[]{:S(2)}, u32[]{:S(2)}) collective-permute-start(f32[12,8,128]{2,1,0:T(8,128)S(1)} %get-tuple-element.47), channel_id=1, source_target_pairs={{0,6},{1,7},{2,0},{3,1},{4,2},{5,3},{6,4},{7,5},{8,14},{9,15},{10,... | collective-permute-start | bytes 147464 | tf_op jit(solution)/shard_map/ppermute | solution.py:236
  169.0 6.9 %collective-permute-start.33 = (f32[12,8,128]{2,1,0:T(8,128)S(1)}, f32[12,8,128]{2,1,0:T(8,128)S(1)}, u32[]{:S(2)}, u32[]{:S(2)}) collective-permute-start(f32[12,8,128]{2,1,0:T(8,128)S(1)} %get-tuple-element.48), channel_id=1, source_target_pairs={{0,4},{1,5},{2,6},{3,7},{4,0},{5,1},{6,2},{7,3},{8,12},{9,13},{10,... | collective-permute-start | bytes 147464 | tf_op jit(solution)/shard_map/ppermute | solution.py:236
  176.1 2.5 %collective-permute-done.33.d = f32[12,8,128]{2,1,0:T(8,128)S(1)} collective-permute-done((f32[12,8,128]{2,1,0:T(8,128)S(1)}, f32[12,8,128]{2,1,0:T(8,128)S(1)}, u32[]{:S(2)}, u32[]{:S(2)}) %collective-permute-start.33) | collective-permute-done | bytes 49184 | tf_op jit(solution)/shard_map/ppermute | solution.py:236
  (59 shorter events, 16.7 us)
Async XLA Ops:
  1.7 12.4 %collective-permute-start.20 = (bf16[2,64,512]{2,1,0:T(8,128)(2,1)S(1)}, bf16[2,64,512]{2,1,0:T(8,128)(2,1)S(1)}, u32[]{:S(2)}, u32[]{:S(2)}) collective-permute-start(bf16[2,64,512]{2,1,0:T(8,128)(2,1)S(1)} %get-tuple-element.36), channel_id=1, source_target_pairs={{0,8},{1,9},{2,10},{3,11},{4,12},{5,13},{6,14},{7,15},{120,112},{1... | collective-permute-start | bytes 393224 | tf_op jit(solution)/shard_map/ppermute | solution.py:236
  4.5 10.9 %collective-permute-start.22 = (bf16[2,64,512]{2,1,0:T(8,128)(2,1)S(1)}, bf16[2,64,512]{2,1,0:T(8,128)(2,1)S(1)}, u32[]{:S(2)}, u32[]{:S(2)}) collective-permute-start(bf16[2,64,512]{2,1,0:T(8,128)(2,1)S(1)} %get-tuple-element.37), channel_id=1, source_target_pairs={{0,96},{1,97},{2,98},{3,99},{4,100},{5,101},{6,102},{7,103},{120,2... | collective-permute-start | bytes 393224 | tf_op jit(solution)/shard_map/ppermute | solution.py:236
  7.9 113.2 %collective-permute-start.2 = (bf16[512,2048]{1,0:T(8,128)(2,1)S(1)}, bf16[512,2048]{1,0:T(8,128)(2,1)S(1)}, u32[]{:S(2)}, u32[]{:S(2)}) collective-permute-start(bf16[512,2048]{1,0:T(8,128)(2,1)S(1)} %get-tuple-element.28), channel_id=1, source_target_pairs={{0,1},{1,0},{2,3},{3,2},{4,5},{5,4},{6,7},{7,6},{8,9},{9,8},{10,11... | collective-permute-start | bytes 6291464 | tf_op jit(solution)/shard_map/ppermute | solution.py:236
  8.0 12.0 %collective-permute-start.19 = (bf16[2,64,512]{2,1,0:T(8,128)(2,1)S(1)}, bf16[2,64,512]{2,1,0:T(8,128)(2,1)S(1)}, u32[]{:S(2)}, u32[]{:S(2)}) collective-permute-start(bf16[2,64,512]{2,1,0:T(8,128)(2,1)S(1)} %get-tuple-element.35), channel_id=1, source_target_pairs={{0,248},{1,249},{2,250},{3,251},{4,252},{5,253},{6,254},{7,255},{1... | collective-permute-start | bytes 393224 | tf_op jit(solution)/shard_map/ppermute | solution.py:236
  12.8 10.5 %collective-permute-start.24 = (bf16[2,64,512]{2,1,0:T(8,128)(2,1)S(1)}, bf16[2,64,512]{2,1,0:T(8,128)(2,1)S(1)}, u32[]{:S(2)}, u32[]{:S(2)}) collective-permute-start(bf16[2,64,512]{2,1,0:T(8,128)(2,1)S(1)} %get-tuple-element.38), channel_id=1, source_target_pairs={{0,32},{1,33},{2,34},{3,35},{4,36},{5,37},{6,38},{7,39},{120,88},{... | collective-permute-start | bytes 393224 | tf_op jit(solution)/shard_map/ppermute | solution.py:236
  14.1 13.7 %collective-permute-start.21 = (bf16[2,64,512]{2,1,0:T(8,128)(2,1)S(1)}, bf16[2,64,512]{2,1,0:T(8,128)(2,1)S(1)}, u32[]{:S(2)}, u32[]{:S(2)}) collective-permute-start(bf16[2,64,512]{2,1,0:T(8,128)(2,1)S(1)} %collective-permute-done.20), channel_id=1, source_target_pairs={{8,248},{9,249},{10,250},{11,251},{12,252},{13,253},{14,254},{15,2... | collective-permute-start | bytes 393224 | tf_op jit(solution)/shard_map/ppermute | solution.py:236
  15.4 13.7 %collective-permute-start.23 = (bf16[2,64,512]{2,1,0:T(8,128)(2,1)S(1)}, bf16[2,64,512]{2,1,0:T(8,128)(2,1)S(1)}, u32[]{:S(2)}, u32[]{:S(2)}) collective-permute-start(bf16[2,64,512]{2,1,0:T(8,128)(2,1)S(1)} %collective-permute-done.22), channel_id=1, source_target_pairs={{24,128},{25,129},{26,130},{27,131},{28,132},{29,133},{30,134},{31... | collective-permute-start | bytes 393224 | tf_op jit(solution)/shard_map/ppermute | solution.py:236
  20.0 37.6 %collective-permute-start = (bf16[8,64,512]{2,1,0:T(8,128)(2,1)S(1)}, bf16[8,64,512]{2,1,0:T(8,128)(2,1)S(1)}, u32[]{:S(2)}, u32[]{:S(2)}) collective-permute-start(bf16[8,64,512]{2,1,0:T(8,128)(2,1)S(1)} %get-tuple-element.53.own), channel_id=1, source_target_pairs={{0,2},{1,3},{2,4},{3,5},{4,6},{5,7},{6,0},{7,1},{8,10},{9,11},{10,... | collective-permute-start | bytes 1572872 | tf_op jit(solution)/shard_map/ppermute | solution.py:236
  23.3 35.6 %collective-permute-start.1 = (bf16[8,64,512]{2,1,0:T(8,128)(2,1)S(1)}, bf16[8,64,512]{2,1,0:T(8,128)(2,1)S(1)}, u32[]{:S(2)}, u32[]{:S(2)}) collective-permute-start(bf16[8,64,512]{2,1,0:T(8,128)(2,1)S(1)} %get-tuple-element.53.own), channel_id=1, source_target_pairs={{0,6},{1,7},{2,0},{3,1},{4,2},{5,3},{6,4},{7,5},{8,14},{9,15},{10,... | collective-permute-start | bytes 1572872 | tf_op jit(solution)/shard_map/ppermute | solution.py:236
  27.8 28.4 %collective-permute-start.25 = (bf16[2,64,512]{2,1,0:T(8,128)(2,1)S(1)}, bf16[2,64,512]{2,1,0:T(8,128)(2,1)S(1)}, u32[]{:S(2)}, u32[]{:S(2)}) collective-permute-start(bf16[2,64,512]{2,1,0:T(8,128)(2,1)S(1)} %collective-permute-done.24), channel_id=1, source_target_pairs={{32,248},{33,249},{34,250},{35,251},{36,252},{37,253},{38,254},{39... | collective-permute-start | bytes 393224 | tf_op jit(solution)/shard_map/ppermute | solution.py:236
  29.1 35.2 %collective-permute-start.7 = (bf16[8,64,512]{2,1,0:T(8,128)(2,1)S(1)}, bf16[8,64,512]{2,1,0:T(8,128)(2,1)S(1)}, u32[]{:S(2)}, u32[]{:S(2)}) collective-permute-start(bf16[8,64,512]{2,1,0:T(8,128)(2,1)S(1)} %get-tuple-element.54), channel_id=1, source_target_pairs={{0,248},{1,249},{2,250},{3,251},{4,252},{5,253},{6,254},{7,255},{8... | collective-permute-start | bytes 1572872 | tf_op jit(solution)/shard_map/ppermute | solution.py:236
  56.3 10.7 %collective-permute-start.17 = (bf16[8,64,512]{2,1,0:T(8,128)(2,1)S(1)}, bf16[8,64,512]{2,1,0:T(8,128)(2,1)S(1)}, u32[]{:S(2)}, u32[]{:S(2)}) collective-permute-start(bf16[8,64,512]{2,1,0:T(8,128)(2,1)S(1)} %get-tuple-element.51.c1), channel_id=1, source_target_pairs={{8,0},{9,1},{10,2},{11,3},{12,4},{13,5},{14,6},{15,7},{16,8},{17,9... | collective-permute-start | bytes 1572872 | tf_op jit(solution)/shard_map/ppermute | solution.py:236
  57.6 16.7 %collective-permute-start.18 = (bf16[8,64,512]{2,1,0:T(8,128)(2,1)S(1)}, bf16[8,64,512]{2,1,0:T(8,128)(2,1)S(1)}, u32[]{:S(2)}, u32[]{:S(2)}) collective-permute-start(bf16[8,64,512]{2,1,0:T(8,128)(2,1)S(1)} %get-tuple-element.49.c2), channel_id=1, source_target_pairs={{0,8},{1,9},{2,10},{3,11},{4,12},{5,13},{6,14},{7,15},{8,16},{9,17... | collective-permute-start | bytes 1572872 | tf_op jit(solution)/shard_map/ppermute | solution.py:236
  58.9 23.8 %collective-permute-start.10 = (bf16[8,64,512]{2,1,0:T(8,128)(2,1)S(1)}, bf16[8,64,512]{2,1,0:T(8,128)(2,1)S(1)}, u32[]{:S(2)}, u32[]{:S(2)}) collective-permute-start(bf16[8,64,512]{2,1,0:T(8,128)(2,1)S(1)} %get-tuple-element.52), channel_id=1, source_target_pairs={{0,8},{1,9},{2,10},{3,11},{4,12},{5,13},{6,14},{7,15},{8,16},{9,17... | collective-permute-start | bytes 1572872 | tf_op jit(solution)/shard_map/ppermute | solution.py:236
  64.4 26.7 %collective-permute-start.8 = (bf16[8,64,512]{2,1,0:T(8,128)(2,1)S(1)}, bf16[8,64,512]{2,1,0:T(8,128)(2,1)S(1)}, u32[]{:S(2)}, u32[]{:S(2)}) collective-permute-start(bf16[8,64,512]{2,1,0:T(8,128)(2,1)S(1)} %get-tuple-element.54), channel_id=1, source_target_pairs={{0,254},{1,255},{2,248},{3,249},{4,250},{5,251},{6,252},{7,253},{8... | collective-permute-start | bytes 1572872 | tf_op jit(solution)/shard_map/ppermute | solution.py:236
  67.0 25.4 %collective-permute-start.9 = (bf16[8,64,512]{2,1,0:T(8,128)(2,1)S(1)}, bf16[8,64,512]{2,1,0:T(8,128)(2,1)S(1)}, u32[]{:S(2)}, u32[]{:S(2)}) collective-permute-start(bf16[8,64,512]{2,1,0:T(8,128)(2,1)S(1)} %collective-permute-done.7.own), channel_id=1, source_target_pairs={{0,6},{1,7},{2,0},{3,1},{4,2},{5,3},{6,4},{7,5},{8,14},{9,15},{10,... | collective-permute-start | bytes 1572872 | tf_op jit(solution)/shard_map/ppermute | solution.py:236
  74.3 28.6 %collective-permute-start.11 = (bf16[8,64,512]{2,1,0:T(8,128)(2,1)S(1)}, bf16[8,64,512]{2,1,0:T(8,128)(2,1)S(1)}, u32[]{:S(2)}, u32[]{:S(2)}) collective-permute-start(bf16[8,64,512]{2,1,0:T(8,128)(2,1)S(1)} %get-tuple-element.52), channel_id=1, source_target_pairs={{0,10},{1,11},{2,12},{3,13},{4,14},{5,15},{6,8},{7,9},{8,18},{9,19... | collective-permute-start | bytes 1572872 | tf_op jit(solution)/shard_map/ppermute | solution.py:236
  82.7 28.6 %collective-permute-start.12 = (bf16[8,64,512]{2,1,0:T(8,128)(2,1)S(1)}, bf16[8,64,512]{2,1,0:T(8,128)(2,1)S(1)}, u32[]{:S(2)}, u32[]{:S(2)}) collective-permute-start(bf16[8,64,512]{2,1,0:T(8,128)(2,1)S(1)} %collective-permute-done.10.own), channel_id=1, source_target_pairs={{0,6},{1,7},{2,0},{3,1},{4,2},{5,3},{6,4},{7,5},{8,14},{9,15},{10,... | collective-permute-start | bytes 1572872 | tf_op jit(solution)/shard_map/ppermute | solution.py:236
  91.1 24.0 %collective-permute-start.26 = (bf16[8,64,512]{2,1,0:T(8,128)(2,1)S(1)}, bf16[8,64,512]{2,1,0:T(8,128)(2,1)S(1)}, u32[]{:S(2)}, u32[]{:S(2)}) collective-permute-start(bf16[8,64,512]{2,1,0:T(8,128)(2,1)S(1)} %get-tuple-element.39.refs_8_), channel_id=1, source_target_pairs={{0,1},{1,0},{2,3},{3,2},{4,5},{5,4},{6,7},{7,6},{8,9},{9,8},{10,11... | collective-permute-start | bytes 1572872 | tf_op jit(solution)/shard_map/ppermute | solution.py:236
  92.4 22.7 %collective-permute-start.27 = (bf16[8,64,512]{2,1,0:T(8,128)(2,1)S(1)}, bf16[8,64,512]{2,1,0:T(8,128)(2,1)S(1)}, u32[]{:S(2)}, u32[]{:S(2)}) collective-permute-start(bf16[8,64,512]{2,1,0:T(8,128)(2,1)S(1)} %get-tuple-element.40.refs_10_), channel_id=1, source_target_pairs={{0,1},{1,0},{2,3},{3,2},{4,5},{5,4},{6,7},{7,6},{8,9},{9,8},{10,11... | collective-permute-start | bytes 1572872 | tf_op jit(solution)/shard_map/ppermute | solution.py:236
  102.8 12.6 %collective-permute-start.13 = (bf16[4,64,512]{2,1,0:T(8,128)(2,1)S(1)}, bf16[4,64,512]{2,1,0:T(8,128)(2,1)S(1)}, u32[]{:S(2)}, u32[]{:S(2)}) collective-permute-start(bf16[4,64,512]{2,1,0:T(8,128)(2,1)S(1)} %get-tuple-element.31), channel_id=1, source_target_pairs={{0,2},{1,3},{2,4},{3,5},{4,6},{5,7},{6,0},{7,1},{8,10},{9,11},{10,... | collective-permute-start | bytes 786440 | tf_op jit(solution)/shard_map/ppermute | solution.py:236
  115.1 21.2 %collective-permute-start.5 = (bf16[8,64,512]{2,1,0:T(8,128)(2,1)S(1)}, bf16[8,64,512]{2,1,0:T(8,128)(2,1)S(1)}, u32[]{:S(2)}, u32[]{:S(2)}) collective-permute-start(bf16[8,64,512]{2,1,0:T(8,128)(2,1)S(1)} %get-tuple-element.50.refs_5_), channel_id=1, source_target_pairs={{0,1},{1,0},{2,3},{3,2},{4,5},{5,4},{6,7},{7,6},{8,9},{9,8},{10,11... | collective-permute-start | bytes 1572872 | tf_op jit(solution)/shard_map/ppermute | solution.py:236
  115.2 16.2 %collective-permute-start.15 = (bf16[4,64,512]{2,1,0:T(8,128)(2,1)S(1)}, bf16[4,64,512]{2,1,0:T(8,128)(2,1)S(1)}, u32[]{:S(2)}, u32[]{:S(2)}) collective-permute-start(bf16[4,64,512]{2,1,0:T(8,128)(2,1)S(1)} %get-tuple-element.33), channel_id=1, source_target_pairs={{0,2},{1,3},{2,4},{3,5},{4,6},{5,7},{6,0},{7,1},{8,10},{9,11},{10,... | collective-permute-start | bytes 786440 | tf_op jit(solution)/shard_map/ppermute | solution.py:236
  115.4 15.9 %collective-permute-start.16 = (bf16[4,64,512]{2,1,0:T(8,128)(2,1)S(1)}, bf16[4,64,512]{2,1,0:T(8,128)(2,1)S(1)}, u32[]{:S(2)}, u32[]{:S(2)}) collective-permute-start(bf16[4,64,512]{2,1,0:T(8,128)(2,1)S(1)} %get-tuple-element.34), channel_id=1, source_target_pairs={{0,6},{1,7},{2,0},{3,1},{4,2},{5,3},{6,4},{7,5},{8,14},{9,15},{10,... | collective-permute-start | bytes 786440 | tf_op jit(solution)/shard_map/ppermute | solution.py:236
  119.6 17.4 %collective-permute-start.3 = (bf16[4,64,512]{2,1,0:T(8,128)(2,1)S(1)}, bf16[4,64,512]{2,1,0:T(8,128)(2,1)S(1)}, u32[]{:S(2)}, u32[]{:S(2)}) collective-permute-start(bf16[4,64,512]{2,1,0:T(8,128)(2,1)S(1)} %slice.32), channel_id=1, source_target_pairs={{0,2},{1,3},{2,4},{3,5},{4,6},{5,7},{6,0},{7,1},{8,10},{9,11},{10,... | collective-permute-start | bytes 786440 | tf_op jit(solution)/shard_map/ppermute | solution.py:236
  121.1 15.9 %collective-permute-start.4 = (bf16[4,64,512]{2,1,0:T(8,128)(2,1)S(1)}, bf16[4,64,512]{2,1,0:T(8,128)(2,1)S(1)}, u32[]{:S(2)}, u32[]{:S(2)}) collective-permute-start(bf16[4,64,512]{2,1,0:T(8,128)(2,1)S(1)} %slice.33), channel_id=1, source_target_pairs={{0,6},{1,7},{2,0},{3,1},{4,2},{5,3},{6,4},{7,5},{8,14},{9,15},{10,... | collective-permute-start | bytes 786440 | tf_op jit(solution)/shard_map/ppermute | solution.py:236
  138.6 17.7 %collective-permute-start.6 = (f32[4,4,8,128]{3,2,1,0:T(8,128)S(1)}, f32[4,4,8,128]{3,2,1,0:T(8,128)S(1)}, u32[]{:S(2)}, u32[]{:S(2)}) collective-permute-start(f32[4,4,8,128]{3,2,1,0:T(8,128)S(1)} %get-tuple-element.30), channel_id=1, source_target_pairs={{0,1},{1,0},{2,3},{3,2},{4,5},{5,4},{6,7},{7,6},{8,9},{9,8},{10,11... | collective-permute-start | bytes 196616 | tf_op jit(solution)/shard_map/ppermute | solution.py:236
  138.8 19.4 %collective-permute-start.29 = (f32[4,4,8,128]{3,2,1,0:T(8,128)S(1)}, f32[4,4,8,128]{3,2,1,0:T(8,128)S(1)}, u32[]{:S(2)}, u32[]{:S(2)}) collective-permute-start(f32[4,4,8,128]{3,2,1,0:T(8,128)S(1)} %get-tuple-element.43), channel_id=1, source_target_pairs={{0,8},{1,9},{2,10},{3,11},{4,12},{5,13},{6,14},{7,15},{8,16},{9,17... | collective-permute-start | bytes 196616 | tf_op jit(solution)/shard_map/ppermute | solution.py:236
  156.3 8.5 %collective-permute-start.30 = (f32[4,4,8,128]{3,2,1,0:T(8,128)S(1)}, f32[4,4,8,128]{3,2,1,0:T(8,128)S(1)}, u32[]{:S(2)}, u32[]{:S(2)}) collective-permute-start(f32[4,4,8,128]{3,2,1,0:T(8,128)S(1)} %get-tuple-element.44), channel_id=1, source_target_pairs={{0,248},{1,249},{2,250},{3,251},{4,252},{5,253},{6,254},{7,255},{8... | collective-permute-start | bytes 196616 | tf_op jit(solution)/shard_map/ppermute | solution.py:236
  164.8 11.2 %collective-permute-start.31 = (f32[12,8,128]{2,1,0:T(8,128)S(1)}, f32[12,8,128]{2,1,0:T(8,128)S(1)}, u32[]{:S(2)}, u32[]{:S(2)}) collective-permute-start(f32[12,8,128]{2,1,0:T(8,128)S(1)} %get-tuple-element.46), channel_id=1, source_target_pairs={{0,2},{1,3},{2,4},{3,5},{4,6},{5,7},{6,0},{7,1},{8,10},{9,11},{10,... | collective-permute-start | bytes 147464 | tf_op jit(solution)/shard_map/ppermute | solution.py:236
  165.7 10.4 %collective-permute-start.32 = (f32[12,8,128]{2,1,0:T(8,128)S(1)}, f32[12,8,128]{2,1,0:T(8,128)S(1)}, u32[]{:S(2)}, u32[]{:S(2)}) collective-permute-start(f32[12,8,128]{2,1,0:T(8,128)S(1)} %get-tuple-element.47), channel_id=1, source_target_pairs={{0,6},{1,7},{2,0},{3,1},{4,2},{5,3},{6,4},{7,5},{8,14},{9,15},{10,... | collective-permute-start | bytes 147464 | tf_op jit(solution)/shard_map/ppermute | solution.py:236
  169.0 9.5 %collective-permute-start.33 = (f32[12,8,128]{2,1,0:T(8,128)S(1)}, f32[12,8,128]{2,1,0:T(8,128)S(1)}, u32[]{:S(2)}, u32[]{:S(2)}) collective-permute-start(f32[12,8,128]{2,1,0:T(8,128)S(1)} %get-tuple-element.48), channel_id=1, source_target_pairs={{0,4},{1,5},{2,6},{3,7},{4,0},{5,1},{6,2},{7,3},{8,12},{9,13},{10,... | collective-permute-start | bytes 147464 | tf_op jit(solution)/shard_map/ppermute | solution.py:236
  (5 other events, 35.3 us)
